TPU v7x, 128 devices: a whole 4x4x4 slice. The times are simulated.
128 devices in a mesh: row: 16 (over y, z), col: 8 (over x, core).
Axes of the slice: x: 4, y: 4, z: 4, core: 2. Of those that a mesh axis runs over, the one named last changes fastest.
Arguments:
- momentum: float32 [8192, 16384], P('row', 'col'), may hold values from -6 to 6
- grads: bfloat16 [2, 8192, 16384], P(None, 'row', 'col'), may hold values from -400 to 400
- basis: float32 [16384, 256], P('col'), may hold values from -0.046875 to 0.046875
Outputs:
- change: bfloat16 [8192, 16384], P('row', 'col')
- state: float32 [8192, 16384], P('row', 'col')
All inputs are finite; a program needn't handle non-finite values.
Results may differ from a plain program's by a relative error of at most 0.0035.
Values sent between devices are 32-bit elements; how exact they have to be, the bound alone decides.
No kernel may reach another device: no remote copies, remote signals or barrier semaphores. Data moves between devices by JAX's collectives and lax.ppermute only.
A program may use at most 128 MiB of HBM per device.

v0:
```python
import functools

import jax
import jax.numpy as jnp
from jax import lax
from jax.experimental import pallas as pl
from jax.experimental.pallas import tpu as pltpu
from jax.sharding import PartitionSpec as P

KEEP_RATE = 0.95
NORM_EPS = 1e-06
LANES = 128
CHUNKS = 4
F32 = jnp.float32
BF16 = jnp.bfloat16
VMEM_LIMIT = 20 * 1024 * 1024
NN = (((1,), (0,)), ((), ()))
NT = (((1,), (1,)), ((), ()))


def split(x):
    high = x.astype(BF16)
    return high, (x - high.astype(F32)).astype(BF16)


def mm(a, b, dims):
    return lax.dot_general(a, b, dims, preferred_element_type=F32)


def dot3(a, b, dims):
    return mm(a[0], b[0], dims) + (mm(a[0], b[1], dims) + mm(a[1], b[0], dims))


def exact(a, b, dims):
    return lax.dot_general(
        a, b, dims, precision=lax.Precision.HIGHEST, preferred_element_type=F32
    )


def call(kernel, in_specs, out_shape, out_specs, scratch, cost):
    return pl.pallas_call(
        kernel,
        in_specs=in_specs,
        out_specs=out_specs,
        out_shape=out_shape,
        scratch_shapes=scratch,
        compiler_params=pltpu.CompilerParams(vmem_limit_bytes=VMEM_LIMIT),
        cost_estimate=pl.CostEstimate(
            flops=cost, transcendentals=0, bytes_accessed=8 * 1024 * 1024
        ),
    )


VM = pl.BlockSpec(memory_space=pltpu.VMEM)
SM = pl.BlockSpec(memory_space=pltpu.SMEM)
ANY = pl.BlockSpec(memory_space=pl.ANY)


def in_hbm(*arrays):
    return [pltpu.with_memory_space_constraint(a, pltpu.HBM) for a in arrays]


def pair(shape):
    return jax.ShapeDtypeStruct((2, *shape), BF16)


def pair_in_hbm(shape):
    return pltpu.HBM((2, *shape), BF16)


def dma(*shape):
    return pltpu.SemaphoreType.DMA(shape)


def fetch(moves, sems):
    def copies(k):
        return [
            pltpu.make_async_copy(a, b, sems.at[k, n]) for n, (a, b) in enumerate(moves(k))
        ]

    for k in range(CHUNKS):
        for copy in copies(k):
            copy.start()

    def wait(k):
        for copy in copies(k):
            copy.wait()

    return wait


def send(moves, sems):
    def copies(k):
        return [
            pltpu.make_async_copy(a, b, sems.at[k, n]) for n, (a, b) in enumerate(moves(k))
        ]

    def start(k):
        for copy in copies(k):
            copy.start()

    def finish():
        for k in range(CHUNKS):
            for copy in copies(k):
                copy.wait()

    return start, finish


def columns(k, width):
    if isinstance(k, int):
        return pl.ds(k * width, width)
    return pl.ds(pl.multiple_of(k * width, width), width)


def each(block, count=CHUNKS):
    lax.fori_loop(0, count, lambda k, _: (block(k), 0)[1], 0)


def same(n):
    i = lax.broadcasted_iota(jnp.int32, (n, n), 0)
    return i == lax.broadcasted_iota(jnp.int32, (n, n), 1)


def buffer_moves(m_ref, g_ref, m, g):
    width = m.shape[1] // CHUNKS

    def moves(k):
        c = columns(k, width)
        pairs = [(m_ref.at[:, c], m.at[:, c])]
        for n in range(g.shape[0]):
            pairs.append((g_ref.at[n, :, c], g.at[n, :, c]))
        return pairs

    return moves


def buffer_block(m, g, c):
    b = m[:, c]
    for n in range(g.shape[0]):
        b = b + g[n, :, c].astype(F32)
    return b


def first_kernel(m_ref, g_ref, v_ref, p_ref, m, g, v, sems):
    width = m.shape[1] // CHUNKS
    moves = buffer_moves(m_ref, g_ref, m, g)
    wait = fetch(
        lambda k: moves(k) + [(v_ref.at[columns(k, width)], v.at[columns(k, width)])], sems
    )
    p_ref[...] = jnp.zeros_like(p_ref)

    def block(k):
        c = columns(k, width)
        wait(k)
        p_ref[...] += dot3(split(buffer_block(m, g, c)), split(v[c]), NN)

    each(block)


def first_projection(momentum, grads, basis):
    rows, cols = momentum.shape
    rank = basis.shape[1]
    return call(
        first_kernel,
        [ANY] * 3,
        jax.ShapeDtypeStruct((rows, rank), F32),
        VM,
        [
            pltpu.VMEM((rows, cols), F32),
            pltpu.VMEM((1, rows, cols), BF16),
            pltpu.VMEM((cols, rank), F32),
            dma(CHUNKS, 3),
        ],
        6 * rows * cols * rank,
    )(*in_hbm(momentum, grads, basis))


def store_products(inputs, outputs, scratch, block, scaled, direct):
    n_ref, mine_ref, theirs_ref = inputs
    x_ref, p_ref, rs_ref = outputs
    parts, t, shares, pair_of_p = scratch[:4]
    held, sems = (None, None) if direct else scratch[4:]
    core = lax.rem(n_ref[0], 2)
    parts[pl.ds(2 * core, 2)] = mine_ref[...]
    parts[pl.ds(2 - 2 * core, 2)] = theirs_ref[...]
    rows, rank = p_ref.shape
    height = rows // 4
    p = jnp.concatenate([parts[k, :height] for k in range(4)], axis=0)
    if scaled:
        rs = lax.rsqrt(parts[0, height : height + 8] + NORM_EPS)
        p = p * rs[:1]
    else:
        rs = jnp.ones(rs_ref.shape, F32)
    rs_ref[...] = rs
    p_ref[...] = p
    turned, half = p.T, LANES
    t[: 2 * half] = exact(turned, p[:, :half], NN)
    t[2 * half :] = exact(turned[half:], p[:, half:], NN)
    size = x_ref.shape[1] - rank
    share = t[pl.ds(pl.multiple_of(n_ref[0] * size, size), size), :]
    pt = split(turned)
    blocks = x_ref.shape[0] // CHUNKS
    shares[...] = share
    pair_of_p[0], pair_of_p[1] = pt
    x = x_ref if direct else held

    def fill(k):
        r = dot3((pair_of_p[0], pair_of_p[1]), block(k), NN)
        for q in range(blocks):
            x[k * blocks + q, :rank] = r[:, q * LANES : (q + 1) * LANES]
            x[k * blocks + q, rank:] = shares[...]
        if not direct:
            start(k)

    if not direct:
        start, finish = send(
            lambda k: [(held.at[columns(k, blocks)], x_ref.at[columns(k, blocks)])], sems
        )
    each(fill)
    if not direct:
        finish()


def first_products_kernel(
    n_ref, mine_ref, theirs_ref, m_ref, g_ref, x_ref, p_ref, rs_ref, m, g, came, *scratch
):
    wait = fetch(buffer_moves(m_ref, g_ref, m, g), came)

    def block(k):
        wait(k)
        return split(buffer_block(m, g, columns(k, m.shape[1] // CHUNKS)))

    store_products(
        (n_ref, mine_ref, theirs_ref), (x_ref, p_ref, rs_ref), scratch, block, False, True
    )


def pair_moves(b_ref, b):
    width = b.shape[2] // CHUNKS

    def moves(k):
        c = columns(k, width)
        return [(b_ref.at[:, :, c], b.at[:, :, c])]

    return moves


def second_products_kernel(
    n_ref, mine_ref, theirs_ref, b_ref, x_ref, p_ref, rs_ref, b, came, *scratch
):
    wait = fetch(pair_moves(b_ref, b), came)

    def block(k):
        wait(k)
        c = columns(k, b.shape[2] // CHUNKS)
        return b[0, :, c], b[1, :, c]

    store_products(
        (n_ref, mine_ref, theirs_ref), (x_ref, p_ref, rs_ref), scratch, block, True, False
    )


def products(kernel, place, mine, theirs, bigs, held, peers, direct):
    rows, cols = bigs[0].shape[-2:]
    _, height, rank = mine.shape
    tail = 3 * LANES // peers
    shape = (cols // LANES, rank + tail, LANES)
    return call(
        kernel,
        [SM, VM, VM] + [ANY] * len(bigs),
        [
            jax.ShapeDtypeStruct(shape, F32) if direct else pltpu.HBM(shape, F32),
            jax.ShapeDtypeStruct((rows, rank), F32),
            jax.ShapeDtypeStruct((8, rank), F32),
        ],
        [VM if direct else ANY, VM, VM],
        held
        + [
            dma(CHUNKS, len(bigs)),
            pltpu.VMEM((4, height, rank), F32),
            pltpu.VMEM((3 * LANES, LANES), F32),
            pltpu.VMEM((tail, LANES), F32),
            pltpu.VMEM((2, rank, rows), BF16),
        ]
        + ([] if direct else [pltpu.VMEM(shape, F32), dma(CHUNKS, 1)]),
        6 * rows * cols * rank,
    )(place, mine, theirs, *in_hbm(*bigs))


def spread_kernel(x_ref, y_ref, t_ref, y, sems):
    count = x_ref.shape[0]
    rank = y.shape[0]
    total = x_ref[0]
    for k in range(1, count):
        total = total + x_ref[k]
    y[...] = total[:rank]
    copies = [
        pltpu.make_async_copy(y, y_ref.at[k], sems.at[k]) for k in range(count)
    ]
    for copy in copies:
        copy.start()
    t_ref[...] = total[rank:]
    for copy in copies:
        copy.wait()


def spread_sum(x, rank):
    count, height, width = x.shape
    return call(
        spread_kernel,
        [VM],
        [
            pltpu.HBM((count, rank, width), F32),
            jax.ShapeDtypeStruct((height - rank, width), F32),
        ],
        [ANY, VM],
        [pltpu.VMEM((rank, width), F32), pltpu.SemaphoreType.DMA((count,))],
        count * height * width,
    )(x)


def eliminated(m):
    n = m.shape[0]
    eye = same(n)
    across = lax.rsqrt(jnp.sum(jnp.where(eye, m, 0.0), axis=0, keepdims=True))
    down = lax.rsqrt(jnp.sum(jnp.where(eye, m, 0.0), axis=1, keepdims=True))
    m = m * down * across
    lane = lax.broadcasted_iota(jnp.int32, (8, n), 1)
    sub = lax.broadcasted_iota(jnp.int32, (8, n), 0)
    tiles = [m[8 * t : 8 * t + 8] for t in range(n // 8)]
    for j in range(0, n, 2):
        t, r = divmod(j, 8)
        first, second = lane[:1] == j, lane[:1] == j + 1
        both = (lane >= j) & (lane < j + 2)
        c0 = [jnp.broadcast_to(x[:, j : j + 1], (8, n)) for x in tiles[t:]]
        c1 = [jnp.broadcast_to(x[:, j + 1 : j + 2], (8, n)) for x in tiles[t:]]
        row0, row1 = tiles[t][r : r + 1], tiles[t][r + 1 : r + 2]
        a, b = c0[0][r : r + 1], c0[0][r + 1 : r + 2]
        d = c1[0][r + 1 : r + 2]
        inv_a = 1.0 / a
        inv_d = a * (1.0 / (a * d - b * b))
        ratio = b * inv_a
        low = row1 - ratio * row0
        use1 = jnp.where(first, -ratio, jnp.where(second, 1.0, low)) * inv_d
        use0 = jnp.where(first, 1.0, jnp.where(second, 0.0, row0)) * inv_a - ratio * use1
        kept = jnp.where(first, -ratio, low)
        for s in range(t, n // 8):
            new = jnp.where(both, 0.0, tiles[s]) - c0[s - t] * use0 - c1[s - t] * use1
            if s == t:
                new = jnp.where(sub > r + 1, new, jnp.where(sub == r + 1, kept, tiles[s]))
            tiles[s] = new
    m = jnp.concatenate(tiles, axis=0)
    i = lax.broadcasted_iota(jnp.int32, (n, n), 0)
    j = lax.broadcasted_iota(jnp.int32, (n, n), 1)
    pivots = jnp.sum(jnp.where(eye, m, 0.0), axis=1, keepdims=True)
    unit = jnp.where(i > j, m, jnp.where(eye, 1.0, 0.0))
    return unit * lax.rsqrt(pivots) * across


def cholesky_kernel(n_ref, p_ref, *refs):
    pieces, (w_ref, o_ref, a, low) = refs[:-4], refs[-4:]
    size = pieces[0].shape[0]
    count = len(pieces)
    for k, piece in enumerate(pieces):
        place = lax.rem(n_ref[0] // 2 + k, count)
        a[pl.ds(pl.multiple_of(place * size, size), size), :] = piece[...]
    half = LANES

    def body(b, carry):
        w = eliminated(a[pl.ds(pl.multiple_of(2 * b * half, half), half), :])
        first = pl.multiple_of(b * half, half)
        w_ref[pl.ds(first, half), pl.ds(first, half)] = w

        @pl.when(b == 0)
        def _():
            low[...] = exact(a[half : 2 * half], w, NT)
            a[2 * half :] -= exact(low[...], low[...], NT)

        return carry

    lax.fori_loop(0, 2, body, 0)
    w_ref[:half, half:] = jnp.zeros((half, half), F32)
    w_ref[half:, :half] = -exact(
        w_ref[half:, half:], exact(low[...], w_ref[:half, :half], NN), NN
    )
    o_ref[...] = exact(p_ref[...], w_ref[...], NT)


def inverse_factor(pieces, place, p):
    rank = p.shape[1]
    return call(
        cholesky_kernel,
        [SM, VM] + [VM] * len(pieces),
        [jax.ShapeDtypeStruct((rank, rank), F32), jax.ShapeDtypeStruct(p.shape, F32)],
        [VM, VM],
        [pltpu.VMEM((3 * LANES, LANES), F32), pltpu.VMEM((LANES, LANES), F32)],
        10**10,
    )(place, p, *pieces)


def middle_kernel(o_ref, w_ref, x_ref, m_ref, g_ref, q_ref, rt_ref, m, g, q_sum, s_ref, sems):
    wait = fetch(buffer_moves(m_ref, g_ref, m, g), sems)

    def turn(k):
        c = columns(k, LANES)
        rt_ref[0, :, c], rt_ref[1, :, c] = split(x_ref[k])

    each(turn, x_ref.shape[0])
    rt = (rt_ref[0], rt_ref[1])
    w = w_ref[...]
    s_ref[...] = exact(exact(w, dot3(rt, rt, NT), NN), w, NT)
    width = m.shape[1] // CHUNKS
    q_sum[...] = jnp.zeros_like(q_sum)

    def block(k):
        c = columns(k, width)
        wait(k)
        q_sum[...] += dot3(
            split(buffer_block(m, g, c)), (rt_ref[0, :, c], rt_ref[1, :, c]), NT
        )

    each(block)
    s = s_ref[...]
    q = dot3(split(q_sum[...]), split(w_ref[...]), NT) - dot3(
        split((1.0 - KEEP_RATE) * o_ref[...]), split(s), NN
    )
    n = s.shape[0]
    squares = jnp.sum(jnp.where(same(n), s, 0.0), axis=0, keepdims=True)
    height = q_ref.shape[1] - 8
    for k in range(q_ref.shape[0]):
        q_ref[k, :height] = q[k * height : (k + 1) * height]
        q_ref[k, height:] = jnp.broadcast_to(squares, (8, n))


def middle(o, w, x, momentum, grads):
    rows, cols = momentum.shape
    rank = o.shape[1]
    return call(
        middle_kernel,
        [VM] * 3 + [ANY] * 2,
        [jax.ShapeDtypeStruct((4, rows // 4 + 8, rank), F32), pair((rank, cols))],
        [VM] * 2,
        [
            pltpu.VMEM((rows, cols), F32),
            pltpu.VMEM(grads.shape, BF16),
            pltpu.VMEM((rows, rank), F32),
            pltpu.VMEM((rank, rank), F32),
            dma(CHUNKS, 3),
        ],
        10 * rows * cols * rank,
    )(o, w, x, *in_hbm(momentum, grads))


def update_kernel(
    o_ref, w_ref, rt_ref, m_ref, g_ref, raw_ref, b_ref, m, g, raw, b, came, sent
):
    wait = fetch(buffer_moves(m_ref, g_ref, m, g), came)
    o = split((1.0 - KEEP_RATE) * o_ref[...])
    w = split(w_ref[...])
    width = m.shape[1] // CHUNKS
    start, finish = send(
        lambda k: [
            (a.at[:, :, columns(k, width)], r.at[:, :, columns(k, width)])
            for a, r in ((raw, raw_ref), (b, b_ref))
        ],
        sent,
    )

    def block(k):
        c = columns(k, width)
        now = split(dot3(w, (rt_ref[0, :, c], rt_ref[1, :, c]), NN))
        raw[0, :, c], raw[1, :, c] = now
        wait(k)
        b[0, :, c], b[1, :, c] = split(buffer_block(m, g, c) - dot3(o, now, NN))
        start(k)

    each(block)
    finish()


def second_buffer(o, w, rt, momentum, grads):
    rows, cols = momentum.shape
    rank = o.shape[1]
    return call(
        update_kernel,
        [VM] * 3 + [ANY] * 2,
        [pair_in_hbm((rank, cols)), pair_in_hbm((rows, cols))],
        [ANY] * 2,
        [
            pltpu.VMEM((rows, cols), F32),
            pltpu.VMEM(grads.shape, BF16),
            pltpu.VMEM((2, rank, cols), BF16),
            pltpu.VMEM((2, rows, cols), BF16),
            dma(CHUNKS, 3),
            dma(CHUNKS, 2),
        ],
        9 * rows * cols * rank,
    )(o, w, rt, *in_hbm(momentum, grads))


def write_out(value, out_ref, buffer, sems):
    width = buffer.shape[1] // CHUNKS
    start, finish = send(
        lambda k: [(buffer.at[:, columns(k, width)], out_ref.at[:, columns(k, width)])], sems
    )

    def block(k):
        c = columns(k, width)
        buffer[:, c] = value(k, c).astype(buffer.dtype)
        start(k)

    each(block)
    finish()


def change_kernel(factor, o_ref, rs_ref, raw_ref, c_ref, raw, buffer, came, sent):
    wait = fetch(pair_moves(raw_ref, raw), came)
    o = split(o_ref[...] * (factor * rs_ref[:1]))

    def value(k, c):
        wait(k)
        return dot3(o, (raw[0, :, c], raw[1, :, c]), NN)

    write_out(value, c_ref, buffer, sent)


def first_change(factor, o, rs, raw):
    rows, rank = o.shape
    cols = raw.shape[2]
    return call(
        functools.partial(change_kernel, factor),
        [VM, VM, ANY],
        pltpu.HBM((rows, cols), F32),
        ANY,
        [
            pltpu.VMEM(raw.shape, BF16),
            pltpu.VMEM((rows, cols), F32),
            dma(CHUNKS, 1),
            dma(CHUNKS, 1),
        ],
        6 * rows * cols * rank,
    )(o, rs, *in_hbm(raw))


def last_raw_kernel(w_ref, x_ref, raw_ref, sq_ref, total):
    blocks = x_ref.shape[0] // CHUNKS
    n = w_ref.shape[0]
    total[...] = jnp.zeros_like(total)

    def block(k):
        c = columns(k, blocks * LANES)
        part = jnp.concatenate([x_ref[k * blocks + q] for q in range(blocks)], axis=1)
        raw = dot3(split(w_ref[...]), split(part), NN)
        raw_ref[0, :, c], raw_ref[1, :, c] = split(raw)
        total[...] += jnp.sum(raw * raw, axis=1, keepdims=True)

    each(block)
    squares = jnp.where(same(n), jnp.broadcast_to(total[:, :1], (n, n)), 0.0)
    row = jnp.sum(squares, axis=0, keepdims=True)
    for k in range(sq_ref.shape[0]):
        sq_ref[k] = jnp.broadcast_to(row, (8, n))


def last_raw(w, x, peers):
    rank = w.shape[0]
    cols = x.shape[0] * LANES
    return call(
        last_raw_kernel,
        [VM] * 2,
        [pair((rank, cols)), jax.ShapeDtypeStruct((peers, 8, rank), F32)],
        [VM] * 2,
        [pltpu.VMEM((rank, LANES), F32)],
        6 * rank * cols * rank,
    )(w, *in_hbm(x))


def state_kernel(o_ref, raw_ref, b_ref, s_ref, b, buffer, came, sent):
    wait = fetch(pair_moves(b_ref, b), came)
    o = split((1.0 - KEEP_RATE) * o_ref[...])

    def value(k, c):
        part = dot3(o, (raw_ref[0, :, c], raw_ref[1, :, c]), NN)
        wait(k)
        return b[0, :, c].astype(F32) + b[1, :, c].astype(F32) - part

    write_out(value, s_ref, buffer, sent)


def last_state(o, raw, b):
    _, rows, cols = b.shape
    rank = o.shape[1]
    return call(
        state_kernel,
        [VM, VM, ANY],
        pltpu.HBM((rows, cols), F32),
        ANY,
        [
            pltpu.VMEM(b.shape, BF16),
            pltpu.VMEM((rows, cols), F32),
            dma(CHUNKS, 1),
            dma(CHUNKS, 1),
        ],
        6 * rows * cols * rank,
    )(o, raw, *in_hbm(b))


def last_change_kernel(
    factor, o_ref, sq_ref, raw_ref, c_ref, out_ref, held, buffer, came, sent
):
    width = held.shape[1] // CHUNKS
    wait = fetch(
        lambda k: [(c_ref.at[:, columns(k, width)], held.at[:, columns(k, width)])], came
    )
    total = sq_ref[0, :1]
    for k in range(1, sq_ref.shape[0]):
        total = total + sq_ref[k, :1]
    o = split(o_ref[...] * (factor * lax.rsqrt(total + NORM_EPS)))

    def value(k, c):
        part = dot3(o, (raw_ref[0, :, c], raw_ref[1, :, c]), NN)
        wait(k)
        return held[:, c] + part

    write_out(value, out_ref, buffer, sent)


def last_change(factor, o, sq, raw, change):
    rows, cols = change.shape
    rank = o.shape[1]
    return call(
        functools.partial(last_change_kernel, factor),
        [VM, VM, VM, ANY],
        pltpu.HBM((rows, cols), BF16),
        ANY,
        [
            pltpu.VMEM((rows, cols), F32),
            pltpu.VMEM((rows, cols), BF16),
            dma(CHUNKS, 1),
            dma(CHUNKS, 1),
        ],
        6 * rows * cols * rank,
    )(o, sq, raw, *in_hbm(change))


SIDE = 4


def chip_permute(x, move):
    pairs = [(2 * k + c, 2 * move(k) + c) for k in range(SIDE) for c in range(2)]
    return lax.ppermute(x, "col", pairs)


def core_permute(x):
    return lax.ppermute(x, "col", [(k, k ^ 1) for k in range(2 * SIDE)])


def near(k):
    return k ^ 1


def far(k):
    return SIDE - 1 - k


def col_sum(parts, beside):
    core = lax.axis_index("col") % 2
    mine = lax.dynamic_slice_in_dim(parts, 2 * core, 2, 0)
    theirs = lax.dynamic_slice_in_dim(parts, 2 - 2 * core, 2, 0)
    mine = mine + core_permute(theirs)
    a, b = mine[0], mine[1]
    near_a, far_b, beside = lax.optimization_barrier(
        (chip_permute(a, near), chip_permute(b, far), beside)
    )
    a, b = a + near_a, b + far_b
    a, b = a + chip_permute(a, far), b + chip_permute(b, near)
    mine = jnp.stack([a, b])
    return mine, core_permute(mine), beside


def by_chip(part):
    core = lax.axis_index("col") % 2
    other = core_permute(part)
    chip = jnp.where(
        core == 0, jnp.concatenate([part, other]), jnp.concatenate([other, part])
    )
    return [chip] + [
        chip_permute(chip, lambda k, d=d: (k - d) % SIDE) for d in range(1, SIDE)
    ]


def exchange(x, axis):
    return lax.all_to_all(x, axis, 0, 0, tiled=True)


def row_total(blocks, p, place, beside):
    got, beside = lax.optimization_barrier((exchange(blocks, "row"), beside))
    own, part = spread_sum(got, p.shape[1])
    total = exchange(own, "row")
    return total, *inverse_factor(by_chip(part), place, p), beside


def shards(momentum, grads, basis):
    rows, cols = momentum.shape
    rank = basis.shape[1]
    peers = lax.axis_size("col")
    factor = (rows * lax.axis_size("row") * cols * peers / rank) ** 0.5
    place = lax.axis_index("col").astype(jnp.int32)[None]

    held = [pltpu.VMEM((rows, cols), F32), pltpu.VMEM((1, rows, cols), BF16)]
    part = first_projection(momentum, grads, basis)
    mine, theirs, _ = col_sum(part.reshape(4, rows // 4, rank), [])
    x1, p1, _ = products(
        first_products_kernel, place, mine, theirs, [momentum, grads], held, peers, True
    )
    x1, w1, o1, _ = row_total(x1, p1, place, [])
    part, rt1 = middle(o1, w1, x1, momentum, grads)
    mine, theirs, (raw1, buffer) = col_sum(
        part, second_buffer(o1, w1, rt1, momentum, grads)
    )
    held = [pltpu.VMEM((2, rows, cols), BF16)]
    x2, p2, rs1 = products(
        second_products_kernel, place, mine, theirs, [buffer], held, peers, False
    )
    change1 = first_change(factor, o1, rs1, raw1)
    x2, w2, o2, change1 = row_total(x2, p2, place, change1)
    raw2, sq2 = last_raw(w2, x2, peers)
    sq2 = exchange(sq2, "col")
    state = last_state(o2, raw2, buffer)
    change = last_change(factor, o2, sq2, raw2, change1)
    return change, state


def solution(mesh):
    return jax.shard_map(
        shards,
        mesh=mesh,
        in_specs=(P("row", "col"), P(None, "row", "col"), P("col", None)),
        out_specs=(P("row", "col"), P("row", "col")),
        check_vma=False,
    )
```

profile of v0, /device:TPU:1, one launch (start us, length us, event | category | flops | bytes accessed | tf_op | source)
XLA Modules:
  0.0 227.6 jit_solution(17273344624649462971)
XLA Ops:
  0.6 4.1 %shard_map.50 = f32[512,256]{1,0:T(8,128)S(1)} custom-call(f32[512,2048]{1,0:T(8,128)} %m_ref.7, bf16[2,512,2048]{2,1,0:T(8,128)(2,1)} %g_ref.7, f32[2048,256]{1,0:T(8,128)} %v_ref.1), custom_call_target="tpu_custom_call" | custom-call | flops 1610612736 | bytes 8388608 | tf_op jit(solution)/shard_map/pallas_call | solution.py:164
  4.8 1.5 collective-permute-start
  6.3 1.2 collective-permute-done
  7.6 1.4 collective-permute-start.1
  8.9 1.8 collective-permute-start.2
  10.8 1.6 collective-permute-done.1
  12.3 2.2 collective-permute-done.2
  14.7 1.9 collective-permute-start.3
  16.6 1.9 collective-permute-done.4
  18.5 1.3 collective-permute-done.3
  19.8 2.8 %collective-permute-start.5 = (f32[2,128,256]{2,1,0:T(8,128)S(1)}, f32[2,128,256]{2,1,0:T(8,128)S(1)}, u32[]{:S(2)}, u32[]{:S(2)}) collective-permute-start(f32[2,128,256]{2,1,0:T(8,128)S(1)} %pad_maximum_fusion.1.mine_ref), channel_id=1, source_target_pairs={{0,1},{1,0},{2,3},{3,2},{4,5},{5,4},{6,7},{7,6},{8,9},{9,8},{10,11... | collective-permute-start | bytes 786440 | tf_op jit(solution)/shard_map/ppermute | solution.py:655
  22.6 1.2 collective-permute-done.5.theirs_ref
  23.7 4.6 %shard_map.51 = (f32[16,304,128]{2,1,0:T(8,128)S(1)}, f32[512,256]{1,0:T(8,128)S(1)}, f32[8,256]{1,0:T(8,128)}) custom-call(s32[1]{0:T(128)} %bitcast.n_ref, f32[2,128,256]{2,1,0:T(8,128)S(1)} %pad_maximum_fusion.1.mine_ref, f32[2,128,256]{2,1,0:T(8,128)S(1)} %collective-permute-done.5.theirs_ref, f32[512,2048]{1,0:T(8,128)} %m_ref.7, ...), custom_call_target="tpu_custom_call" | custom-call | flops 1610612736 | bytes 8388608 | tf_op jit(solution)/shard_map/pallas_call | solution.py:269
  28.3 38.5 %all_to_all.25.x_ref = f32[16,304,128]{2,1,0:T(8,128)S(1)} all-to-all(f32[16,304,128]{2,1,0:T(8,128)S(1)} %get-tuple-element.32), channel_id=1, replica_groups=mesh['row'=16,'col'=8] {'row'}, dimensions={0} | all-to-all | bytes 4980736 | tf_op jit(solution)/shard_map/all_to_all | solution.py:693
  66.8 1.5 shard_map.52
  68.4 4.2 %all-to-all-start.1 = ((f32[16,256,128]{2,1,0:T(8,128)}), f32[16,256,128]{2,1,0:T(8,128)S(1)}, u32[]{:S(2)}, u32[]{:S(2)}) async-start(f32[16,256,128]{2,1,0:T(8,128)} %get-tuple-element.36), calls=%async_computation.1 | async-start | bytes 4194304 | tf_op jit(solution)/shard_map/all_to_all | solution.py:693
  72.6 1.9 collective-permute-start.6
  74.5 0.8 collective-permute-done.6
  75.4 1.8 collective-permute-start.7
  78.6 3.3 %collective-permute-done.8.refs_2_ = f32[96,128]{1,0:T(8,128)S(1)} collective-permute-done((f32[96,128]{1,0:T(8,128)S(1)}, f32[96,128]{1,0:T(8,128)S(1)}, u32[]{:S(2)}, u32[]{:S(2)}) %collective-permute-start.8) | collective-permute-done | bytes 49184 | tf_op jit(solution)/shard_map/ppermute | solution.py:651
  82.5 15.1 %shard_map.53 = (f32[256,256]{1,0:T(8,128)S(1)}, f32[512,256]{1,0:T(8,128)S(1)}) custom-call(s32[1]{0:T(128)} %bitcast.n_ref, f32[512,256]{1,0:T(8,128)S(1)} %get-tuple-element.31.p_ref, f32[96,128]{1,0:T(8,128)S(1)} %maximum_select_fusion.refs_0_, f32[96,128]{1,0:T(8,128)S(1)} %collective-permute-done.7.refs_1_, ...), custom_call_target="tpu_custom_call" | custom-call | flops 10000000000 | bytes 8388608 | tf_op jit(solution)/shard_map/pallas_call | solution.py:392
  98.2 6.3 %shard_map.54 = (f32[4,136,256]{2,1,0:T(8,128)S(1)}, bf16[2,256,2048]{2,1,0:T(8,128)(2,1)S(1)}) custom-call(f32[512,256]{1,0:T(8,128)S(1)} %get-tuple-element.34.o_ref, f32[256,256]{1,0:T(8,128)S(1)} %get-tuple-element.35.w_ref, f32[16,256,128]{2,1,0:T(8,128)S(1)} %all-to-all-done.1.x_ref, f32[512,2048]{1,0:T(8,128)} %m_ref.7, bf16[2,512,2048]{2,1,0:T(8,128)(2,1)} %g_ref.7), custom_call_target="tpu_custom_call" | custom-call | flops 2684354560 | bytes 8388608 | tf_op jit(solution)/shard_map/pallas_call | solution.py:439
  104.6 5.2 %collective-permute-start.10 = (f32[2,136,256]{2,1,0:T(8,128)S(1)}, f32[2,136,256]{2,1,0:T(8,128)S(1)}, u32[]{:S(2)}, u32[]{:S(2)}) collective-permute-start(f32[2,136,256]{2,1,0:T(8,128)S(1)} %constant_dynamic-slice_fusion), channel_id=1, source_target_pairs={{0,1},{1,0},{2,3},{3,2},{4,5},{5,4},{6,7},{7,6},{8,9},{9,8},{10,11... | collective-permute-start | bytes 835592 | tf_op jit(solution)/shard_map/ppermute | solution.py:655
  109.8 1.2 collective-permute-done.10
  111.6 1.8 collective-permute-start.12
  113.4 6.6 %shard_map.55 = (bf16[2,256,2048]{2,1,0:T(8,128)(2,1)}, bf16[2,512,2048]{2,1,0:T(8,128)(2,1)}) custom-call(f32[512,256]{1,0:T(8,128)S(1)} %get-tuple-element.34.o_ref, f32[256,256]{1,0:T(8,128)S(1)} %get-tuple-element.35.w_ref, bf16[2,256,2048]{2,1,0:T(8,128)(2,1)S(1)} %get-tuple-element.38.rt_ref, f32[512,2048]{1,0:T(8,128)} %m_ref.7, ...), custom_call_target="tpu_custom_call" | custom-call | flops 2415919104 | bytes 8388608 | tf_op jit(solution)/shard_map/pallas_call | solution.py:485
  120.6 0.9 collective-permute-start.13
  121.4 3.0 %collective-permute-done.14 = f32[136,256]{1,0:T(8,128)S(1)} collective-permute-done((f32[136,256]{1,0:T(8,128)S(1)}, f32[136,256]{1,0:T(8,128)S(1)}, u32[]{:S(2)}, u32[]{:S(2)}) %collective-permute-start.14) | collective-permute-done | bytes 139296 | tf_op jit(solution)/shard_map/ppermute | solution.py:651
  124.4 1.3 collective-permute-done.13
  125.7 2.4 %collective-permute-start.15 = (f32[2,136,256]{2,1,0:T(8,128)S(1)}, f32[2,136,256]{2,1,0:T(8,128)S(1)}, u32[]{:S(2)}, u32[]{:S(2)}) collective-permute-start(f32[2,136,256]{2,1,0:T(8,128)S(1)} %pad_maximum_fusion.mine_ref), channel_id=1, source_target_pairs={{0,1},{1,0},{2,3},{3,2},{4,5},{5,4},{6,7},{7,6},{8,9},{9,8},{10,11... | collective-permute-start | bytes 835592 | tf_op jit(solution)/shard_map/ppermute | solution.py:655
  128.2 1.2 collective-permute-done.15.theirs_ref
  129.4 5.1 %shard_map.56 = (f32[16,304,128]{2,1,0:T(8,128)}, f32[512,256]{1,0:T(8,128)S(1)}, f32[8,256]{1,0:T(8,128)S(1)}) custom-call(s32[1]{0:T(128)} %bitcast.n_ref, f32[2,136,256]{2,1,0:T(8,128)S(1)} %pad_maximum_fusion.mine_ref, f32[2,136,256]{2,1,0:T(8,128)S(1)} %collective-permute-done.15.theirs_ref, bf16[2,512,2048]{2,1,0:T(8,128)(2,1)} %get-tuple-element.43.b_ref), custom_call_target="tpu_custom_call" | custom-call | flops 1610612736 | bytes 8388608 | tf_op jit(solution)/shard_map/pallas_call | solution.py:269
  134.5 3.7 %all-to-all-start.2 = ((f32[16,304,128]{2,1,0:T(8,128)}), f32[16,304,128]{2,1,0:T(8,128)S(1)}, u32[]{:S(2)}, u32[]{:S(2)}) async-start(f32[16,304,128]{2,1,0:T(8,128)} %get-tuple-element.45), calls=%async_computation.2 | async-start | bytes 4980736 | tf_op jit(solution)/shard_map/all_to_all | solution.py:693
  138.2 4.5 %shard_map.57.c_ref = f32[512,2048]{1,0:T(8,128)} custom-call(f32[512,256]{1,0:T(8,128)S(1)} %get-tuple-element.34.o_ref, f32[8,256]{1,0:T(8,128)S(1)} %get-tuple-element.46.rs_ref, bf16[2,256,2048]{2,1,0:T(8,128)(2,1)} %get-tuple-element.47.raw_ref), custom_call_target="tpu_custom_call" | custom-call | flops 1610612736 | bytes 8388608 | tf_op jit(solution)/shard_map/pallas_call | solution.py:531
  142.8 28.9 %all-to-all-done.2.x_ref = f32[16,304,128]{2,1,0:T(8,128)S(1)} async-done(((f32[16,304,128]{2,1,0:T(8,128)}), f32[16,304,128]{2,1,0:T(8,128)S(1)}, u32[]{:S(2)}, u32[]{:S(2)}) %all-to-all-start.2) | async-done | bytes 2490400 | tf_op jit(solution)/shard_map/all_to_all | solution.py:693
  171.7 1.5 shard_map.58
  173.2 6.9 %all-to-all-start.3 = ((f32[16,256,128]{2,1,0:T(8,128)}), f32[16,256,128]{2,1,0:T(8,128)}, u32[]{:S(2)}, u32[]{:S(2)}) async-start(f32[16,256,128]{2,1,0:T(8,128)} %get-tuple-element.52), calls=%async_computation.3 | async-start | bytes 4194304 | tf_op jit(solution)/shard_map/all_to_all | solution.py:693
  180.1 1.7 collective-permute-start.16
  181.8 0.8 collective-permute-done.16
  182.6 0.9 collective-permute-start.17
  184.3 1.7 collective-permute-done.17.refs_1_
  186.0 2.4 %collective-permute-done.18.refs_2_ = f32[96,128]{1,0:T(8,128)S(1)} collective-permute-done((f32[96,128]{1,0:T(8,128)S(1)}, f32[96,128]{1,0:T(8,128)S(1)}, u32[]{:S(2)}, u32[]{:S(2)}) %collective-permute-start.18) | collective-permute-done | bytes 49184 | tf_op jit(solution)/shard_map/ppermute | solution.py:651
  188.9 15.1 %shard_map.59 = (f32[256,256]{1,0:T(8,128)S(1)}, f32[512,256]{1,0:T(8,128)S(1)}) custom-call(s32[1]{0:T(128)} %bitcast.n_ref, f32[512,256]{1,0:T(8,128)S(1)} %get-tuple-element.44.p_ref, f32[96,128]{1,0:T(8,128)S(1)} %maximum_select_fusion.1.refs_0_, f32[96,128]{1,0:T(8,128)S(1)} %collective-permute-done.17.refs_1_, ...), custom_call_target="tpu_custom_call" | custom-call | flops 10000000000 | bytes 8388608 | tf_op jit(solution)/shard_map/pallas_call | solution.py:392
  204.0 1.6 all-to-all-done.3.x_ref
  205.7 4.3 %shard_map.60 = (bf16[2,256,2048]{2,1,0:T(8,128)(2,1)S(1)}, f32[8,8,256]{2,1,0:T(8,128)}) custom-call(f32[256,256]{1,0:T(8,128)S(1)} %get-tuple-element.51.w_ref, f32[16,256,128]{2,1,0:T(8,128)} %all-to-all-done.3.x_ref), custom_call_target="tpu_custom_call" | custom-call | flops 805306368 | bytes 8388608 | tf_op jit(solution)/shard_map/pallas_call | solution.py:568
  210.0 8.4 %all-to-all-start.4 = ((f32[8,8,256]{2,1,0:T(8,128)}), f32[8,8,256]{2,1,0:T(8,128)S(1)}, u32[]{:S(2)}, u32[]{:S(2)}) async-start(f32[8,8,256]{2,1,0:T(8,128)} %get-tuple-element.53), calls=%async_computation.4 | async-start | bytes 131072 | tf_op jit(solution)/shard_map/all_to_all | solution.py:693
  218.4 4.6 %shard_map.62 = f32[512,2048]{1,0:T(8,128)} custom-call(f32[512,256]{1,0:T(8,128)S(1)} %get-tuple-element.50.o_ref, bf16[2,256,2048]{2,1,0:T(8,128)(2,1)S(1)} %get-tuple-element.54.raw_ref, bf16[2,512,2048]{2,1,0:T(8,128)(2,1)} %get-tuple-element.43.b_ref), custom_call_target="tpu_custom_call" | custom-call | flops 1610612736 | bytes 8388608 | tf_op jit(solution)/shard_map/pallas_call | solution.py:593
  223.2 4.2 %shard_map.61 = bf16[512,2048]{1,0:T(8,128)(2,1)} custom-call(f32[512,256]{1,0:T(8,128)S(1)} %get-tuple-element.50.o_ref, f32[8,8,256]{2,1,0:T(8,128)S(1)} %all-to-all-done.4.sq_ref, bf16[2,256,2048]{2,1,0:T(8,128)(2,1)S(1)} %get-tuple-element.54.raw_ref, f32[512,2048]{1,0:T(8,128)} %shard_map.57.c_ref), custom_call_target="tpu_custom_call" | custom-call | flops 1610612736 | bytes 8388608 | tf_op jit(solution)/shard_map/pallas_call | solution.py:631
  (30 shorter events, 5.6 us)
Async XLA Ops:
  4.8 2.7 %collective-permute-start = (f32[2,128,256]{2,1,0:T(8,128)S(1)}, f32[2,128,256]{2,1,0:T(8,128)S(1)}, u32[]{:S(2)}, u32[]{:S(2)}) collective-permute-start(f32[2,128,256]{2,1,0:T(8,128)S(1)} %constant_dynamic-slice_fusion.1), channel_id=1, source_target_pairs={{0,1},{1,0},{2,3},{3,2},{4,5},{5,4},{6,7},{7,6},{8,9},{9,8},{10,11... | collective-permute-start | bytes 786440 | tf_op jit(solution)/shard_map/ppermute | solution.py:655
  7.6 4.8 %collective-permute-start.1 = (f32[128,256]{1,0:T(8,128)S(1)}, f32[128,256]{1,0:T(8,128)S(1)}, u32[]{:S(2)}, u32[]{:S(2)}) collective-permute-start(f32[128,256]{1,0:T(8,128)S(1)} %get-tuple-element.63), channel_id=1, source_target_pairs={{0,2},{1,3},{2,0},{3,1},{4,6},{5,7},{6,4},{7,5},{8,10},{9,11},{10,... | collective-permute-start | bytes 393224 | tf_op jit(solution)/shard_map/ppermute | solution.py:651
  8.9 5.6 %collective-permute-start.2 = (f32[128,256]{1,0:T(8,128)S(1)}, f32[128,256]{1,0:T(8,128)S(1)}, u32[]{:S(2)}, u32[]{:S(2)}) collective-permute-start(f32[128,256]{1,0:T(8,128)S(1)} %get-tuple-element.62), channel_id=1, source_target_pairs={{0,6},{1,7},{2,4},{3,5},{4,2},{5,3},{6,0},{7,1},{8,14},{9,15},{10,... | collective-permute-start | bytes 393224 | tf_op jit(solution)/shard_map/ppermute | solution.py:651
  14.6 3.9 %collective-permute-start.4 = (f32[128,256]{1,0:T(8,128)S(1)}, f32[128,256]{1,0:T(8,128)S(1)}, u32[]{:S(2)}, u32[]{:S(2)}) collective-permute-start(f32[128,256]{1,0:T(8,128)S(1)} %get-tuple-element.61), channel_id=1, source_target_pairs={{0,2},{1,3},{2,0},{3,1},{4,6},{5,7},{6,4},{7,5},{8,10},{9,11},{10,... | collective-permute-start | bytes 393224 | tf_op jit(solution)/shard_map/ppermute | solution.py:651
  14.7 5.1 %collective-permute-start.3 = (f32[128,256]{1,0:T(8,128)S(1)}, f32[128,256]{1,0:T(8,128)S(1)}, u32[]{:S(2)}, u32[]{:S(2)}) collective-permute-start(f32[128,256]{1,0:T(8,128)S(1)} %get-tuple-element.60), channel_id=1, source_target_pairs={{0,6},{1,7},{2,4},{3,5},{4,2},{5,3},{6,0},{7,1},{8,14},{9,15},{10,... | collective-permute-start | bytes 393224 | tf_op jit(solution)/shard_map/ppermute | solution.py:651
  19.8 3.9 %collective-permute-start.5 = (f32[2,128,256]{2,1,0:T(8,128)S(1)}, f32[2,128,256]{2,1,0:T(8,128)S(1)}, u32[]{:S(2)}, u32[]{:S(2)}) collective-permute-start(f32[2,128,256]{2,1,0:T(8,128)S(1)} %pad_maximum_fusion.1.mine_ref), channel_id=1, source_target_pairs={{0,1},{1,0},{2,3},{3,2},{4,5},{5,4},{6,7},{7,6},{8,9},{9,8},{10,11... | collective-permute-start | bytes 786440 | tf_op jit(solution)/shard_map/ppermute | solution.py:655
  68.4 29.9 %all-to-all-start.1 = ((f32[16,256,128]{2,1,0:T(8,128)}), f32[16,256,128]{2,1,0:T(8,128)S(1)}, u32[]{:S(2)}, u32[]{:S(2)}) async-start(f32[16,256,128]{2,1,0:T(8,128)} %get-tuple-element.36), calls=%async_computation.1 | async-start | bytes 4194304 | tf_op jit(solution)/shard_map/all_to_all | solution.py:693
  72.6 2.7 %collective-permute-start.6 = (f32[48,128]{1,0:T(8,128)S(1)}, f32[48,128]{1,0:T(8,128)S(1)}, u32[]{:S(2)}, u32[]{:S(2)}) collective-permute-start(f32[48,128]{1,0:T(8,128)S(1)} %get-tuple-element.33), channel_id=1, source_target_pairs={{0,1},{1,0},{2,3},{3,2},{4,5},{5,4},{6,7},{7,6},{8,9},{9,8},{10,11... | collective-permute-start | bytes 73736 | tf_op jit(solution)/shard_map/ppermute | solution.py:655
  75.4 3.2 %collective-permute-start.7 = (f32[96,128]{1,0:T(8,128)S(1)}, f32[96,128]{1,0:T(8,128)S(1)}, u32[]{:S(2)}, u32[]{:S(2)}) collective-permute-start(f32[96,128]{1,0:T(8,128)S(1)} %maximum_select_fusion.refs_0_), channel_id=1, source_target_pairs={{0,6},{1,7},{2,0},{3,1},{4,2},{5,3},{6,4},{7,5},{8,14},{9,15},{10,... | collective-permute-start | bytes 147464 | tf_op jit(solution)/shard_map/ppermute | solution.py:651
  77.2 4.7 %collective-permute-start.8 = (f32[96,128]{1,0:T(8,128)S(1)}, f32[96,128]{1,0:T(8,128)S(1)}, u32[]{:S(2)}, u32[]{:S(2)}) collective-permute-start(f32[96,128]{1,0:T(8,128)S(1)} %maximum_select_fusion.refs_0_), channel_id=1, source_target_pairs={{0,4},{1,5},{2,6},{3,7},{4,0},{5,1},{6,2},{7,3},{8,12},{9,13},{10,... | collective-permute-start | bytes 147464 | tf_op jit(solution)/shard_map/ppermute | solution.py:651
  77.6 4.9 %collective-permute-start.9 = (f32[96,128]{1,0:T(8,128)S(1)}, f32[96,128]{1,0:T(8,128)S(1)}, u32[]{:S(2)}, u32[]{:S(2)}) collective-permute-start(f32[96,128]{1,0:T(8,128)S(1)} %maximum_select_fusion.refs_0_), channel_id=1, source_target_pairs={{0,2},{1,3},{2,4},{3,5},{4,6},{5,7},{6,0},{7,1},{8,10},{9,11},{10,... | collective-permute-start | bytes 147464 | tf_op jit(solution)/shard_map/ppermute | solution.py:651
  104.6 6.4 %collective-permute-start.10 = (f32[2,136,256]{2,1,0:T(8,128)S(1)}, f32[2,136,256]{2,1,0:T(8,128)S(1)}, u32[]{:S(2)}, u32[]{:S(2)}) collective-permute-start(f32[2,136,256]{2,1,0:T(8,128)S(1)} %constant_dynamic-slice_fusion), channel_id=1, source_target_pairs={{0,1},{1,0},{2,3},{3,2},{4,5},{5,4},{6,7},{7,6},{8,9},{9,8},{10,11... | collective-permute-start | bytes 835592 | tf_op jit(solution)/shard_map/ppermute | solution.py:655
  111.0 9.0 %collective-permute-start.11 = (f32[136,256]{1,0:T(8,128)S(1)}, f32[136,256]{1,0:T(8,128)S(1)}, u32[]{:S(2)}, u32[]{:S(2)}) collective-permute-start(f32[136,256]{1,0:T(8,128)S(1)} %get-tuple-element.59), channel_id=1, source_target_pairs={{0,2},{1,3},{2,0},{3,1},{4,6},{5,7},{6,4},{7,5},{8,10},{9,11},{10,... | collective-permute-start | bytes 417800 | tf_op jit(solution)/shard_map/ppermute | solution.py:651
  111.6 8.5 %collective-permute-start.12 = (f32[136,256]{1,0:T(8,128)S(1)}, f32[136,256]{1,0:T(8,128)S(1)}, u32[]{:S(2)}, u32[]{:S(2)}) collective-permute-start(f32[136,256]{1,0:T(8,128)S(1)} %get-tuple-element.58), channel_id=1, source_target_pairs={{0,6},{1,7},{2,4},{3,5},{4,2},{5,3},{6,0},{7,1},{8,14},{9,15},{10,... | collective-permute-start | bytes 417800 | tf_op jit(solution)/shard_map/ppermute | solution.py:651
  120.1 4.3 %collective-permute-start.14 = (f32[136,256]{1,0:T(8,128)S(1)}, f32[136,256]{1,0:T(8,128)S(1)}, u32[]{:S(2)}, u32[]{:S(2)}) collective-permute-start(f32[136,256]{1,0:T(8,128)S(1)} %get-tuple-element.57), channel_id=1, source_target_pairs={{0,2},{1,3},{2,0},{3,1},{4,6},{5,7},{6,4},{7,5},{8,10},{9,11},{10,... | collective-permute-start | bytes 417800 | tf_op jit(solution)/shard_map/ppermute | solution.py:651
  120.6 5.1 %collective-permute-start.13 = (f32[136,256]{1,0:T(8,128)S(1)}, f32[136,256]{1,0:T(8,128)S(1)}, u32[]{:S(2)}, u32[]{:S(2)}) collective-permute-start(f32[136,256]{1,0:T(8,128)S(1)} %get-tuple-element.56), channel_id=1, source_target_pairs={{0,6},{1,7},{2,4},{3,5},{4,2},{5,3},{6,0},{7,1},{8,14},{9,15},{10,... | collective-permute-start | bytes 417800 | tf_op jit(solution)/shard_map/ppermute | solution.py:651
  125.7 3.6 %collective-permute-start.15 = (f32[2,136,256]{2,1,0:T(8,128)S(1)}, f32[2,136,256]{2,1,0:T(8,128)S(1)}, u32[]{:S(2)}, u32[]{:S(2)}) collective-permute-start(f32[2,136,256]{2,1,0:T(8,128)S(1)} %pad_maximum_fusion.mine_ref), channel_id=1, source_target_pairs={{0,1},{1,0},{2,3},{3,2},{4,5},{5,4},{6,7},{7,6},{8,9},{9,8},{10,11... | collective-permute-start | bytes 835592 | tf_op jit(solution)/shard_map/ppermute | solution.py:655
  134.5 37.2 %all-to-all-start.2 = ((f32[16,304,128]{2,1,0:T(8,128)}), f32[16,304,128]{2,1,0:T(8,128)S(1)}, u32[]{:S(2)}, u32[]{:S(2)}) async-start(f32[16,304,128]{2,1,0:T(8,128)} %get-tuple-element.45), calls=%async_computation.2 | async-start | bytes 4980736 | tf_op jit(solution)/shard_map/all_to_all | solution.py:693
  173.2 32.5 %all-to-all-start.3 = ((f32[16,256,128]{2,1,0:T(8,128)}), f32[16,256,128]{2,1,0:T(8,128)}, u32[]{:S(2)}, u32[]{:S(2)}) async-start(f32[16,256,128]{2,1,0:T(8,128)} %get-tuple-element.52), calls=%async_computation.3 | async-start | bytes 4194304 | tf_op jit(solution)/shard_map/all_to_all | solution.py:693
  180.1 2.6 %collective-permute-start.16 = (f32[48,128]{1,0:T(8,128)S(1)}, f32[48,128]{1,0:T(8,128)S(1)}, u32[]{:S(2)}, u32[]{:S(2)}) collective-permute-start(f32[48,128]{1,0:T(8,128)S(1)} %get-tuple-element.49), channel_id=1, source_target_pairs={{0,1},{1,0},{2,3},{3,2},{4,5},{5,4},{6,7},{7,6},{8,9},{9,8},{10,11... | collective-permute-start | bytes 73736 | tf_op jit(solution)/shard_map/ppermute | solution.py:655
  182.6 3.3 %collective-permute-start.17 = (f32[96,128]{1,0:T(8,128)S(1)}, f32[96,128]{1,0:T(8,128)S(1)}, u32[]{:S(2)}, u32[]{:S(2)}) collective-permute-start(f32[96,128]{1,0:T(8,128)S(1)} %maximum_select_fusion.1.refs_0_), channel_id=1, source_target_pairs={{0,6},{1,7},{2,0},{3,1},{4,2},{5,3},{6,4},{7,5},{8,14},{9,15},{10,... | collective-permute-start | bytes 147464 | tf_op jit(solution)/shard_map/ppermute | solution.py:651
  183.5 4.8 %collective-permute-start.18 = (f32[96,128]{1,0:T(8,128)S(1)}, f32[96,128]{1,0:T(8,128)S(1)}, u32[]{:S(2)}, u32[]{:S(2)}) collective-permute-start(f32[96,128]{1,0:T(8,128)S(1)} %maximum_select_fusion.1.refs_0_), channel_id=1, source_target_pairs={{0,4},{1,5},{2,6},{3,7},{4,0},{5,1},{6,2},{7,3},{8,12},{9,13},{10,... | collective-permute-start | bytes 147464 | tf_op jit(solution)/shard_map/ppermute | solution.py:651
  184.3 4.6 %collective-permute-start.19 = (f32[96,128]{1,0:T(8,128)S(1)}, f32[96,128]{1,0:T(8,128)S(1)}, u32[]{:S(2)}, u32[]{:S(2)}) collective-permute-start(f32[96,128]{1,0:T(8,128)S(1)} %maximum_select_fusion.1.refs_0_), channel_id=1, source_target_pairs={{0,2},{1,3},{2,4},{3,5},{4,6},{5,7},{6,0},{7,1},{8,10},{9,11},{10,... | collective-permute-start | bytes 147464 | tf_op jit(solution)/shard_map/ppermute | solution.py:651
  210.0 13.2 %all-to-all-start.4 = ((f32[8,8,256]{2,1,0:T(8,128)}), f32[8,8,256]{2,1,0:T(8,128)S(1)}, u32[]{:S(2)}, u32[]{:S(2)}) async-start(f32[8,8,256]{2,1,0:T(8,128)} %get-tuple-element.53), calls=%async_computation.4 | async-start | bytes 131072 | tf_op jit(solution)/shard_map/all_to_all | solution.py:693
where the time goes:
time: 228 us
  Pallas kernels  77.8 us (34%)
  waiting for transfers between devices  57.8 us (25%)
  starting transfers between devices  52.1 us (23%)
  blocking collectives  38.5 us (17%)
    all_to_all x1, blocking collectives, exchange(): return lax.all_to_all(x, axis, 0, 0, tiled=True)  38.5 us
    all_to_all x4, waiting for transfers between devices, exchange(): return lax.all_to_all(x, axis, 0, 0, tiled=True)  31.4 us
    pallas_call x2, Pallas kernels, inverse_factor(): call(cholesky_kernel, [SM, VM] + [VM] * len(pieces), [jax.ShapeDtypeStruc...  30.3 us
    all_to_all x4, starting transfers between devices, exchange(): return lax.all_to_all(x, axis, 0, 0, tiled=True)  23.2 us
    ppermute x14, waiting for transfers between devices, chip_permute(): return lax.ppermute(x, 'col', pairs)  20 us
    ppermute x6, starting transfers between devices, core_permute(): return lax.ppermute(x, 'col', [(k, k ^ 1) for k in range(2 * SIDE)])  15.5 us
    ppermute x14, starting transfers between devices, chip_permute(): return lax.ppermute(x, 'col', pairs)  13.4 us
    pallas_call x2, Pallas kernels, products(): call(kernel, [SM, VM, VM] + [ANY] * len(bigs), [jax.ShapeDtypeStruct(shap...  9.69 us
  transfers between devices with their start and end apart: 24, of which 22 were waited for; matrix products, arithmetic and copies ran while one was open for 0% of the time, Pallas kernels for 20%

commit v1 on v0

--- a/solution.py
+++ b/solution.py
@@ -37,13 +37,14 @@
     )
 
 
-def call(kernel, in_specs, out_shape, out_specs, scratch, cost):
+def call(kernel, in_specs, out_shape, out_specs, scratch, cost, aliases=None):
     return pl.pallas_call(
         kernel,
         in_specs=in_specs,
         out_specs=out_specs,
         out_shape=out_shape,
         scratch_shapes=scratch,
+        input_output_aliases=aliases or {},
         compiler_params=pltpu.CompilerParams(vmem_limit_bytes=VMEM_LIMIT),
         cost_estimate=pl.CostEstimate(
             flops=cost, transcendentals=0, bytes_accessed=8 * 1024 * 1024
@@ -72,13 +73,13 @@
     return pltpu.SemaphoreType.DMA(shape)
 
 
-def fetch(moves, sems):
+def fetch(moves, sems, count=CHUNKS):
     def copies(k):
         return [
             pltpu.make_async_copy(a, b, sems.at[k, n]) for n, (a, b) in enumerate(moves(k))
         ]
 
-    for k in range(CHUNKS):
+    for k in range(count):
         for copy in copies(k):
             copy.start()
 
@@ -89,7 +90,7 @@
     return wait
 
 
-def send(moves, sems):
+def send(moves, sems, count=CHUNKS):
     def copies(k):
         return [
             pltpu.make_async_copy(a, b, sems.at[k, n]) for n, (a, b) in enumerate(moves(k))
@@ -100,7 +101,7 @@
             copy.start()
 
     def finish():
-        for k in range(CHUNKS):
+        for k in range(count):
             for copy in copies(k):
                 copy.wait()
 
@@ -176,11 +177,10 @@
     )(*in_hbm(momentum, grads, basis))
 
 
-def store_products(inputs, outputs, scratch, block, scaled, direct):
+def store_products(inputs, outputs, scratch, block, scaled):
     n_ref, mine_ref, theirs_ref = inputs
     x_ref, p_ref, rs_ref = outputs
-    parts, t, shares, pair_of_p = scratch[:4]
-    held, sems = (None, None) if direct else scratch[4:]
+    parts, t, shares, pair_of_p = scratch
     core = lax.rem(n_ref[0], 2)
     parts[pl.ds(2 * core, 2)] = mine_ref[...]
     parts[pl.ds(2 - 2 * core, 2)] = theirs_ref[...]
@@ -203,23 +203,14 @@
     blocks = x_ref.shape[0] // CHUNKS
     shares[...] = share
     pair_of_p[0], pair_of_p[1] = pt
-    x = x_ref if direct else held
 
     def fill(k):
         r = dot3((pair_of_p[0], pair_of_p[1]), block(k), NN)
         for q in range(blocks):
-            x[k * blocks + q, :rank] = r[:, q * LANES : (q + 1) * LANES]
-            x[k * blocks + q, rank:] = shares[...]
-        if not direct:
-            start(k)
-
-    if not direct:
-        start, finish = send(
-            lambda k: [(held.at[columns(k, blocks)], x_ref.at[columns(k, blocks)])], sems
-        )
+            x_ref[k * blocks + q, :rank] = r[:, q * LANES : (q + 1) * LANES]
+            x_ref[k * blocks + q, rank:] = shares[...]
+
     each(fill)
-    if not direct:
-        finish()
 
 
 def first_products_kernel(
@@ -232,7 +223,7 @@
         return split(buffer_block(m, g, columns(k, m.shape[1] // CHUNKS)))
 
     store_products(
-        (n_ref, mine_ref, theirs_ref), (x_ref, p_ref, rs_ref), scratch, block, False, True
+        (n_ref, mine_ref, theirs_ref), (x_ref, p_ref, rs_ref), scratch, block, False
     )
 
 
@@ -257,11 +248,11 @@
         return b[0, :, c], b[1, :, c]
 
     store_products(
-        (n_ref, mine_ref, theirs_ref), (x_ref, p_ref, rs_ref), scratch, block, True, False
-    )
-
-
-def products(kernel, place, mine, theirs, bigs, held, peers, direct):
+        (n_ref, mine_ref, theirs_ref), (x_ref, p_ref, rs_ref), scratch, block, True
+    )
+
+
+def products(kernel, place, mine, theirs, bigs, held, peers):
     rows, cols = bigs[0].shape[-2:]
     _, height, rank = mine.shape
     tail = 3 * LANES // peers
@@ -270,11 +261,11 @@
         kernel,
         [SM, VM, VM] + [ANY] * len(bigs),
         [
-            jax.ShapeDtypeStruct(shape, F32) if direct else pltpu.HBM(shape, F32),
+            jax.ShapeDtypeStruct(shape, F32),
             jax.ShapeDtypeStruct((rows, rank), F32),
             jax.ShapeDtypeStruct((8, rank), F32),
         ],
-        [VM if direct else ANY, VM, VM],
+        [VM, VM, VM],
         held
         + [
             dma(CHUNKS, len(bigs)),
@@ -282,8 +273,7 @@
             pltpu.VMEM((3 * LANES, LANES), F32),
             pltpu.VMEM((tail, LANES), F32),
             pltpu.VMEM((2, rank, rows), BF16),
-        ]
-        + ([] if direct else [pltpu.VMEM(shape, F32), dma(CHUNKS, 1)]),
+        ],
         6 * rows * cols * rank,
     )(place, mine, theirs, *in_hbm(*bigs))
 
@@ -452,51 +442,69 @@
     )(o, w, x, *in_hbm(momentum, grads))
 
 
-def update_kernel(
-    o_ref, w_ref, rt_ref, m_ref, g_ref, raw_ref, b_ref, m, g, raw, b, came, sent
-):
-    wait = fetch(buffer_moves(m_ref, g_ref, m, g), came)
+def update_kernel(half, o_ref, w_ref, rt_ref, m_ref, g_ref, *refs):
+    raw_ref, b_ref, m, g, raw, b, came, sent = refs[-8:]
+    count = CHUNKS // 2
+    width = m.shape[1] // count
+    base = half * m.shape[1]
+
+    def placed(k):
+        if isinstance(k, int):
+            return pl.ds(base + k * width, width)
+        return pl.ds(pl.multiple_of(base + k * width, width), width)
+
+    def moves(k):
+        c, there = columns(k, width), placed(k)
+        return [
+            (m_ref.at[:, there], m.at[:, c]),
+            (g_ref.at[0, :, there], g.at[0, :, c]),
+            (g_ref.at[1, :, there], g.at[1, :, c]),
+        ]
+
+    wait = fetch(moves, came, count)
+    start, finish = send(
+        lambda k: [
+            (raw.at[:, :, columns(k, width)], raw_ref.at[:, :, placed(k)]),
+            (b.at[:, :, columns(k, width)], b_ref.at[:, :, placed(k)]),
+        ],
+        sent,
+        count,
+    )
     o = split((1.0 - KEEP_RATE) * o_ref[...])
     w = split(w_ref[...])
-    width = m.shape[1] // CHUNKS
-    start, finish = send(
-        lambda k: [
-            (a.at[:, :, columns(k, width)], r.at[:, :, columns(k, width)])
-            for a, r in ((raw, raw_ref), (b, b_ref))
-        ],
-        sent,
-    )
 
     def block(k):
-        c = columns(k, width)
-        now = split(dot3(w, (rt_ref[0, :, c], rt_ref[1, :, c]), NN))
+        c, there = columns(k, width), placed(k)
+        now = split(dot3(w, (rt_ref[0, :, there], rt_ref[1, :, there]), NN))
         raw[0, :, c], raw[1, :, c] = now
         wait(k)
         b[0, :, c], b[1, :, c] = split(buffer_block(m, g, c) - dot3(o, now, NN))
         start(k)
 
-    each(block)
+    each(block, count)
     finish()
 
 
-def second_buffer(o, w, rt, momentum, grads):
+def second_buffer(half, o, w, rt, momentum, grads, begun):
     rows, cols = momentum.shape
     rank = o.shape[1]
+    part = cols // 2
     return call(
-        update_kernel,
-        [VM] * 3 + [ANY] * 2,
+        functools.partial(update_kernel, half),
+        [VM] * 3 + [ANY] * (2 + len(begun)),
         [pair_in_hbm((rank, cols)), pair_in_hbm((rows, cols))],
         [ANY] * 2,
         [
-            pltpu.VMEM((rows, cols), F32),
-            pltpu.VMEM(grads.shape, BF16),
-            pltpu.VMEM((2, rank, cols), BF16),
-            pltpu.VMEM((2, rows, cols), BF16),
-            dma(CHUNKS, 3),
-            dma(CHUNKS, 2),
-        ],
-        9 * rows * cols * rank,
-    )(o, w, rt, *in_hbm(momentum, grads))
+            pltpu.VMEM((rows, part), F32),
+            pltpu.VMEM((2, rows, part), BF16),
+            pltpu.VMEM((2, rank, part), BF16),
+            pltpu.VMEM((2, rows, part), BF16),
+            dma(CHUNKS // 2, 3),
+            dma(CHUNKS // 2, 2),
+        ],
+        5 * rows * cols * rank,
+        {5: 0, 6: 1} if begun else None,
+    )(o, w, rt, *in_hbm(momentum, grads), *in_hbm(*begun))
 
 
 def write_out(value, out_ref, buffer, sems):
@@ -514,133 +522,95 @@
     finish()
 
 
-def change_kernel(factor, o_ref, rs_ref, raw_ref, c_ref, raw, buffer, came, sent):
-    wait = fetch(pair_moves(raw_ref, raw), came)
-    o = split(o_ref[...] * (factor * rs_ref[:1]))
+def last_raw_kernel(
+    o_ref, w_ref, x_ref, b_ref, raw_ref, sq_ref, s_ref, x, b, buffer, total, came, sent
+):
+    blocks = x_ref.shape[0] // CHUNKS
+    bring = pair_moves(b_ref, b)
+    wait = fetch(
+        lambda k: [(x_ref.at[columns(k, blocks)], x.at[columns(k, blocks)])] + bring(k),
+        came,
+    )
+    total[...] = jnp.zeros_like(total)
+    o = split((1.0 - KEEP_RATE) * o_ref[...])
+    w = split(w_ref[...])
 
     def value(k, c):
         wait(k)
-        return dot3(o, (raw[0, :, c], raw[1, :, c]), NN)
-
-    write_out(value, c_ref, buffer, sent)
-
-
-def first_change(factor, o, rs, raw):
+        part = jnp.concatenate([x[k * blocks + q] for q in range(blocks)], axis=1)
+        raw = dot3(w, split(part), NN)
+        now = split(raw)
+        raw_ref[0, :, c], raw_ref[1, :, c] = now
+        total[...] += jnp.sum(raw * raw, axis=1, keepdims=True)
+        return b[0, :, c].astype(F32) + b[1, :, c].astype(F32) - dot3(o, now, NN)
+
+    write_out(value, s_ref, buffer, sent)
+    n = w_ref.shape[0]
+    squares = jnp.where(same(n), jnp.broadcast_to(total[:, :1], (n, n)), 0.0)
+    row = jnp.sum(squares, axis=0, keepdims=True)
+    for k in range(sq_ref.shape[0]):
+        sq_ref[k] = jnp.broadcast_to(row, (8, n))
+
+
+def last_raw(o, w, x, b, peers):
+    _, rows, cols = b.shape
+    rank = w.shape[0]
+    return call(
+        last_raw_kernel,
+        [VM, VM, ANY, ANY],
+        [
+            pair((rank, cols)),
+            jax.ShapeDtypeStruct((peers, 8, rank), F32),
+            pltpu.HBM((rows, cols), F32),
+        ],
+        [VM, VM, ANY],
+        [
+            pltpu.VMEM(x.shape, F32),
+            pltpu.VMEM(b.shape, BF16),
+            pltpu.VMEM((rows, cols), F32),
+            pltpu.VMEM((rank, LANES), F32),
+            dma(CHUNKS, 2),
+            dma(CHUNKS, 1),
+        ],
+        9 * rows * cols * rank,
+    )(o, w, *in_hbm(x), *in_hbm(b))
+
+
+def change_kernel(
+    factor, o1_ref, rs_ref, raw1_ref, o_ref, sq_ref, raw_ref, out_ref, raw1, buffer, came, sent
+):
+    wait = fetch(pair_moves(raw1_ref, raw1), came)
+    total = sq_ref[0, :1]
+    for k in range(1, sq_ref.shape[0]):
+        total = total + sq_ref[k, :1]
+    o = split(o_ref[...] * (factor * lax.rsqrt(total + NORM_EPS)))
+    o1 = split(o1_ref[...] * (factor * rs_ref[:1]))
+
+    def value(k, c):
+        wait(k)
+        return dot3(o1, (raw1[0, :, c], raw1[1, :, c]), NN) + dot3(
+            o, (raw_ref[0, :, c], raw_ref[1, :, c]), NN
+        )
+
+    write_out(value, out_ref, buffer, sent)
+
+
+def both_changes(factor, o1, rs, raw1, o, sq, raw):
     rows, rank = o.shape
     cols = raw.shape[2]
     return call(
         functools.partial(change_kernel, factor),
-        [VM, VM, ANY],
-        pltpu.HBM((rows, cols), F32),
-        ANY,
-        [
-            pltpu.VMEM(raw.shape, BF16),
-            pltpu.VMEM((rows, cols), F32),
-            dma(CHUNKS, 1),
-            dma(CHUNKS, 1),
-        ],
-        6 * rows * cols * rank,
-    )(o, rs, *in_hbm(raw))
-
-
-def last_raw_kernel(w_ref, x_ref, raw_ref, sq_ref, total):
-    blocks = x_ref.shape[0] // CHUNKS
-    n = w_ref.shape[0]
-    total[...] = jnp.zeros_like(total)
-
-    def block(k):
-        c = columns(k, blocks * LANES)
-        part = jnp.concatenate([x_ref[k * blocks + q] for q in range(blocks)], axis=1)
-        raw = dot3(split(w_ref[...]), split(part), NN)
-        raw_ref[0, :, c], raw_ref[1, :, c] = split(raw)
-        total[...] += jnp.sum(raw * raw, axis=1, keepdims=True)
-
-    each(block)
-    squares = jnp.where(same(n), jnp.broadcast_to(total[:, :1], (n, n)), 0.0)
-    row = jnp.sum(squares, axis=0, keepdims=True)
-    for k in range(sq_ref.shape[0]):
-        sq_ref[k] = jnp.broadcast_to(row, (8, n))
-
-
-def last_raw(w, x, peers):
-    rank = w.shape[0]
-    cols = x.shape[0] * LANES
-    return call(
-        last_raw_kernel,
-        [VM] * 2,
-        [pair((rank, cols)), jax.ShapeDtypeStruct((peers, 8, rank), F32)],
-        [VM] * 2,
-        [pltpu.VMEM((rank, LANES), F32)],
-        6 * rank * cols * rank,
-    )(w, *in_hbm(x))
-
-
-def state_kernel(o_ref, raw_ref, b_ref, s_ref, b, buffer, came, sent):
-    wait = fetch(pair_moves(b_ref, b), came)
-    o = split((1.0 - KEEP_RATE) * o_ref[...])
-
-    def value(k, c):
-        part = dot3(o, (raw_ref[0, :, c], raw_ref[1, :, c]), NN)
-        wait(k)
-        return b[0, :, c].astype(F32) + b[1, :, c].astype(F32) - part
-
-    write_out(value, s_ref, buffer, sent)
-
-
-def last_state(o, raw, b):
-    _, rows, cols = b.shape
-    rank = o.shape[1]
-    return call(
-        state_kernel,
-        [VM, VM, ANY],
-        pltpu.HBM((rows, cols), F32),
-        ANY,
-        [
-            pltpu.VMEM(b.shape, BF16),
-            pltpu.VMEM((rows, cols), F32),
-            dma(CHUNKS, 1),
-            dma(CHUNKS, 1),
-        ],
-        6 * rows * cols * rank,
-    )(o, raw, *in_hbm(b))
-
-
-def last_change_kernel(
-    factor, o_ref, sq_ref, raw_ref, c_ref, out_ref, held, buffer, came, sent
-):
-    width = held.shape[1] // CHUNKS
-    wait = fetch(
-        lambda k: [(c_ref.at[:, columns(k, width)], held.at[:, columns(k, width)])], came
-    )
-    total = sq_ref[0, :1]
-    for k in range(1, sq_ref.shape[0]):
-        total = total + sq_ref[k, :1]
-    o = split(o_ref[...] * (factor * lax.rsqrt(total + NORM_EPS)))
-
-    def value(k, c):
-        part = dot3(o, (raw_ref[0, :, c], raw_ref[1, :, c]), NN)
-        wait(k)
-        return held[:, c] + part
-
-    write_out(value, out_ref, buffer, sent)
-
-
-def last_change(factor, o, sq, raw, change):
-    rows, cols = change.shape
-    rank = o.shape[1]
-    return call(
-        functools.partial(last_change_kernel, factor),
-        [VM, VM, VM, ANY],
+        [VM, VM, ANY, VM, VM, VM],
         pltpu.HBM((rows, cols), BF16),
         ANY,
         [
-            pltpu.VMEM((rows, cols), F32),
+            pltpu.VMEM(raw1.shape, BF16),
             pltpu.VMEM((rows, cols), BF16),
             dma(CHUNKS, 1),
             dma(CHUNKS, 1),
         ],
-        6 * rows * cols * rank,
-    )(o, sq, raw, *in_hbm(change))
+        12 * rows * cols * rank,
+    )(o1, rs, *in_hbm(raw1), o, sq, raw)
 
 
 SIDE = 4
@@ -668,14 +638,14 @@
     mine = lax.dynamic_slice_in_dim(parts, 2 * core, 2, 0)
     theirs = lax.dynamic_slice_in_dim(parts, 2 - 2 * core, 2, 0)
     mine = mine + core_permute(theirs)
-    a, b = mine[0], mine[1]
-    near_a, far_b, beside = lax.optimization_barrier(
-        (chip_permute(a, near), chip_permute(b, far), beside)
-    )
-    a, b = a + near_a, b + far_b
-    a, b = a + chip_permute(a, far), b + chip_permute(b, near)
+    a, b, done = mine[0], mine[1], []
+    for half, moves in enumerate(((near, far), (far, near))):
+        from_a, from_b, done = lax.optimization_barrier(
+            (chip_permute(a, moves[0]), chip_permute(b, moves[1]), beside(half, done))
+        )
+        a, b = a + from_a, b + from_b
     mine = jnp.stack([a, b])
-    return mine, core_permute(mine), beside
+    return mine, core_permute(mine), done
 
 
 def by_chip(part):
@@ -693,11 +663,10 @@
     return lax.all_to_all(x, axis, 0, 0, tiled=True)
 
 
-def row_total(blocks, p, place, beside):
-    got, beside = lax.optimization_barrier((exchange(blocks, "row"), beside))
-    own, part = spread_sum(got, p.shape[1])
+def row_total(blocks, p, place):
+    own, part = spread_sum(exchange(blocks, "row"), p.shape[1])
     total = exchange(own, "row")
-    return total, *inverse_factor(by_chip(part), place, p), beside
+    return total, *inverse_factor(by_chip(part), place, p)
 
 
 def shards(momentum, grads, basis):
@@ -709,25 +678,24 @@
 
     held = [pltpu.VMEM((rows, cols), F32), pltpu.VMEM((1, rows, cols), BF16)]
     part = first_projection(momentum, grads, basis)
-    mine, theirs, _ = col_sum(part.reshape(4, rows // 4, rank), [])
+    mine, theirs, _ = col_sum(part.reshape(4, rows // 4, rank), lambda half, done: [])
     x1, p1, _ = products(
-        first_products_kernel, place, mine, theirs, [momentum, grads], held, peers, True
-    )
-    x1, w1, o1, _ = row_total(x1, p1, place, [])
+        first_products_kernel, place, mine, theirs, [momentum, grads], held, peers
+    )
+    x1, w1, o1 = row_total(x1, p1, place)
     part, rt1 = middle(o1, w1, x1, momentum, grads)
     mine, theirs, (raw1, buffer) = col_sum(
-        part, second_buffer(o1, w1, rt1, momentum, grads)
+        part,
+        lambda half, done: second_buffer(half, o1, w1, rt1, momentum, grads, done),
     )
     held = [pltpu.VMEM((2, rows, cols), BF16)]
     x2, p2, rs1 = products(
-        second_products_kernel, place, mine, theirs, [buffer], held, peers, False
-    )
-    change1 = first_change(factor, o1, rs1, raw1)
-    x2, w2, o2, change1 = row_total(x2, p2, place, change1)
-    raw2, sq2 = last_raw(w2, x2, peers)
+        second_products_kernel, place, mine, theirs, [buffer], held, peers
+    )
+    x2, w2, o2 = row_total(x2, p2, place)
+    raw2, sq2, state = last_raw(o2, w2, x2, buffer, peers)
     sq2 = exchange(sq2, "col")
-    state = last_state(o2, raw2, buffer)
-    change = last_change(factor, o2, sq2, raw2, change1)
+    change = both_changes(factor, o1, rs1, raw1, o2, sq2, raw2)
     return change, state
 
 

time: 228 us -> 224 us (0.982)
  blocking collectives: 38.5 us -> 86.2 us
  waiting for transfers between devices: 57.8 us -> 22.5 us
  starting transfers between devices: 52.1 us -> 39.5 us
  Pallas kernels: 77.8 us -> 73.6 us
    all_to_all x1 -> x3, blocking collectives: 38.5 us -> 86.2 us  [exchange(): return lax.all_to_all(x, axis, 0, 0, tiled=True)]
    all_to_all x4 -> x2, waiting for transfers between devices: 31.4 us -> 2.49 us  [exchange(): return lax.all_to_all(x, axis, 0, 0, tiled=True)]
    all_to_all x4 -> x2, starting transfers between devices: 23.2 us -> 8.91 us  [exchange(): return lax.all_to_all(x, axis, 0, 0, tiled=True)]
    ppermute x14, waiting for transfers between devices: 20 us -> 13.6 us  [chip_permute(): return lax.ppermute(x, 'col', pairs)]
    pallas_call x5 -> x4, Pallas kernels: 24.3 us -> 20.9 us  [the longest x2 8.75 us: second_buffer(): call(functools.partial(update_kernel, half), [VM] * 3 + [ANY] * (2 + len(...]
  transfers between devices with their start and end apart: 24 -> 22, of which waited for: 22 -> 19; matrix products, arithmetic and copies ran while one was open for 0% -> 0% of each run, Pallas kernels for 20% -> 17%
where the time goes in v1:
time: 224 us; the launch traced here: 223 us
  blocking collectives  86.2 us (38%)
  Pallas kernels  73.6 us (33%)
  starting transfers between devices  39.5 us (18%)
  waiting for transfers between devices  22.5 us (10%)
    all_to_all x3, blocking collectives, exchange(): return lax.all_to_all(x, axis, 0, 0, tiled=True)  86.2 us
    pallas_call x2, Pallas kernels, inverse_factor(): call(cholesky_kernel, [SM, VM] + [VM] * len(pieces), [jax.ShapeDtypeStruc...  30.3 us
    ppermute x6, starting transfers between devices, core_permute(): return lax.ppermute(x, 'col', [(k, k ^ 1) for k in range(2 * SIDE)])  15.5 us
    ppermute x14, starting transfers between devices, chip_permute(): return lax.ppermute(x, 'col', pairs)  15.1 us
    ppermute x14, waiting for transfers between devices, chip_permute(): return lax.ppermute(x, 'col', pairs)  13.6 us
    all_to_all x2, starting transfers between devices, exchange(): return lax.all_to_all(x, axis, 0, 0, tiled=True)  8.91 us
    pallas_call x2, Pallas kernels, products(): call(kernel, [SM, VM, VM] + [ANY] * len(bigs), [jax.ShapeDtypeStruct(shap...  8.86 us
    pallas_call x2, Pallas kernels, second_buffer(): call(functools.partial(update_kernel, half), [VM] * 3 + [ANY] * (2 + len(...  8.75 us
  transfers between devices with their start and end apart: 22, of which 19 were waited for; matrix products, arithmetic and copies ran while one was open for 0% of the time, Pallas kernels for 17%

profile of v1, /device:TPU:1, one launch (start us, length us, event | category | flops | bytes accessed | tf_op | source)
XLA Modules:
  0.0 223.2 jit_solution(2936241815922009792)
XLA Ops:
  0.6 4.1 %shard_map.50 = f32[512,256]{1,0:T(8,128)S(1)} custom-call(f32[512,2048]{1,0:T(8,128)} %m_ref.9, bf16[2,512,2048]{2,1,0:T(8,128)(2,1)} %g_ref.9, f32[2048,256]{1,0:T(8,128)} %v_ref.1), custom_call_target="tpu_custom_call" | custom-call | flops 1610612736 | bytes 8388608 | tf_op jit(solution)/shard_map/pallas_call | solution.py:165
  4.8 1.5 collective-permute-start
  6.3 1.2 collective-permute-done
  7.6 2.6 %collective-permute-start.2 = (f32[128,256]{1,0:T(8,128)S(1)}, f32[128,256]{1,0:T(8,128)S(1)}, u32[]{:S(2)}, u32[]{:S(2)}) collective-permute-start(f32[128,256]{1,0:T(8,128)S(1)} %get-tuple-element.76), channel_id=1, source_target_pairs={{0,6},{1,7},{2,4},{3,5},{4,2},{5,3},{6,0},{7,1},{8,14},{9,15},{10,... | collective-permute-start | bytes 393224 | tf_op jit(solution)/shard_map/ppermute | solution.py:621
  10.2 3.3 %collective-permute-done.2 = f32[128,256]{1,0:T(8,128)S(1)} collective-permute-done((f32[128,256]{1,0:T(8,128)S(1)}, f32[128,256]{1,0:T(8,128)S(1)}, u32[]{:S(2)}, u32[]{:S(2)}) %collective-permute-start.2) | collective-permute-done | bytes 131104 | tf_op jit(solution)/shard_map/ppermute | solution.py:621
  13.6 1.0 collective-permute-done.1
  14.6 1.6 collective-permute-start.3
  16.2 3.5 %collective-permute-done.3 = f32[128,256]{1,0:T(8,128)S(1)} collective-permute-done((f32[128,256]{1,0:T(8,128)S(1)}, f32[128,256]{1,0:T(8,128)S(1)}, u32[]{:S(2)}, u32[]{:S(2)}) %collective-permute-start.3) | collective-permute-done | bytes 131104 | tf_op jit(solution)/shard_map/ppermute | solution.py:621
  20.1 2.7 %collective-permute-start.5 = (f32[2,128,256]{2,1,0:T(8,128)S(1)}, f32[2,128,256]{2,1,0:T(8,128)S(1)}, u32[]{:S(2)}, u32[]{:S(2)}) collective-permute-start(f32[2,128,256]{2,1,0:T(8,128)S(1)} %pad_maximum_fusion.1.mine_ref), channel_id=1, source_target_pairs={{0,1},{1,0},{2,3},{3,2},{4,5},{5,4},{6,7},{7,6},{8,9},{9,8},{10,11... | collective-permute-start | bytes 786440 | tf_op jit(solution)/shard_map/ppermute | solution.py:625
  22.8 1.2 collective-permute-done.5.theirs_ref
  24.0 4.6 %shard_map.51 = (f32[16,304,128]{2,1,0:T(8,128)S(1)}, f32[512,256]{1,0:T(8,128)S(1)}, f32[8,256]{1,0:T(8,128)}) custom-call(s32[1]{0:T(128)} %bitcast.n_ref, f32[2,128,256]{2,1,0:T(8,128)S(1)} %pad_maximum_fusion.1.mine_ref, f32[2,128,256]{2,1,0:T(8,128)S(1)} %collective-permute-done.5.theirs_ref, f32[512,2048]{1,0:T(8,128)} %m_ref.9, ...), custom_call_target="tpu_custom_call" | custom-call | flops 1610612736 | bytes 8388608 | tf_op jit(solution)/shard_map/pallas_call | solution.py:260
  28.6 38.5 %all_to_all.25.x_ref = f32[16,304,128]{2,1,0:T(8,128)S(1)} all-to-all(f32[16,304,128]{2,1,0:T(8,128)S(1)} %get-tuple-element.41), channel_id=1, replica_groups=mesh['row'=16,'col'=8] {'row'}, dimensions={0} | all-to-all | bytes 4980736 | tf_op jit(solution)/shard_map/all_to_all | solution.py:663
  67.1 1.5 shard_map.52
  68.6 4.2 %all-to-all-start.1 = ((f32[16,256,128]{2,1,0:T(8,128)}), f32[16,256,128]{2,1,0:T(8,128)S(1)}, u32[]{:S(2)}, u32[]{:S(2)}) async-start(f32[16,256,128]{2,1,0:T(8,128)} %get-tuple-element.45), calls=%async_computation.1 | async-start | bytes 4194304 | tf_op jit(solution)/shard_map/all_to_all | solution.py:663
  72.9 1.9 collective-permute-start.6
  74.8 0.8 collective-permute-done.6
  75.6 2.6 %collective-permute-start.8 = (f32[96,128]{1,0:T(8,128)S(1)}, f32[96,128]{1,0:T(8,128)S(1)}, u32[]{:S(2)}, u32[]{:S(2)}) collective-permute-start(f32[96,128]{1,0:T(8,128)S(1)} %maximum_select_fusion.refs_0_), channel_id=1, source_target_pairs={{0,4},{1,5},{2,6},{3,7},{4,0},{5,1},{6,2},{7,3},{8,12},{9,13},{10,... | collective-permute-start | bytes 147464 | tf_op jit(solution)/shard_map/ppermute | solution.py:621
  78.6 1.5 collective-permute-done.9.refs_3_
  80.1 0.8 collective-permute-done.8.refs_2_
  80.9 1.0 collective-permute-done.7.refs_1_
  81.8 15.1 %shard_map.53 = (f32[256,256]{1,0:T(8,128)S(1)}, f32[512,256]{1,0:T(8,128)S(1)}) custom-call(s32[1]{0:T(128)} %bitcast.n_ref, f32[512,256]{1,0:T(8,128)S(1)} %get-tuple-element.40.p_ref, f32[96,128]{1,0:T(8,128)S(1)} %maximum_select_fusion.refs_0_, f32[96,128]{1,0:T(8,128)S(1)} %collective-permute-done.7.refs_1_, ...), custom_call_target="tpu_custom_call" | custom-call | flops 10000000000 | bytes 8388608 | tf_op jit(solution)/shard_map/pallas_call | solution.py:382
  97.0 1.5 all-to-all-done.1.x_ref
  98.5 6.3 %shard_map.54 = (f32[4,136,256]{2,1,0:T(8,128)S(1)}, bf16[2,256,2048]{2,1,0:T(8,128)(2,1)S(1)}) custom-call(f32[512,256]{1,0:T(8,128)S(1)} %get-tuple-element.43.o_ref.o1_ref, f32[256,256]{1,0:T(8,128)S(1)} %get-tuple-element.44.w_ref, f32[16,256,128]{2,1,0:T(8,128)S(1)} %all-to-all-done.1.x_ref, f32[512,2048]{1,0:T(8,128)} %m_ref.9, bf16[2,512,2048]{2,1,0:T(8,128)(2,1)} %g_ref.9), custom_call_target="tpu_custom_call" | custom-call | flops 2684354560 | bytes 8388608 | tf_op jit(solution)/shard_map/pallas_call | solution.py:429
  104.9 5.2 %collective-permute-start.10 = (f32[2,136,256]{2,1,0:T(8,128)S(1)}, f32[2,136,256]{2,1,0:T(8,128)S(1)}, u32[]{:S(2)}, u32[]{:S(2)}) collective-permute-start(f32[2,136,256]{2,1,0:T(8,128)S(1)} %constant_dynamic-slice_fusion), channel_id=1, source_target_pairs={{0,1},{1,0},{2,3},{3,2},{4,5},{5,4},{6,7},{7,6},{8,9},{9,8},{10,11... | collective-permute-start | bytes 835592 | tf_op jit(solution)/shard_map/ppermute | solution.py:625
  110.0 1.2 collective-permute-done.10
  111.3 1.5 collective-permute-start.12
  112.9 4.4 %shard_map.55 = (bf16[2,256,2048]{2,1,0:T(8,128)(2,1)}, bf16[2,512,2048]{2,1,0:T(8,128)(2,1)}) custom-call(f32[512,256]{1,0:T(8,128)S(1)} %get-tuple-element.43.o_ref.o1_ref, f32[256,256]{1,0:T(8,128)S(1)} %get-tuple-element.44.w_ref, bf16[2,256,2048]{2,1,0:T(8,128)(2,1)S(1)} %get-tuple-element.47.rt_ref, f32[512,2048]{1,0:T(8,128)} %m_ref.9, ...), custom_call_target="tpu_custom_call" | custom-call | flops 1342177280 | bytes 8388608 | tf_op jit(solution)/shard_map/pallas_call | solution.py:492
  117.5 1.5 collective-permute-start.13
  119.1 0.4 collective-permute-start.14
  119.5 4.4 %shard_map.56 = (bf16[2,256,2048]{2,1,0:T(8,128)(2,1)}, bf16[2,512,2048]{2,1,0:T(8,128)(2,1)}) custom-call(f32[512,256]{1,0:T(8,128)S(1)} %get-tuple-element.43.o_ref.o1_ref, f32[256,256]{1,0:T(8,128)S(1)} %get-tuple-element.44.w_ref, bf16[2,256,2048]{2,1,0:T(8,128)(2,1)S(1)} %get-tuple-element.47.rt_ref, ...), custom_call_target="tpu_custom_call", output_to_operand_aliasing={{0}: (5, {}), {1}: (6, {})} | custom-call | flops 1342177280 | bytes 8388608 | tf_op jit(solution)/shard_map/pallas_call | solution.py:492
  123.9 1.8 collective-permute-start.15
  125.8 1.2 collective-permute-done.15.theirs_ref
  127.0 4.3 %shard_map.57 = (f32[16,304,128]{2,1,0:T(8,128)S(1)}, f32[512,256]{1,0:T(8,128)S(1)}, f32[8,256]{1,0:T(8,128)S(1)}) custom-call(s32[1]{0:T(128)} %bitcast.n_ref, f32[2,136,256]{2,1,0:T(8,128)S(1)} %pad_maximum_fusion.mine_ref, f32[2,136,256]{2,1,0:T(8,128)S(1)} %collective-permute-done.15.theirs_ref, bf16[2,512,2048]{2,1,0:T(8,128)(2,1)} %get-tuple-element.58.b_ref), custom_call_target="tpu_custom_call" | custom-call | flops 1610612736 | bytes 8388608 | tf_op jit(solution)/shard_map/pallas_call | solution.py:260
  131.3 34.2 %all_to_all.26.x_ref = f32[16,304,128]{2,1,0:T(8,128)S(1)} all-to-all(f32[16,304,128]{2,1,0:T(8,128)S(1)} %get-tuple-element.62), channel_id=1, replica_groups=mesh['row'=16,'col'=8] {'row'}, dimensions={0} | all-to-all | bytes 4980736 | tf_op jit(solution)/shard_map/all_to_all | solution.py:663
  165.5 1.5 shard_map.58
  167.0 4.7 %all-to-all-start.3 = ((f32[16,256,128]{2,1,0:T(8,128)}), f32[16,256,128]{2,1,0:T(8,128)}, u32[]{:S(2)}, u32[]{:S(2)}) async-start(f32[16,256,128]{2,1,0:T(8,128)} %get-tuple-element.66), calls=%async_computation.3 | async-start | bytes 4194304 | tf_op jit(solution)/shard_map/all_to_all | solution.py:663
  171.7 2.4 %collective-permute-start.16 = (f32[48,128]{1,0:T(8,128)S(1)}, f32[48,128]{1,0:T(8,128)S(1)}, u32[]{:S(2)}, u32[]{:S(2)}) collective-permute-start(f32[48,128]{1,0:T(8,128)S(1)} %get-tuple-element.63), channel_id=1, source_target_pairs={{0,1},{1,0},{2,3},{3,2},{4,5},{5,4},{6,7},{7,6},{8,9},{9,8},{10,11... | collective-permute-start | bytes 73736 | tf_op jit(solution)/shard_map/ppermute | solution.py:625
  174.1 0.8 collective-permute-done.16
  175.0 1.1 collective-permute-start.19
  176.1 1.5 collective-permute-start.18
  177.6 1.7 collective-permute-start.17
  179.5 1.4 collective-permute-done.18.refs_2_
  180.9 0.3 collective-permute-done.17.refs_1_
  181.2 15.1 %shard_map.59 = (f32[256,256]{1,0:T(8,128)S(1)}, f32[512,256]{1,0:T(8,128)S(1)}) custom-call(s32[1]{0:T(128)} %bitcast.n_ref, f32[512,256]{1,0:T(8,128)S(1)} %get-tuple-element.61.p_ref, f32[96,128]{1,0:T(8,128)S(1)} %maximum_select_fusion.1.refs_0_, f32[96,128]{1,0:T(8,128)S(1)} %collective-permute-done.17.refs_1_, ...), custom_call_target="tpu_custom_call" | custom-call | flops 10000000000 | bytes 8388608 | tf_op jit(solution)/shard_map/pallas_call | solution.py:382
  196.4 1.0 all-to-all-done.3.x_ref
  197.3 6.3 %shard_map.60 = (bf16[2,256,2048]{2,1,0:T(8,128)(2,1)S(1)}, f32[8,8,256]{2,1,0:T(8,128)S(1)}, f32[512,2048]{1,0:T(8,128)}) custom-call(f32[512,256]{1,0:T(8,128)S(1)} %get-tuple-element.64.o_ref, f32[256,256]{1,0:T(8,128)S(1)} %get-tuple-element.65.w_ref, f32[16,256,128]{2,1,0:T(8,128)} %all-to-all-done.3.x_ref, bf16[2,512,2048]{2,1,0:T(8,128)(2,1)} %get-tuple-element.58.b_ref), custom_call_target="tpu_custom_call" | custom-call | flops 2415919104 | bytes 8388608 | tf_op jit(solution)/shard_map/pallas_call | solution.py:558
  203.7 13.5 %all_to_all.27.sq_ref = f32[8,8,256]{2,1,0:T(8,128)S(1)} all-to-all(f32[8,8,256]{2,1,0:T(8,128)S(1)} %get-tuple-element.67), channel_id=1, replica_groups=mesh['row'=16,'col'=8] {'col'}, dimensions={0} | all-to-all | bytes 131072 | tf_op jit(solution)/shard_map/all_to_all | solution.py:663
  217.2 5.8 %shard_map.61 = bf16[512,2048]{1,0:T(8,128)(2,1)} custom-call(f32[512,256]{1,0:T(8,128)S(1)} %get-tuple-element.43.o_ref.o1_ref, f32[8,256]{1,0:T(8,128)S(1)} %get-tuple-element.59.rs_ref, bf16[2,256,2048]{2,1,0:T(8,128)(2,1)} %get-tuple-element.60.raw1_ref, f32[512,256]{1,0:T(8,128)S(1)} %get-tuple-element.64.o_ref, f32[8,8,256]{2,1,0:T(8,128)S(1)} %all_to_all.27.sq_ref, ...), custom_call_target="tpu_custom_call" | custom-call | flops 3221225472 | bytes 8388608 | tf_op jit(solution)/shard_map/pallas_call | solution.py:601
  (26 shorter events, 1.5 us)
Async XLA Ops:
  4.8 2.7 %collective-permute-start = (f32[2,128,256]{2,1,0:T(8,128)S(1)}, f32[2,128,256]{2,1,0:T(8,128)S(1)}, u32[]{:S(2)}, u32[]{:S(2)}) collective-permute-start(f32[2,128,256]{2,1,0:T(8,128)S(1)} %constant_dynamic-slice_fusion.1), channel_id=1, source_target_pairs={{0,1},{1,0},{2,3},{3,2},{4,5},{5,4},{6,7},{7,6},{8,9},{9,8},{10,11... | collective-permute-start | bytes 786440 | tf_op jit(solution)/shard_map/ppermute | solution.py:625
  7.6 6.0 %collective-permute-start.2 = (f32[128,256]{1,0:T(8,128)S(1)}, f32[128,256]{1,0:T(8,128)S(1)}, u32[]{:S(2)}, u32[]{:S(2)}) collective-permute-start(f32[128,256]{1,0:T(8,128)S(1)} %get-tuple-element.76), channel_id=1, source_target_pairs={{0,6},{1,7},{2,4},{3,5},{4,2},{5,3},{6,0},{7,1},{8,14},{9,15},{10,... | collective-permute-start | bytes 393224 | tf_op jit(solution)/shard_map/ppermute | solution.py:621
  10.2 4.4 %collective-permute-start.1 = (f32[128,256]{1,0:T(8,128)S(1)}, f32[128,256]{1,0:T(8,128)S(1)}, u32[]{:S(2)}, u32[]{:S(2)}) collective-permute-start(f32[128,256]{1,0:T(8,128)S(1)} %get-tuple-element.77), channel_id=1, source_target_pairs={{0,2},{1,3},{2,0},{3,1},{4,6},{5,7},{6,4},{7,5},{8,10},{9,11},{10,... | collective-permute-start | bytes 393224 | tf_op jit(solution)/shard_map/ppermute | solution.py:621
  14.6 5.1 %collective-permute-start.3 = (f32[128,256]{1,0:T(8,128)S(1)}, f32[128,256]{1,0:T(8,128)S(1)}, u32[]{:S(2)}, u32[]{:S(2)}) collective-permute-start(f32[128,256]{1,0:T(8,128)S(1)} %get-tuple-element.74), channel_id=1, source_target_pairs={{0,6},{1,7},{2,4},{3,5},{4,2},{5,3},{6,0},{7,1},{8,14},{9,15},{10,... | collective-permute-start | bytes 393224 | tf_op jit(solution)/shard_map/ppermute | solution.py:621
  16.2 3.8 %collective-permute-start.4 = (f32[128,256]{1,0:T(8,128)S(1)}, f32[128,256]{1,0:T(8,128)S(1)}, u32[]{:S(2)}, u32[]{:S(2)}) collective-permute-start(f32[128,256]{1,0:T(8,128)S(1)} %get-tuple-element.75), channel_id=1, source_target_pairs={{0,2},{1,3},{2,0},{3,1},{4,6},{5,7},{6,4},{7,5},{8,10},{9,11},{10,... | collective-permute-start | bytes 393224 | tf_op jit(solution)/shard_map/ppermute | solution.py:621
  20.1 3.9 %collective-permute-start.5 = (f32[2,128,256]{2,1,0:T(8,128)S(1)}, f32[2,128,256]{2,1,0:T(8,128)S(1)}, u32[]{:S(2)}, u32[]{:S(2)}) collective-permute-start(f32[2,128,256]{2,1,0:T(8,128)S(1)} %pad_maximum_fusion.1.mine_ref), channel_id=1, source_target_pairs={{0,1},{1,0},{2,3},{3,2},{4,5},{5,4},{6,7},{7,6},{8,9},{9,8},{10,11... | collective-permute-start | bytes 786440 | tf_op jit(solution)/shard_map/ppermute | solution.py:625
  68.6 29.8 %all-to-all-start.1 = ((f32[16,256,128]{2,1,0:T(8,128)}), f32[16,256,128]{2,1,0:T(8,128)S(1)}, u32[]{:S(2)}, u32[]{:S(2)}) async-start(f32[16,256,128]{2,1,0:T(8,128)} %get-tuple-element.45), calls=%async_computation.1 | async-start | bytes 4194304 | tf_op jit(solution)/shard_map/all_to_all | solution.py:663
  72.9 2.8 %collective-permute-start.6 = (f32[48,128]{1,0:T(8,128)S(1)}, f32[48,128]{1,0:T(8,128)S(1)}, u32[]{:S(2)}, u32[]{:S(2)}) collective-permute-start(f32[48,128]{1,0:T(8,128)S(1)} %get-tuple-element.42), channel_id=1, source_target_pairs={{0,1},{1,0},{2,3},{3,2},{4,5},{5,4},{6,7},{7,6},{8,9},{9,8},{10,11... | collective-permute-start | bytes 73736 | tf_op jit(solution)/shard_map/ppermute | solution.py:625
  75.6 4.5 %collective-permute-start.9 = (f32[96,128]{1,0:T(8,128)S(1)}, f32[96,128]{1,0:T(8,128)S(1)}, u32[]{:S(2)}, u32[]{:S(2)}) collective-permute-start(f32[96,128]{1,0:T(8,128)S(1)} %maximum_select_fusion.refs_0_), channel_id=1, source_target_pairs={{0,2},{1,3},{2,4},{3,5},{4,6},{5,7},{6,0},{7,1},{8,10},{9,11},{10,... | collective-permute-start | bytes 147464 | tf_op jit(solution)/shard_map/ppermute | solution.py:621
  75.6 5.2 %collective-permute-start.8 = (f32[96,128]{1,0:T(8,128)S(1)}, f32[96,128]{1,0:T(8,128)S(1)}, u32[]{:S(2)}, u32[]{:S(2)}) collective-permute-start(f32[96,128]{1,0:T(8,128)S(1)} %maximum_select_fusion.refs_0_), channel_id=1, source_target_pairs={{0,4},{1,5},{2,6},{3,7},{4,0},{5,1},{6,2},{7,3},{8,12},{9,13},{10,... | collective-permute-start | bytes 147464 | tf_op jit(solution)/shard_map/ppermute | solution.py:621
  78.3 3.5 %collective-permute-start.7 = (f32[96,128]{1,0:T(8,128)S(1)}, f32[96,128]{1,0:T(8,128)S(1)}, u32[]{:S(2)}, u32[]{:S(2)}) collective-permute-start(f32[96,128]{1,0:T(8,128)S(1)} %maximum_select_fusion.refs_0_), channel_id=1, source_target_pairs={{0,6},{1,7},{2,0},{3,1},{4,2},{5,3},{6,4},{7,5},{8,14},{9,15},{10,... | collective-permute-start | bytes 147464 | tf_op jit(solution)/shard_map/ppermute | solution.py:621
  104.9 6.4 %collective-permute-start.10 = (f32[2,136,256]{2,1,0:T(8,128)S(1)}, f32[2,136,256]{2,1,0:T(8,128)S(1)}, u32[]{:S(2)}, u32[]{:S(2)}) collective-permute-start(f32[2,136,256]{2,1,0:T(8,128)S(1)} %constant_dynamic-slice_fusion), channel_id=1, source_target_pairs={{0,1},{1,0},{2,3},{3,2},{4,5},{5,4},{6,7},{7,6},{8,9},{9,8},{10,11... | collective-permute-start | bytes 835592 | tf_op jit(solution)/shard_map/ppermute | solution.py:625
  111.3 6.2 %collective-permute-start.12 = (f32[136,256]{1,0:T(8,128)S(1)}, f32[136,256]{1,0:T(8,128)S(1)}, u32[]{:S(2)}, u32[]{:S(2)}) collective-permute-start(f32[136,256]{1,0:T(8,128)S(1)} %get-tuple-element.72), channel_id=1, source_target_pairs={{0,6},{1,7},{2,4},{3,5},{4,2},{5,3},{6,0},{7,1},{8,14},{9,15},{10,... | collective-permute-start | bytes 417800 | tf_op jit(solution)/shard_map/ppermute | solution.py:621
  112.8 4.6 %collective-permute-start.11 = (f32[136,256]{1,0:T(8,128)S(1)}, f32[136,256]{1,0:T(8,128)S(1)}, u32[]{:S(2)}, u32[]{:S(2)}) collective-permute-start(f32[136,256]{1,0:T(8,128)S(1)} %get-tuple-element.73), channel_id=1, source_target_pairs={{0,2},{1,3},{2,0},{3,1},{4,6},{5,7},{6,4},{7,5},{8,10},{9,11},{10,... | collective-permute-start | bytes 417800 | tf_op jit(solution)/shard_map/ppermute | solution.py:621
  117.5 6.3 %collective-permute-start.13 = (f32[136,256]{1,0:T(8,128)S(1)}, f32[136,256]{1,0:T(8,128)S(1)}, u32[]{:S(2)}, u32[]{:S(2)}) collective-permute-start(f32[136,256]{1,0:T(8,128)S(1)} %get-tuple-element.70), channel_id=1, source_target_pairs={{0,6},{1,7},{2,4},{3,5},{4,2},{5,3},{6,0},{7,1},{8,14},{9,15},{10,... | collective-permute-start | bytes 417800 | tf_op jit(solution)/shard_map/ppermute | solution.py:621
  119.1 4.8 %collective-permute-start.14 = (f32[136,256]{1,0:T(8,128)S(1)}, f32[136,256]{1,0:T(8,128)S(1)}, u32[]{:S(2)}, u32[]{:S(2)}) collective-permute-start(f32[136,256]{1,0:T(8,128)S(1)} %get-tuple-element.71), channel_id=1, source_target_pairs={{0,2},{1,3},{2,0},{3,1},{4,6},{5,7},{6,4},{7,5},{8,10},{9,11},{10,... | collective-permute-start | bytes 417800 | tf_op jit(solution)/shard_map/ppermute | solution.py:621
  123.9 3.0 %collective-permute-start.15 = (f32[2,136,256]{2,1,0:T(8,128)S(1)}, f32[2,136,256]{2,1,0:T(8,128)S(1)}, u32[]{:S(2)}, u32[]{:S(2)}) collective-permute-start(f32[2,136,256]{2,1,0:T(8,128)S(1)} %pad_maximum_fusion.mine_ref), channel_id=1, source_target_pairs={{0,1},{1,0},{2,3},{3,2},{4,5},{5,4},{6,7},{7,6},{8,9},{9,8},{10,11... | collective-permute-start | bytes 835592 | tf_op jit(solution)/shard_map/ppermute | solution.py:625
  167.0 30.3 %all-to-all-start.3 = ((f32[16,256,128]{2,1,0:T(8,128)}), f32[16,256,128]{2,1,0:T(8,128)}, u32[]{:S(2)}, u32[]{:S(2)}) async-start(f32[16,256,128]{2,1,0:T(8,128)} %get-tuple-element.66), calls=%async_computation.3 | async-start | bytes 4194304 | tf_op jit(solution)/shard_map/all_to_all | solution.py:663
  171.7 3.2 %collective-permute-start.16 = (f32[48,128]{1,0:T(8,128)S(1)}, f32[48,128]{1,0:T(8,128)S(1)}, u32[]{:S(2)}, u32[]{:S(2)}) collective-permute-start(f32[48,128]{1,0:T(8,128)S(1)} %get-tuple-element.63), channel_id=1, source_target_pairs={{0,1},{1,0},{2,3},{3,2},{4,5},{5,4},{6,7},{7,6},{8,9},{9,8},{10,11... | collective-permute-start | bytes 73736 | tf_op jit(solution)/shard_map/ppermute | solution.py:625
  175.0 4.6 %collective-permute-start.19 = (f32[96,128]{1,0:T(8,128)S(1)}, f32[96,128]{1,0:T(8,128)S(1)}, u32[]{:S(2)}, u32[]{:S(2)}) collective-permute-start(f32[96,128]{1,0:T(8,128)S(1)} %maximum_select_fusion.1.refs_0_), channel_id=1, source_target_pairs={{0,2},{1,3},{2,4},{3,5},{4,6},{5,7},{6,0},{7,1},{8,10},{9,11},{10,... | collective-permute-start | bytes 147464 | tf_op jit(solution)/shard_map/ppermute | solution.py:621
  176.1 4.8 %collective-permute-start.18 = (f32[96,128]{1,0:T(8,128)S(1)}, f32[96,128]{1,0:T(8,128)S(1)}, u32[]{:S(2)}, u32[]{:S(2)}) collective-permute-start(f32[96,128]{1,0:T(8,128)S(1)} %maximum_select_fusion.1.refs_0_), channel_id=1, source_target_pairs={{0,4},{1,5},{2,6},{3,7},{4,0},{5,1},{6,2},{7,3},{8,12},{9,13},{10,... | collective-permute-start | bytes 147464 | tf_op jit(solution)/shard_map/ppermute | solution.py:621
  177.6 3.6 %collective-permute-start.17 = (f32[96,128]{1,0:T(8,128)S(1)}, f32[96,128]{1,0:T(8,128)S(1)}, u32[]{:S(2)}, u32[]{:S(2)}) collective-permute-start(f32[96,128]{1,0:T(8,128)S(1)} %maximum_select_fusion.1.refs_0_), channel_id=1, source_target_pairs={{0,6},{1,7},{2,0},{3,1},{4,2},{5,3},{6,4},{7,5},{8,14},{9,15},{10,... | collective-permute-start | bytes 147464 | tf_op jit(solution)/shard_map/ppermute | solution.py:621

commit v2 on v1

--- a/solution.py
+++ b/solution.py
@@ -310,6 +310,16 @@
     )(x)
 
 
+def two_columns(a, b, d, row0, row1, first, second):
+    inv = 1.0 / (a * d - b * b)
+    i00, i01, i11 = d * inv, -b * inv, a * inv
+    e0 = jnp.where(first, 1.0, jnp.where(second, 0.0, row0))
+    e1 = jnp.where(first, 0.0, jnp.where(second, 1.0, row1))
+    ratio = b / a
+    kept = jnp.where(first, -ratio, row1 - ratio * row0)
+    return (i00, i01, i11), i00 * e0 + i01 * e1, i01 * e0 + i11 * e1, kept
+
+
 def eliminated(m):
     n = m.shape[0]
     eye = same(n)
@@ -319,26 +329,48 @@
     lane = lax.broadcasted_iota(jnp.int32, (8, n), 1)
     sub = lax.broadcasted_iota(jnp.int32, (8, n), 0)
     tiles = [m[8 * t : 8 * t + 8] for t in range(n // 8)]
-    for j in range(0, n, 2):
+    for j in range(0, n, 4):
         t, r = divmod(j, 8)
-        first, second = lane[:1] == j, lane[:1] == j + 1
-        both = (lane >= j) & (lane < j + 2)
-        c0 = [jnp.broadcast_to(x[:, j : j + 1], (8, n)) for x in tiles[t:]]
-        c1 = [jnp.broadcast_to(x[:, j + 1 : j + 2], (8, n)) for x in tiles[t:]]
-        row0, row1 = tiles[t][r : r + 1], tiles[t][r + 1 : r + 2]
-        a, b = c0[0][r : r + 1], c0[0][r + 1 : r + 2]
-        d = c1[0][r + 1 : r + 2]
-        inv_a = 1.0 / a
-        inv_d = a * (1.0 / (a * d - b * b))
-        ratio = b * inv_a
-        low = row1 - ratio * row0
-        use1 = jnp.where(first, -ratio, jnp.where(second, 1.0, low)) * inv_d
-        use0 = jnp.where(first, 1.0, jnp.where(second, 0.0, row0)) * inv_a - ratio * use1
-        kept = jnp.where(first, -ratio, low)
+        here = [lane[:1] == j + k for k in range(4)]
+        left, right = here[0] | here[1], here[2] | here[3]
+        all_four = (lane >= j) & (lane < j + 4)
+        c = [
+            [jnp.broadcast_to(x[:, j + k : j + k + 1], (8, n)) for x in tiles[t:]]
+            for k in range(4)
+        ]
+        rows = [tiles[t][r + k : r + k + 1] for k in range(4)]
+
+        def at(k, l):
+            return c[l][0][r + k : r + k + 1]
+
+        (i00, i01, i11), use0, use1, kept1 = two_columns(
+            at(0, 0), at(1, 0), at(1, 1), rows[0], rows[1], here[0], here[1]
+        )
+        f2, g2 = i00 * at(2, 0) + i01 * at(2, 1), i01 * at(2, 0) + i11 * at(2, 1)
+        f3, g3 = i00 * at(3, 0) + i01 * at(3, 1), i01 * at(3, 0) + i11 * at(3, 1)
+        row2 = jnp.where(left, 0.0, rows[2]) - at(2, 0) * use0 - at(2, 1) * use1
+        row3 = jnp.where(left, 0.0, rows[3]) - at(3, 0) * use0 - at(3, 1) * use1
+        _, use2, use3, kept3 = two_columns(
+            at(2, 2) - at(2, 0) * f2 - at(2, 1) * g2,
+            at(3, 2) - at(3, 0) * f2 - at(3, 1) * g2,
+            at(3, 3) - at(3, 0) * f3 - at(3, 1) * g3,
+            row2,
+            row3,
+            here[2],
+            here[3],
+        )
+        use0, use1 = jnp.where(right, 0.0, use0), jnp.where(right, 0.0, use1)
         for s in range(t, n // 8):
-            new = jnp.where(both, 0.0, tiles[s]) - c0[s - t] * use0 - c1[s - t] * use1
+            c0, c1, c2, c3 = (c[k][s - t] for k in range(4))
+            c2 = c2 - c0 * f2 - c1 * g2
+            c3 = c3 - c0 * f3 - c1 * g3
+            new = jnp.where(all_four, 0.0, tiles[s]) - c0 * use0 - c1 * use1
+            new = new - c2 * use2 - c3 * use3
             if s == t:
-                new = jnp.where(sub > r + 1, new, jnp.where(sub == r + 1, kept, tiles[s]))
+                own = jnp.where(sub == r + 1, kept1, tiles[s])
+                own = jnp.where(sub == r + 2, row2, own)
+                own = jnp.where(sub == r + 3, kept3, own)
+                new = jnp.where(sub > r + 3, new, own)
             tiles[s] = new
     m = jnp.concatenate(tiles, axis=0)
     i = lax.broadcasted_iota(jnp.int32, (n, n), 0)
@@ -389,8 +421,44 @@
     )(place, p, *pieces)
 
 
-def middle_kernel(o_ref, w_ref, x_ref, m_ref, g_ref, q_ref, rt_ref, m, g, q_sum, s_ref, sems):
-    wait = fetch(buffer_moves(m_ref, g_ref, m, g), sems)
+def ahead_kernel(after_ref, m_ref, g_ref, a_ref, m, g, a, came, sent):
+    del after_ref
+    width = m.shape[1] // CHUNKS
+    wait = fetch(buffer_moves(m_ref, g_ref, m, g), came)
+    start, finish = send(
+        lambda k: [(a.at[:, :, columns(k, width)], a_ref.at[:, :, columns(k, width)])], sent
+    )
+
+    def block(k):
+        c = columns(k, width)
+        wait(k)
+        a[0, :, c], a[1, :, c] = split(buffer_block(m, g, c))
+        start(k)
+
+    each(block)
+    finish()
+
+
+def buffer_ahead(after, momentum, grads):
+    rows, cols = momentum.shape
+    return call(
+        ahead_kernel,
+        [VM] + [ANY] * 2,
+        pair_in_hbm((rows, cols)),
+        ANY,
+        [
+            pltpu.VMEM((rows, cols), F32),
+            pltpu.VMEM(grads.shape, BF16),
+            pltpu.VMEM((2, rows, cols), BF16),
+            dma(CHUNKS, 3),
+            dma(CHUNKS, 1),
+        ],
+        8 * rows * cols,
+    )(after, *in_hbm(momentum, grads))
+
+
+def middle_kernel(o_ref, w_ref, x_ref, a_ref, q_ref, rt_ref, a, q_sum, s_ref, sems):
+    wait = fetch(pair_moves(a_ref, a), sems)
 
     def turn(k):
         c = columns(k, LANES)
@@ -400,14 +468,14 @@
     rt = (rt_ref[0], rt_ref[1])
     w = w_ref[...]
     s_ref[...] = exact(exact(w, dot3(rt, rt, NT), NN), w, NT)
-    width = m.shape[1] // CHUNKS
+    width = a.shape[2] // CHUNKS
     q_sum[...] = jnp.zeros_like(q_sum)
 
     def block(k):
         c = columns(k, width)
         wait(k)
         q_sum[...] += dot3(
-            split(buffer_block(m, g, c)), (rt_ref[0, :, c], rt_ref[1, :, c]), NT
+            (a[0, :, c], a[1, :, c]), (rt_ref[0, :, c], rt_ref[1, :, c]), NT
         )
 
     each(block)
@@ -423,30 +491,29 @@
         q_ref[k, height:] = jnp.broadcast_to(squares, (8, n))
 
 
-def middle(o, w, x, momentum, grads):
-    rows, cols = momentum.shape
+def middle(o, w, x, ahead):
+    _, rows, cols = ahead.shape
     rank = o.shape[1]
     return call(
         middle_kernel,
-        [VM] * 3 + [ANY] * 2,
+        [VM] * 3 + [ANY],
         [jax.ShapeDtypeStruct((4, rows // 4 + 8, rank), F32), pair((rank, cols))],
         [VM] * 2,
         [
-            pltpu.VMEM((rows, cols), F32),
-            pltpu.VMEM(grads.shape, BF16),
+            pltpu.VMEM((2, rows, cols), BF16),
             pltpu.VMEM((rows, rank), F32),
             pltpu.VMEM((rank, rank), F32),
-            dma(CHUNKS, 3),
+            dma(CHUNKS, 1),
         ],
         10 * rows * cols * rank,
-    )(o, w, x, *in_hbm(momentum, grads))
-
-
-def update_kernel(half, o_ref, w_ref, rt_ref, m_ref, g_ref, *refs):
-    raw_ref, b_ref, m, g, raw, b, came, sent = refs[-8:]
+    )(o, w, x, *in_hbm(ahead))
+
+
+def update_kernel(half, o_ref, w_ref, rt_ref, a_ref, *refs):
+    raw_ref, b_ref, a, raw, b, came, sent = refs[-7:]
     count = CHUNKS // 2
-    width = m.shape[1] // count
-    base = half * m.shape[1]
+    width = a.shape[2] // count
+    base = half * a.shape[2]
 
     def placed(k):
         if isinstance(k, int):
@@ -454,12 +521,7 @@
         return pl.ds(pl.multiple_of(base + k * width, width), width)
 
     def moves(k):
-        c, there = columns(k, width), placed(k)
-        return [
-            (m_ref.at[:, there], m.at[:, c]),
-            (g_ref.at[0, :, there], g.at[0, :, c]),
-            (g_ref.at[1, :, there], g.at[1, :, c]),
-        ]
+        return [(a_ref.at[:, :, placed(k)], a.at[:, :, columns(k, width)])]
 
     wait = fetch(moves, came, count)
     start, finish = send(
@@ -478,33 +540,34 @@
         now = split(dot3(w, (rt_ref[0, :, there], rt_ref[1, :, there]), NN))
         raw[0, :, c], raw[1, :, c] = now
         wait(k)
-        b[0, :, c], b[1, :, c] = split(buffer_block(m, g, c) - dot3(o, now, NN))
+        b[0, :, c], b[1, :, c] = split(
+            a[0, :, c].astype(F32) + a[1, :, c].astype(F32) - dot3(o, now, NN)
+        )
         start(k)
 
     each(block, count)
     finish()
 
 
-def second_buffer(half, o, w, rt, momentum, grads, begun):
-    rows, cols = momentum.shape
+def second_buffer(half, o, w, rt, ahead, begun):
+    _, rows, cols = ahead.shape
     rank = o.shape[1]
     part = cols // 2
     return call(
         functools.partial(update_kernel, half),
-        [VM] * 3 + [ANY] * (2 + len(begun)),
+        [VM] * 3 + [ANY] * (1 + len(begun)),
         [pair_in_hbm((rank, cols)), pair_in_hbm((rows, cols))],
         [ANY] * 2,
         [
-            pltpu.VMEM((rows, part), F32),
             pltpu.VMEM((2, rows, part), BF16),
             pltpu.VMEM((2, rank, part), BF16),
             pltpu.VMEM((2, rows, part), BF16),
-            dma(CHUNKS // 2, 3),
+            dma(CHUNKS // 2, 1),
             dma(CHUNKS // 2, 2),
         ],
         5 * rows * cols * rank,
-        {5: 0, 6: 1} if begun else None,
-    )(o, w, rt, *in_hbm(momentum, grads), *in_hbm(*begun))
+        {4: 0, 5: 1} if begun else None,
+    )(o, w, rt, *in_hbm(ahead), *in_hbm(*begun))
 
 
 def write_out(value, out_ref, buffer, sems):
@@ -522,29 +585,55 @@
     finish()
 
 
-def last_raw_kernel(
-    o_ref, w_ref, x_ref, b_ref, raw_ref, sq_ref, s_ref, x, b, buffer, total, came, sent
+def first_change_kernel(
+    factor, after_ref, o_ref, rs_ref, raw_ref, c_ref, raw, buffer, came, sent
 ):
+    del after_ref
+    wait = fetch(pair_moves(raw_ref, raw), came)
+    o = split(o_ref[...] * (factor * rs_ref[:1]))
+
+    def value(k, c):
+        wait(k)
+        return dot3(o, (raw[0, :, c], raw[1, :, c]), NN)
+
+    write_out(value, c_ref, buffer, sent)
+
+
+def first_change(factor, after, o, rs, raw):
+    rows, rank = o.shape
+    cols = raw.shape[2]
+    return call(
+        functools.partial(first_change_kernel, factor),
+        [VM, VM, VM, ANY],
+        pltpu.HBM((rows, cols), F32),
+        ANY,
+        [
+            pltpu.VMEM(raw.shape, BF16),
+            pltpu.VMEM((rows, cols), F32),
+            dma(CHUNKS, 1),
+            dma(CHUNKS, 1),
+        ],
+        6 * rows * cols * rank,
+    )(after, o, rs, *in_hbm(raw))
+
+
+def last_raw_kernel(w_ref, x_ref, raw_ref, sq_ref, x, total, came):
     blocks = x_ref.shape[0] // CHUNKS
-    bring = pair_moves(b_ref, b)
     wait = fetch(
-        lambda k: [(x_ref.at[columns(k, blocks)], x.at[columns(k, blocks)])] + bring(k),
-        came,
+        lambda k: [(x_ref.at[columns(k, blocks)], x.at[columns(k, blocks)])], came
     )
     total[...] = jnp.zeros_like(total)
-    o = split((1.0 - KEEP_RATE) * o_ref[...])
     w = split(w_ref[...])
 
-    def value(k, c):
+    def block(k):
+        c = columns(k, blocks * LANES)
         wait(k)
         part = jnp.concatenate([x[k * blocks + q] for q in range(blocks)], axis=1)
         raw = dot3(w, split(part), NN)
-        now = split(raw)
-        raw_ref[0, :, c], raw_ref[1, :, c] = now
+        raw_ref[0, :, c], raw_ref[1, :, c] = split(raw)
         total[...] += jnp.sum(raw * raw, axis=1, keepdims=True)
-        return b[0, :, c].astype(F32) + b[1, :, c].astype(F32) - dot3(o, now, NN)
-
-    write_out(value, s_ref, buffer, sent)
+
+    each(block)
     n = w_ref.shape[0]
     squares = jnp.where(same(n), jnp.broadcast_to(total[:, :1], (n, n)), 0.0)
     row = jnp.sum(squares, axis=0, keepdims=True)
@@ -552,65 +641,86 @@
         sq_ref[k] = jnp.broadcast_to(row, (8, n))
 
 
-def last_raw(o, w, x, b, peers):
+def last_raw(w, x, peers):
+    rank = w.shape[0]
+    cols = x.shape[0] * LANES
+    return call(
+        last_raw_kernel,
+        [VM, ANY],
+        [pair((rank, cols)), jax.ShapeDtypeStruct((peers, 8, rank), F32)],
+        [VM] * 2,
+        [
+            pltpu.VMEM(x.shape, F32),
+            pltpu.VMEM((rank, LANES), F32),
+            dma(CHUNKS, 1),
+        ],
+        6 * rank * cols * rank,
+    )(w, *in_hbm(x))
+
+
+def state_kernel(o_ref, raw_ref, b_ref, s_ref, b, buffer, came, sent):
+    wait = fetch(pair_moves(b_ref, b), came)
+    o = split((1.0 - KEEP_RATE) * o_ref[...])
+
+    def value(k, c):
+        wait(k)
+        b_now = b[0, :, c].astype(F32) + b[1, :, c].astype(F32)
+        return b_now - dot3(o, (raw_ref[0, :, c], raw_ref[1, :, c]), NN)
+
+    write_out(value, s_ref, buffer, sent)
+
+
+def last_state(o, raw, b):
     _, rows, cols = b.shape
-    rank = w.shape[0]
-    return call(
-        last_raw_kernel,
-        [VM, VM, ANY, ANY],
-        [
-            pair((rank, cols)),
-            jax.ShapeDtypeStruct((peers, 8, rank), F32),
-            pltpu.HBM((rows, cols), F32),
-        ],
+    return call(
+        state_kernel,
         [VM, VM, ANY],
-        [
-            pltpu.VMEM(x.shape, F32),
+        pltpu.HBM((rows, cols), F32),
+        ANY,
+        [
             pltpu.VMEM(b.shape, BF16),
             pltpu.VMEM((rows, cols), F32),
-            pltpu.VMEM((rank, LANES), F32),
-            dma(CHUNKS, 2),
             dma(CHUNKS, 1),
-        ],
-        9 * rows * cols * rank,
-    )(o, w, *in_hbm(x), *in_hbm(b))
-
-
-def change_kernel(
-    factor, o1_ref, rs_ref, raw1_ref, o_ref, sq_ref, raw_ref, out_ref, raw1, buffer, came, sent
+            dma(CHUNKS, 1),
+        ],
+        6 * rows * cols * o.shape[1],
+    )(o, raw, *in_hbm(b))
+
+
+def last_change_kernel(
+    factor, o_ref, sq_ref, raw_ref, c_ref, out_ref, held, buffer, came, sent
 ):
-    wait = fetch(pair_moves(raw1_ref, raw1), came)
+    width = held.shape[1] // CHUNKS
+    wait = fetch(
+        lambda k: [(c_ref.at[:, columns(k, width)], held.at[:, columns(k, width)])], came
+    )
     total = sq_ref[0, :1]
     for k in range(1, sq_ref.shape[0]):
         total = total + sq_ref[k, :1]
     o = split(o_ref[...] * (factor * lax.rsqrt(total + NORM_EPS)))
-    o1 = split(o1_ref[...] * (factor * rs_ref[:1]))
 
     def value(k, c):
         wait(k)
-        return dot3(o1, (raw1[0, :, c], raw1[1, :, c]), NN) + dot3(
-            o, (raw_ref[0, :, c], raw_ref[1, :, c]), NN
-        )
+        return held[:, c] + dot3(o, (raw_ref[0, :, c], raw_ref[1, :, c]), NN)
 
     write_out(value, out_ref, buffer, sent)
 
 
-def both_changes(factor, o1, rs, raw1, o, sq, raw):
-    rows, rank = o.shape
-    cols = raw.shape[2]
-    return call(
-        functools.partial(change_kernel, factor),
-        [VM, VM, ANY, VM, VM, VM],
+def last_change(factor, o, sq, raw, change):
+    rows, cols = change.shape
+    return call(
+        functools.partial(last_change_kernel, factor),
+        [VM, VM, VM, ANY],
         pltpu.HBM((rows, cols), BF16),
         ANY,
         [
-            pltpu.VMEM(raw1.shape, BF16),
+            pltpu.VMEM((rows, cols), F32),
             pltpu.VMEM((rows, cols), BF16),
             dma(CHUNKS, 1),
             dma(CHUNKS, 1),
         ],
-        12 * rows * cols * rank,
-    )(o1, rs, *in_hbm(raw1), o, sq, raw)
+        6 * rows * cols * o.shape[1],
+    )(o, sq, raw, *in_hbm(change))
 
 
 SIDE = 4
@@ -663,10 +773,10 @@
     return lax.all_to_all(x, axis, 0, 0, tiled=True)
 
 
-def row_total(blocks, p, place):
+def row_total(blocks, p, place, beside):
     own, part = spread_sum(exchange(blocks, "row"), p.shape[1])
-    total = exchange(own, "row")
-    return total, *inverse_factor(by_chip(part), place, p)
+    total, extra = lax.optimization_barrier((exchange(own, "row"), beside(part)))
+    return total, *inverse_factor(by_chip(part), place, p), extra
 
 
 def shards(momentum, grads, basis):
@@ -682,20 +792,25 @@
     x1, p1, _ = products(
         first_products_kernel, place, mine, theirs, [momentum, grads], held, peers
     )
-    x1, w1, o1 = row_total(x1, p1, place)
-    part, rt1 = middle(o1, w1, x1, momentum, grads)
+    x1, w1, o1, ahead = row_total(
+        x1, p1, place, lambda part: buffer_ahead(part, momentum, grads)
+    )
+    part, rt1 = middle(o1, w1, x1, ahead)
     mine, theirs, (raw1, buffer) = col_sum(
-        part,
-        lambda half, done: second_buffer(half, o1, w1, rt1, momentum, grads, done),
+        part, lambda half, done: second_buffer(half, o1, w1, rt1, ahead, done)
     )
     held = [pltpu.VMEM((2, rows, cols), BF16)]
     x2, p2, rs1 = products(
         second_products_kernel, place, mine, theirs, [buffer], held, peers
     )
-    x2, w2, o2 = row_total(x2, p2, place)
-    raw2, sq2, state = last_raw(o2, w2, x2, buffer, peers)
-    sq2 = exchange(sq2, "col")
-    change = both_changes(factor, o1, rs1, raw1, o2, sq2, raw2)
+    x2, w2, o2, change1 = row_total(
+        x2, p2, place, lambda part: first_change(factor, part, o1, rs1, raw1)
+    )
+    raw2, sq2 = last_raw(w2, x2, peers)
+    sq2, state = lax.optimization_barrier(
+        (exchange(sq2, "col"), last_state(o2, raw2, buffer))
+    )
+    change = last_change(factor, o2, sq2, raw2, change1)
     return change, state
 
 

time: 224 us -> 220 us (0.982)
  blocking collectives: 86.2 us -> 72.7 us
  starting transfers between devices: 39.5 us -> 45.9 us
  waiting for transfers between devices: 22.5 us -> 24.8 us
    all_to_all x3 -> x2, blocking collectives: 86.2 us -> 72.7 us  [exchange(): return lax.all_to_all(x, axis, 0, 0, tiled=True)]
    pallas_call x5 -> x8, Pallas kernels: 27.3 us -> 36.9 us  [the longest x2 8.05 us: second_buffer(): call(functools.partial(update_kernel, half), [VM] * 3 + [ANY] * (1 + len(...]
    pallas_call x2, Pallas kernels: 30.3 us -> 21.3 us  [inverse_factor(): call(cholesky_kernel, [SM, VM] + [VM] * len(pieces), [jax.ShapeDtypeStruc...]
    all_to_all x2 -> x3, starting transfers between devices: 8.91 us -> 17.8 us  [exchange(): return lax.all_to_all(x, axis, 0, 0, tiled=True)]
    all_to_all x2 -> x3, waiting for transfers between devices: 2.49 us -> 9.35 us  [exchange(): return lax.all_to_all(x, axis, 0, 0, tiled=True)]
    ppermute x14, waiting for transfers between devices: 13.6 us -> 9.11 us  [chip_permute(): return lax.ppermute(x, 'col', pairs)]
    ppermute x14, starting transfers between devices: 15.1 us -> 11.9 us  [chip_permute(): return lax.ppermute(x, 'col', pairs)]
  transfers between devices with their start and end apart: 22 -> 23, of which waited for: 19 -> 15; matrix products, arithmetic and copies ran while one was open for 0% -> 0% of each run, Pallas kernels for 17% -> 20%
where the time goes in v2:
time: 220 us; the launch traced here: 219 us
  Pallas kernels  74.3 us (34%)
  blocking collectives  72.7 us (33%)
  starting transfers between devices  45.9 us (21%)
  waiting for transfers between devices  24.8 us (11%)
    all_to_all x2, blocking collectives, exchange(): return lax.all_to_all(x, axis, 0, 0, tiled=True)  72.7 us
    pallas_call x2, Pallas kernels, inverse_factor(): call(cholesky_kernel, [SM, VM] + [VM] * len(pieces), [jax.ShapeDtypeStruc...  21.3 us
    all_to_all x3, starting transfers between devices, exchange(): return lax.all_to_all(x, axis, 0, 0, tiled=True)  17.8 us
    ppermute x6, starting transfers between devices, core_permute(): return lax.ppermute(x, 'col', [(k, k ^ 1) for k in range(2 * SIDE)])  16.1 us
    ppermute x14, starting transfers between devices, chip_permute(): return lax.ppermute(x, 'col', pairs)  11.9 us
    all_to_all x3, waiting for transfers between devices, exchange(): return lax.all_to_all(x, axis, 0, 0, tiled=True)  9.35 us
    ppermute x14, waiting for transfers between devices, chip_permute(): return lax.ppermute(x, 'col', pairs)  9.11 us
    pallas_call x2, Pallas kernels, products(): call(kernel, [SM, VM, VM] + [ANY] * len(bigs), [jax.ShapeDtypeStruct(shap...  8.87 us
  transfers between devices with their start and end apart: 23, of which 15 were waited for; matrix products, arithmetic and copies ran while one was open for 0% of the time, Pallas kernels for 20%

profile of v2, /device:TPU:1, one launch (start us, length us, event | category | flops | bytes accessed | tf_op | source)
XLA Modules:
  0.0 219.2 jit_solution(9297933584712437783)
XLA Ops:
  0.6 4.1 %shard_map.50 = f32[512,256]{1,0:T(8,128)S(1)} custom-call(f32[512,2048]{1,0:T(8,128)} %m_ref.5, bf16[2,512,2048]{2,1,0:T(8,128)(2,1)} %g_ref.5, f32[2048,256]{1,0:T(8,128)} %v_ref.1), custom_call_target="tpu_custom_call" | custom-call | flops 1610612736 | bytes 8388608 | tf_op jit(solution)/shard_map/pallas_call | solution.py:165
  4.8 1.5 collective-permute-start
  6.3 1.2 collective-permute-done
  7.6 1.4 collective-permute-start.1
  8.9 1.8 collective-permute-start.2
  10.8 1.6 collective-permute-done.1
  12.3 2.2 collective-permute-done.2
  14.6 1.9 collective-permute-start.3
  16.5 3.2 %collective-permute-done.3 = f32[128,256]{1,0:T(8,128)S(1)} collective-permute-done((f32[128,256]{1,0:T(8,128)S(1)}, f32[128,256]{1,0:T(8,128)S(1)}, u32[]{:S(2)}, u32[]{:S(2)}) %collective-permute-start.3) | collective-permute-done | bytes 131104 | tf_op jit(solution)/shard_map/ppermute | solution.py:731
  19.7 0.9 collective-permute-done.4
  20.6 2.7 %collective-permute-start.5 = (f32[2,128,256]{2,1,0:T(8,128)S(1)}, f32[2,128,256]{2,1,0:T(8,128)S(1)}, u32[]{:S(2)}, u32[]{:S(2)}) collective-permute-start(f32[2,128,256]{2,1,0:T(8,128)S(1)} %pad_maximum_fusion.1.mine_ref), channel_id=1, source_target_pairs={{0,1},{1,0},{2,3},{3,2},{4,5},{5,4},{6,7},{7,6},{8,9},{9,8},{10,11... | collective-permute-start | bytes 786440 | tf_op jit(solution)/shard_map/ppermute | solution.py:735
  23.4 1.2 collective-permute-done.5.theirs_ref
  24.5 4.6 %shard_map.51 = (f32[16,304,128]{2,1,0:T(8,128)S(1)}, f32[512,256]{1,0:T(8,128)S(1)}, f32[8,256]{1,0:T(8,128)}) custom-call(s32[1]{0:T(128)} %bitcast.n_ref, f32[2,128,256]{2,1,0:T(8,128)S(1)} %pad_maximum_fusion.1.mine_ref, f32[2,128,256]{2,1,0:T(8,128)S(1)} %collective-permute-done.5.theirs_ref, f32[512,2048]{1,0:T(8,128)} %m_ref.5, ...), custom_call_target="tpu_custom_call" | custom-call | flops 1610612736 | bytes 8388608 | tf_op jit(solution)/shard_map/pallas_call | solution.py:260
  29.1 38.5 %all_to_all.25.x_ref = f32[16,304,128]{2,1,0:T(8,128)S(1)} all-to-all(f32[16,304,128]{2,1,0:T(8,128)S(1)} %get-tuple-element.46), channel_id=1, replica_groups=mesh['row'=16,'col'=8] {'row'}, dimensions={0} | all-to-all | bytes 4980736 | tf_op jit(solution)/shard_map/all_to_all | solution.py:773
  67.6 1.5 shard_map.52
  69.2 4.2 %all-to-all-start.1 = ((f32[16,256,128]{2,1,0:T(8,128)}), f32[16,256,128]{2,1,0:T(8,128)S(1)}, u32[]{:S(2)}, u32[]{:S(2)}) async-start(f32[16,256,128]{2,1,0:T(8,128)} %get-tuple-element.50), calls=%async_computation.1 | async-start | bytes 4194304 | tf_op jit(solution)/shard_map/all_to_all | solution.py:773
  73.4 1.9 collective-permute-start.6
  75.3 0.8 collective-permute-done.6
  76.2 0.9 collective-permute-start.7
  77.1 0.6 collective-permute-start.8
  77.8 5.5 %shard_map.54.a_ref = bf16[2,512,2048]{2,1,0:T(8,128)(2,1)} custom-call(f32[48,128]{1,0:T(8,128)S(1)} %get-tuple-element.47.after_ref, f32[512,2048]{1,0:T(8,128)} %m_ref.5, bf16[2,512,2048]{2,1,0:T(8,128)(2,1)} %g_ref.5), custom_call_target="tpu_custom_call" | custom-call | flops 8388608 | bytes 8388608 | tf_op jit(solution)/shard_map/pallas_call | solution.py:444
  83.4 10.7 %shard_map.53 = (f32[256,256]{1,0:T(8,128)S(1)}, f32[512,256]{1,0:T(8,128)S(1)}) custom-call(s32[1]{0:T(128)} %bitcast.n_ref, f32[512,256]{1,0:T(8,128)S(1)} %get-tuple-element.45.p_ref, f32[96,128]{1,0:T(8,128)S(1)} %maximum_select_fusion.refs_0_, f32[96,128]{1,0:T(8,128)S(1)} %collective-permute-done.7.refs_1_, ...), custom_call_target="tpu_custom_call" | custom-call | flops 10000000000 | bytes 8388608 | tf_op jit(solution)/shard_map/pallas_call | solution.py:414
  94.1 5.0 %all-to-all-done.1.x_ref = f32[16,256,128]{2,1,0:T(8,128)S(1)} async-done(((f32[16,256,128]{2,1,0:T(8,128)}), f32[16,256,128]{2,1,0:T(8,128)S(1)}, u32[]{:S(2)}, u32[]{:S(2)}) %all-to-all-start.1) | async-done | bytes 2097184 | tf_op jit(solution)/shard_map/all_to_all | solution.py:773
  99.0 6.1 %shard_map.55 = (f32[4,136,256]{2,1,0:T(8,128)S(1)}, bf16[2,256,2048]{2,1,0:T(8,128)(2,1)S(1)}) custom-call(f32[512,256]{1,0:T(8,128)S(1)} %get-tuple-element.48.o_ref, f32[256,256]{1,0:T(8,128)S(1)} %get-tuple-element.49.w_ref, f32[16,256,128]{2,1,0:T(8,128)S(1)} %all-to-all-done.1.x_ref, bf16[2,512,2048]{2,1,0:T(8,128)(2,1)} %shard_map.54.a_ref), custom_call_target="tpu_custom_call" | custom-call | flops 2684354560 | bytes 8388608 | tf_op jit(solution)/shard_map/pallas_call | solution.py:497
  105.1 5.1 %collective-permute-start.10 = (f32[2,136,256]{2,1,0:T(8,128)S(1)}, f32[2,136,256]{2,1,0:T(8,128)S(1)}, u32[]{:S(2)}, u32[]{:S(2)}) collective-permute-start(f32[2,136,256]{2,1,0:T(8,128)S(1)} %constant_dynamic-slice_fusion), channel_id=1, source_target_pairs={{0,1},{1,0},{2,3},{3,2},{4,5},{5,4},{6,7},{7,6},{8,9},{9,8},{10,11... | collective-permute-start | bytes 835592 | tf_op jit(solution)/shard_map/ppermute | solution.py:735
  110.3 1.2 collective-permute-done.10
  111.6 1.0 collective-permute-start.12
  112.7 4.0 %shard_map.56 = (bf16[2,256,2048]{2,1,0:T(8,128)(2,1)}, bf16[2,512,2048]{2,1,0:T(8,128)(2,1)}) custom-call(f32[512,256]{1,0:T(8,128)S(1)} %get-tuple-element.48.o_ref, f32[256,256]{1,0:T(8,128)S(1)} %get-tuple-element.49.w_ref, bf16[2,256,2048]{2,1,0:T(8,128)(2,1)S(1)} %get-tuple-element.54.rt_ref, bf16[2,512,2048]{2,1,0:T(8,128)(2,1)} %shard_map.54.a_ref), custom_call_target="tpu_custom_call" | custom-call | flops 1342177280 | bytes 8388608 | tf_op jit(solution)/shard_map/pallas_call | solution.py:556
  116.7 1.1 collective-permute-done.12
  117.9 1.0 collective-permute-start.13
  118.9 4.0 %shard_map.57 = (bf16[2,256,2048]{2,1,0:T(8,128)(2,1)}, bf16[2,512,2048]{2,1,0:T(8,128)(2,1)}) custom-call(f32[512,256]{1,0:T(8,128)S(1)} %get-tuple-element.48.o_ref, f32[256,256]{1,0:T(8,128)S(1)} %get-tuple-element.49.w_ref, bf16[2,256,2048]{2,1,0:T(8,128)(2,1)S(1)} %get-tuple-element.54.rt_ref, ...), custom_call_target="tpu_custom_call", output_to_operand_aliasing={{0}: (4, {}), {1}: (5, {})} | custom-call | flops 1342177280 | bytes 8388608 | tf_op jit(solution)/shard_map/pallas_call | solution.py:556
  123.1 2.5 %collective-permute-start.15 = (f32[2,136,256]{2,1,0:T(8,128)S(1)}, f32[2,136,256]{2,1,0:T(8,128)S(1)}, u32[]{:S(2)}, u32[]{:S(2)}) collective-permute-start(f32[2,136,256]{2,1,0:T(8,128)S(1)} %pad_maximum_fusion.mine_ref), channel_id=1, source_target_pairs={{0,1},{1,0},{2,3},{3,2},{4,5},{5,4},{6,7},{7,6},{8,9},{9,8},{10,11... | collective-permute-start | bytes 835592 | tf_op jit(solution)/shard_map/ppermute | solution.py:735
  125.6 1.2 collective-permute-done.15.theirs_ref
  126.8 4.3 %shard_map.58 = (f32[16,304,128]{2,1,0:T(8,128)S(1)}, f32[512,256]{1,0:T(8,128)S(1)}, f32[8,256]{1,0:T(8,128)S(1)}) custom-call(s32[1]{0:T(128)} %bitcast.n_ref, f32[2,136,256]{2,1,0:T(8,128)S(1)} %pad_maximum_fusion.mine_ref, f32[2,136,256]{2,1,0:T(8,128)S(1)} %collective-permute-done.15.theirs_ref, bf16[2,512,2048]{2,1,0:T(8,128)(2,1)} %get-tuple-element.65.b_ref), custom_call_target="tpu_custom_call" | custom-call | flops 1610612736 | bytes 8388608 | tf_op jit(solution)/shard_map/pallas_call | solution.py:260
  131.1 34.2 %all_to_all.26.x_ref = f32[16,304,128]{2,1,0:T(8,128)S(1)} all-to-all(f32[16,304,128]{2,1,0:T(8,128)S(1)} %get-tuple-element.67), channel_id=1, replica_groups=mesh['row'=16,'col'=8] {'row'}, dimensions={0} | all-to-all | bytes 4980736 | tf_op jit(solution)/shard_map/all_to_all | solution.py:773
  165.3 1.5 shard_map.59
  166.8 4.7 %all-to-all-start.3 = ((f32[16,256,128]{2,1,0:T(8,128)}), f32[16,256,128]{2,1,0:T(8,128)}, u32[]{:S(2)}, u32[]{:S(2)}) async-start(f32[16,256,128]{2,1,0:T(8,128)} %get-tuple-element.71), calls=%async_computation.3 | async-start | bytes 4194304 | tf_op jit(solution)/shard_map/all_to_all | solution.py:773
  171.5 2.4 %collective-permute-start.16 = (f32[48,128]{1,0:T(8,128)S(1)}, f32[48,128]{1,0:T(8,128)S(1)}, u32[]{:S(2)}, u32[]{:S(2)}) collective-permute-start(f32[48,128]{1,0:T(8,128)S(1)} %get-tuple-element.68.after_ref), channel_id=1, source_target_pairs={{0,1},{1,0},{2,3},{3,2},{4,5},{5,4},{6,7},{7,6},{8,9},{9,8},{10,11... | collective-permute-start | bytes 73736 | tf_op jit(solution)/shard_map/ppermute | solution.py:735
  173.9 0.8 collective-permute-done.16
  174.8 1.7 collective-permute-start.17
  176.5 0.8 collective-permute-start.18
  177.8 4.5 %shard_map.61.c_ref = f32[512,2048]{1,0:T(8,128)} custom-call(f32[48,128]{1,0:T(8,128)S(1)} %get-tuple-element.68.after_ref, f32[512,256]{1,0:T(8,128)S(1)} %get-tuple-element.48.o_ref, f32[8,256]{1,0:T(8,128)S(1)} %get-tuple-element.72.rs_ref, bf16[2,256,2048]{2,1,0:T(8,128)(2,1)} %get-tuple-element.73.raw_ref), custom_call_target="tpu_custom_call" | custom-call | flops 1610612736 | bytes 8388608 | tf_op jit(solution)/shard_map/pallas_call | solution.py:605
  182.3 10.7 %shard_map.60 = (f32[256,256]{1,0:T(8,128)S(1)}, f32[512,256]{1,0:T(8,128)S(1)}) custom-call(s32[1]{0:T(128)} %bitcast.n_ref, f32[512,256]{1,0:T(8,128)S(1)} %get-tuple-element.66.p_ref, f32[96,128]{1,0:T(8,128)S(1)} %maximum_select_fusion.1.refs_0_, f32[96,128]{1,0:T(8,128)S(1)} %collective-permute-done.17.refs_1_, ...), custom_call_target="tpu_custom_call" | custom-call | flops 10000000000 | bytes 8388608 | tf_op jit(solution)/shard_map/pallas_call | solution.py:414
  193.0 4.1 %all-to-all-done.3.x_ref = f32[16,256,128]{2,1,0:T(8,128)} async-done(((f32[16,256,128]{2,1,0:T(8,128)}), f32[16,256,128]{2,1,0:T(8,128)}, u32[]{:S(2)}, u32[]{:S(2)}) %all-to-all-start.3) | async-done | bytes 2097184 | tf_op jit(solution)/shard_map/all_to_all | solution.py:773
  197.1 3.8 %shard_map.62 = (bf16[2,256,2048]{2,1,0:T(8,128)(2,1)S(1)}, f32[8,8,256]{2,1,0:T(8,128)}) custom-call(f32[256,256]{1,0:T(8,128)S(1)} %get-tuple-element.70.w_ref, f32[16,256,128]{2,1,0:T(8,128)} %all-to-all-done.3.x_ref), custom_call_target="tpu_custom_call" | custom-call | flops 805306368 | bytes 8388608 | tf_op jit(solution)/shard_map/pallas_call | solution.py:647
  200.9 8.9 %all-to-all-start.4 = ((f32[8,8,256]{2,1,0:T(8,128)}), f32[8,8,256]{2,1,0:T(8,128)S(1)}, u32[]{:S(2)}, u32[]{:S(2)}) async-start(f32[8,8,256]{2,1,0:T(8,128)} %get-tuple-element.75), calls=%async_computation.4 | async-start | bytes 131072 | tf_op jit(solution)/shard_map/all_to_all | solution.py:773
  209.8 4.6 %shard_map.63 = f32[512,2048]{1,0:T(8,128)} custom-call(f32[512,256]{1,0:T(8,128)S(1)} %get-tuple-element.69.o_ref, bf16[2,256,2048]{2,1,0:T(8,128)(2,1)S(1)} %get-tuple-element.76.raw_ref, bf16[2,512,2048]{2,1,0:T(8,128)(2,1)} %get-tuple-element.65.b_ref), custom_call_target="tpu_custom_call" | custom-call | flops 1610612736 | bytes 8388608 | tf_op jit(solution)/shard_map/pallas_call | solution.py:675
  214.6 4.4 %shard_map.64 = bf16[512,2048]{1,0:T(8,128)(2,1)} custom-call(f32[512,256]{1,0:T(8,128)S(1)} %get-tuple-element.69.o_ref, f32[8,8,256]{2,1,0:T(8,128)S(1)} %all-to-all-done.4.sq_ref, bf16[2,256,2048]{2,1,0:T(8,128)(2,1)S(1)} %get-tuple-element.76.raw_ref, f32[512,2048]{1,0:T(8,128)} %shard_map.61.c_ref), custom_call_target="tpu_custom_call" | custom-call | flops 1610612736 | bytes 8388608 | tf_op jit(solution)/shard_map/pallas_call | solution.py:711
  (30 shorter events, 1.5 us)
Async XLA Ops:
  4.8 2.7 %collective-permute-start = (f32[2,128,256]{2,1,0:T(8,128)S(1)}, f32[2,128,256]{2,1,0:T(8,128)S(1)}, u32[]{:S(2)}, u32[]{:S(2)}) collective-permute-start(f32[2,128,256]{2,1,0:T(8,128)S(1)} %constant_dynamic-slice_fusion.1), channel_id=1, source_target_pairs={{0,1},{1,0},{2,3},{3,2},{4,5},{5,4},{6,7},{7,6},{8,9},{9,8},{10,11... | collective-permute-start | bytes 786440 | tf_op jit(solution)/shard_map/ppermute | solution.py:735
  7.6 4.8 %collective-permute-start.1 = (f32[128,256]{1,0:T(8,128)S(1)}, f32[128,256]{1,0:T(8,128)S(1)}, u32[]{:S(2)}, u32[]{:S(2)}) collective-permute-start(f32[128,256]{1,0:T(8,128)S(1)} %get-tuple-element.87), channel_id=1, source_target_pairs={{0,2},{1,3},{2,0},{3,1},{4,6},{5,7},{6,4},{7,5},{8,10},{9,11},{10,... | collective-permute-start | bytes 393224 | tf_op jit(solution)/shard_map/ppermute | solution.py:731
  8.9 5.6 %collective-permute-start.2 = (f32[128,256]{1,0:T(8,128)S(1)}, f32[128,256]{1,0:T(8,128)S(1)}, u32[]{:S(2)}, u32[]{:S(2)}) collective-permute-start(f32[128,256]{1,0:T(8,128)S(1)} %get-tuple-element.86), channel_id=1, source_target_pairs={{0,6},{1,7},{2,4},{3,5},{4,2},{5,3},{6,0},{7,1},{8,14},{9,15},{10,... | collective-permute-start | bytes 393224 | tf_op jit(solution)/shard_map/ppermute | solution.py:731
  14.6 5.1 %collective-permute-start.3 = (f32[128,256]{1,0:T(8,128)S(1)}, f32[128,256]{1,0:T(8,128)S(1)}, u32[]{:S(2)}, u32[]{:S(2)}) collective-permute-start(f32[128,256]{1,0:T(8,128)S(1)} %get-tuple-element.84), channel_id=1, source_target_pairs={{0,6},{1,7},{2,4},{3,5},{4,2},{5,3},{6,0},{7,1},{8,14},{9,15},{10,... | collective-permute-start | bytes 393224 | tf_op jit(solution)/shard_map/ppermute | solution.py:731
  16.5 4.1 %collective-permute-start.4 = (f32[128,256]{1,0:T(8,128)S(1)}, f32[128,256]{1,0:T(8,128)S(1)}, u32[]{:S(2)}, u32[]{:S(2)}) collective-permute-start(f32[128,256]{1,0:T(8,128)S(1)} %get-tuple-element.85), channel_id=1, source_target_pairs={{0,2},{1,3},{2,0},{3,1},{4,6},{5,7},{6,4},{7,5},{8,10},{9,11},{10,... | collective-permute-start | bytes 393224 | tf_op jit(solution)/shard_map/ppermute | solution.py:731
  20.6 3.9 %collective-permute-start.5 = (f32[2,128,256]{2,1,0:T(8,128)S(1)}, f32[2,128,256]{2,1,0:T(8,128)S(1)}, u32[]{:S(2)}, u32[]{:S(2)}) collective-permute-start(f32[2,128,256]{2,1,0:T(8,128)S(1)} %pad_maximum_fusion.1.mine_ref), channel_id=1, source_target_pairs={{0,1},{1,0},{2,3},{3,2},{4,5},{5,4},{6,7},{7,6},{8,9},{9,8},{10,11... | collective-permute-start | bytes 786440 | tf_op jit(solution)/shard_map/ppermute | solution.py:735
  69.2 29.9 %all-to-all-start.1 = ((f32[16,256,128]{2,1,0:T(8,128)}), f32[16,256,128]{2,1,0:T(8,128)S(1)}, u32[]{:S(2)}, u32[]{:S(2)}) async-start(f32[16,256,128]{2,1,0:T(8,128)} %get-tuple-element.50), calls=%async_computation.1 | async-start | bytes 4194304 | tf_op jit(solution)/shard_map/all_to_all | solution.py:773
  73.4 2.7 %collective-permute-start.6 = (f32[48,128]{1,0:T(8,128)S(1)}, f32[48,128]{1,0:T(8,128)S(1)}, u32[]{:S(2)}, u32[]{:S(2)}) collective-permute-start(f32[48,128]{1,0:T(8,128)S(1)} %get-tuple-element.47.after_ref), channel_id=1, source_target_pairs={{0,1},{1,0},{2,3},{3,2},{4,5},{5,4},{6,7},{7,6},{8,9},{9,8},{10,11... | collective-permute-start | bytes 73736 | tf_op jit(solution)/shard_map/ppermute | solution.py:735
  76.2 7.2 %collective-permute-start.7 = (f32[96,128]{1,0:T(8,128)S(1)}, f32[96,128]{1,0:T(8,128)S(1)}, u32[]{:S(2)}, u32[]{:S(2)}) collective-permute-start(f32[96,128]{1,0:T(8,128)S(1)} %maximum_select_fusion.refs_0_), channel_id=1, source_target_pairs={{0,6},{1,7},{2,0},{3,1},{4,2},{5,3},{6,4},{7,5},{8,14},{9,15},{10,... | collective-permute-start | bytes 147464 | tf_op jit(solution)/shard_map/ppermute | solution.py:731
  77.1 6.2 %collective-permute-start.8 = (f32[96,128]{1,0:T(8,128)S(1)}, f32[96,128]{1,0:T(8,128)S(1)}, u32[]{:S(2)}, u32[]{:S(2)}) collective-permute-start(f32[96,128]{1,0:T(8,128)S(1)} %maximum_select_fusion.refs_0_), channel_id=1, source_target_pairs={{0,4},{1,5},{2,6},{3,7},{4,0},{5,1},{6,2},{7,3},{8,12},{9,13},{10,... | collective-permute-start | bytes 147464 | tf_op jit(solution)/shard_map/ppermute | solution.py:731
  77.7 5.7 %collective-permute-start.9 = (f32[96,128]{1,0:T(8,128)S(1)}, f32[96,128]{1,0:T(8,128)S(1)}, u32[]{:S(2)}, u32[]{:S(2)}) collective-permute-start(f32[96,128]{1,0:T(8,128)S(1)} %maximum_select_fusion.refs_0_), channel_id=1, source_target_pairs={{0,2},{1,3},{2,4},{3,5},{4,6},{5,7},{6,0},{7,1},{8,10},{9,11},{10,... | collective-permute-start | bytes 147464 | tf_op jit(solution)/shard_map/ppermute | solution.py:731
  105.1 6.3 %collective-permute-start.10 = (f32[2,136,256]{2,1,0:T(8,128)S(1)}, f32[2,136,256]{2,1,0:T(8,128)S(1)}, u32[]{:S(2)}, u32[]{:S(2)}) collective-permute-start(f32[2,136,256]{2,1,0:T(8,128)S(1)} %constant_dynamic-slice_fusion), channel_id=1, source_target_pairs={{0,1},{1,0},{2,3},{3,2},{4,5},{5,4},{6,7},{7,6},{8,9},{9,8},{10,11... | collective-permute-start | bytes 835592 | tf_op jit(solution)/shard_map/ppermute | solution.py:735
  111.5 5.2 %collective-permute-start.11 = (f32[136,256]{1,0:T(8,128)S(1)}, f32[136,256]{1,0:T(8,128)S(1)}, u32[]{:S(2)}, u32[]{:S(2)}) collective-permute-start(f32[136,256]{1,0:T(8,128)S(1)} %get-tuple-element.83), channel_id=1, source_target_pairs={{0,2},{1,3},{2,0},{3,1},{4,6},{5,7},{6,4},{7,5},{8,10},{9,11},{10,... | collective-permute-start | bytes 417800 | tf_op jit(solution)/shard_map/ppermute | solution.py:731
  111.6 6.2 %collective-permute-start.12 = (f32[136,256]{1,0:T(8,128)S(1)}, f32[136,256]{1,0:T(8,128)S(1)}, u32[]{:S(2)}, u32[]{:S(2)}) collective-permute-start(f32[136,256]{1,0:T(8,128)S(1)} %get-tuple-element.82), channel_id=1, source_target_pairs={{0,6},{1,7},{2,4},{3,5},{4,2},{5,3},{6,0},{7,1},{8,14},{9,15},{10,... | collective-permute-start | bytes 417800 | tf_op jit(solution)/shard_map/ppermute | solution.py:731
  117.9 5.2 %collective-permute-start.13 = (f32[136,256]{1,0:T(8,128)S(1)}, f32[136,256]{1,0:T(8,128)S(1)}, u32[]{:S(2)}, u32[]{:S(2)}) collective-permute-start(f32[136,256]{1,0:T(8,128)S(1)} %get-tuple-element.80), channel_id=1, source_target_pairs={{0,6},{1,7},{2,4},{3,5},{4,2},{5,3},{6,0},{7,1},{8,14},{9,15},{10,... | collective-permute-start | bytes 417800 | tf_op jit(solution)/shard_map/ppermute | solution.py:731
  118.9 4.2 %collective-permute-start.14 = (f32[136,256]{1,0:T(8,128)S(1)}, f32[136,256]{1,0:T(8,128)S(1)}, u32[]{:S(2)}, u32[]{:S(2)}) collective-permute-start(f32[136,256]{1,0:T(8,128)S(1)} %get-tuple-element.81), channel_id=1, source_target_pairs={{0,2},{1,3},{2,0},{3,1},{4,6},{5,7},{6,4},{7,5},{8,10},{9,11},{10,... | collective-permute-start | bytes 417800 | tf_op jit(solution)/shard_map/ppermute | solution.py:731
  123.1 3.6 %collective-permute-start.15 = (f32[2,136,256]{2,1,0:T(8,128)S(1)}, f32[2,136,256]{2,1,0:T(8,128)S(1)}, u32[]{:S(2)}, u32[]{:S(2)}) collective-permute-start(f32[2,136,256]{2,1,0:T(8,128)S(1)} %pad_maximum_fusion.mine_ref), channel_id=1, source_target_pairs={{0,1},{1,0},{2,3},{3,2},{4,5},{5,4},{6,7},{7,6},{8,9},{9,8},{10,11... | collective-permute-start | bytes 835592 | tf_op jit(solution)/shard_map/ppermute | solution.py:735
  166.8 30.3 %all-to-all-start.3 = ((f32[16,256,128]{2,1,0:T(8,128)}), f32[16,256,128]{2,1,0:T(8,128)}, u32[]{:S(2)}, u32[]{:S(2)}) async-start(f32[16,256,128]{2,1,0:T(8,128)} %get-tuple-element.71), calls=%async_computation.3 | async-start | bytes 4194304 | tf_op jit(solution)/shard_map/all_to_all | solution.py:773
  171.5 3.2 %collective-permute-start.16 = (f32[48,128]{1,0:T(8,128)S(1)}, f32[48,128]{1,0:T(8,128)S(1)}, u32[]{:S(2)}, u32[]{:S(2)}) collective-permute-start(f32[48,128]{1,0:T(8,128)S(1)} %get-tuple-element.68.after_ref), channel_id=1, source_target_pairs={{0,1},{1,0},{2,3},{3,2},{4,5},{5,4},{6,7},{7,6},{8,9},{9,8},{10,11... | collective-permute-start | bytes 73736 | tf_op jit(solution)/shard_map/ppermute | solution.py:735
  174.8 7.6 %collective-permute-start.17 = (f32[96,128]{1,0:T(8,128)S(1)}, f32[96,128]{1,0:T(8,128)S(1)}, u32[]{:S(2)}, u32[]{:S(2)}) collective-permute-start(f32[96,128]{1,0:T(8,128)S(1)} %maximum_select_fusion.1.refs_0_), channel_id=1, source_target_pairs={{0,6},{1,7},{2,0},{3,1},{4,2},{5,3},{6,4},{7,5},{8,14},{9,15},{10,... | collective-permute-start | bytes 147464 | tf_op jit(solution)/shard_map/ppermute | solution.py:731
  176.5 5.8 %collective-permute-start.18 = (f32[96,128]{1,0:T(8,128)S(1)}, f32[96,128]{1,0:T(8,128)S(1)}, u32[]{:S(2)}, u32[]{:S(2)}) collective-permute-start(f32[96,128]{1,0:T(8,128)S(1)} %maximum_select_fusion.1.refs_0_), channel_id=1, source_target_pairs={{0,4},{1,5},{2,6},{3,7},{4,0},{5,1},{6,2},{7,3},{8,12},{9,13},{10,... | collective-permute-start | bytes 147464 | tf_op jit(solution)/shard_map/ppermute | solution.py:731
  177.3 5.0 %collective-permute-start.19 = (f32[96,128]{1,0:T(8,128)S(1)}, f32[96,128]{1,0:T(8,128)S(1)}, u32[]{:S(2)}, u32[]{:S(2)}) collective-permute-start(f32[96,128]{1,0:T(8,128)S(1)} %maximum_select_fusion.1.refs_0_), channel_id=1, source_target_pairs={{0,2},{1,3},{2,4},{3,5},{4,6},{5,7},{6,0},{7,1},{8,10},{9,11},{10,... | collective-permute-start | bytes 147464 | tf_op jit(solution)/shard_map/ppermute | solution.py:731
  200.9 13.7 %all-to-all-start.4 = ((f32[8,8,256]{2,1,0:T(8,128)}), f32[8,8,256]{2,1,0:T(8,128)S(1)}, u32[]{:S(2)}, u32[]{:S(2)}) async-start(f32[8,8,256]{2,1,0:T(8,128)} %get-tuple-element.75), calls=%async_computation.4 | async-start | bytes 131072 | tf_op jit(solution)/shard_map/all_to_all | solution.py:773

commit v3 on v2

--- a/solution.py
+++ b/solution.py
@@ -195,8 +195,9 @@
     rs_ref[...] = rs
     p_ref[...] = p
     turned, half = p.T, LANES
-    t[: 2 * half] = exact(turned, p[:, :half], NN)
-    t[2 * half :] = exact(turned[half:], p[:, half:], NN)
+    gram = exact(turned, p, NN)
+    t[: 2 * half] = gram[:, :half]
+    t[2 * half :] = gram[half:, half:]
     size = x_ref.shape[1] - rank
     share = t[pl.ds(pl.multiple_of(n_ref[0] * size, size), size), :]
     pt = split(turned)
@@ -466,8 +467,8 @@
 
     each(turn, x_ref.shape[0])
     rt = (rt_ref[0], rt_ref[1])
-    w = w_ref[...]
-    s_ref[...] = exact(exact(w, dot3(rt, rt, NT), NN), w, NT)
+    w = split(w_ref[...])
+    s_ref[...] = dot3(split(dot3(w, split(dot3(rt, rt, NT)), NN)), w, NT)
     width = a.shape[2] // CHUNKS
     q_sum[...] = jnp.zeros_like(q_sum)
 
@@ -631,14 +632,14 @@
         part = jnp.concatenate([x[k * blocks + q] for q in range(blocks)], axis=1)
         raw = dot3(w, split(part), NN)
         raw_ref[0, :, c], raw_ref[1, :, c] = split(raw)
-        total[...] += jnp.sum(raw * raw, axis=1, keepdims=True)
+        square = raw * raw
+        for q in range(blocks):
+            total[...] += square[:, q * LANES : (q + 1) * LANES]
 
     each(block)
-    n = w_ref.shape[0]
-    squares = jnp.where(same(n), jnp.broadcast_to(total[:, :1], (n, n)), 0.0)
-    row = jnp.sum(squares, axis=0, keepdims=True)
+    row = exact(jnp.ones((8, LANES), F32), total[...], NT)
     for k in range(sq_ref.shape[0]):
-        sq_ref[k] = jnp.broadcast_to(row, (8, n))
+        sq_ref[k] = row
 
 
 def last_raw(w, x, peers):

time: 220 us -> 218 us (level)
  no operation moved by 1% of the time
where the time goes in v3:
time: 218 us
  Pallas kernels  73 us (33%)
  blocking collectives  72.7 us (33%)
  starting transfers between devices  45.7 us (21%)
  waiting for transfers between devices  25 us (11%)
    all_to_all x2, blocking collectives, exchange(): return lax.all_to_all(x, axis, 0, 0, tiled=True)  72.7 us
    pallas_call x2, Pallas kernels, inverse_factor(): call(cholesky_kernel, [SM, VM] + [VM] * len(pieces), [jax.ShapeDtypeStruc...  21.3 us
    all_to_all x3, starting transfers between devices, exchange(): return lax.all_to_all(x, axis, 0, 0, tiled=True)  17.6 us
    ppermute x6, starting transfers between devices, core_permute(): return lax.ppermute(x, 'col', [(k, k ^ 1) for k in range(2 * SIDE)])  16.3 us
    ppermute x14, starting transfers between devices, chip_permute(): return lax.ppermute(x, 'col', pairs)  11.8 us
    all_to_all x3, waiting for transfers between devices, exchange(): return lax.all_to_all(x, axis, 0, 0, tiled=True)  9.33 us
    ppermute x14, waiting for transfers between devices, chip_permute(): return lax.ppermute(x, 'col', pairs)  9.26 us
    pallas_call x2, Pallas kernels, products(): call(kernel, [SM, VM, VM] + [ANY] * len(bigs), [jax.ShapeDtypeStruct(shap...  8.25 us
  transfers between devices with their start and end apart: 23, of which 15 were waited for; matrix products, arithmetic and copies ran while one was open for 0% of the time, Pallas kernels for 20%

profile of v3, /device:TPU:1, one launch (start us, length us, event | category | flops | bytes accessed | tf_op | source)
XLA Modules:
  0.0 217.8 jit_solution(5212265205748024952)
XLA Ops:
  0.6 4.1 %shard_map.50 = f32[512,256]{1,0:T(8,128)S(1)} custom-call(f32[512,2048]{1,0:T(8,128)} %m_ref.5, bf16[2,512,2048]{2,1,0:T(8,128)(2,1)} %g_ref.5, f32[2048,256]{1,0:T(8,128)} %v_ref.1), custom_call_target="tpu_custom_call" | custom-call | flops 1610612736 | bytes 8388608 | tf_op jit(solution)/shard_map/pallas_call | solution.py:165
  4.8 1.5 collective-permute-start
  6.3 1.2 collective-permute-done
  7.6 1.4 collective-permute-start.1
  8.9 1.8 collective-permute-start.2
  10.8 1.6 collective-permute-done.1
  12.3 2.2 %collective-permute-done.2 = f32[128,256]{1,0:T(8,128)S(1)} collective-permute-done((f32[128,256]{1,0:T(8,128)S(1)}, f32[128,256]{1,0:T(8,128)S(1)}, u32[]{:S(2)}, u32[]{:S(2)}) %collective-permute-start.2) | collective-permute-done | bytes 131104 | tf_op jit(solution)/shard_map/ppermute | solution.py:732
  14.6 1.9 collective-permute-start.3
  16.5 3.2 %collective-permute-done.3 = f32[128,256]{1,0:T(8,128)S(1)} collective-permute-done((f32[128,256]{1,0:T(8,128)S(1)}, f32[128,256]{1,0:T(8,128)S(1)}, u32[]{:S(2)}, u32[]{:S(2)}) %collective-permute-start.3) | collective-permute-done | bytes 131104 | tf_op jit(solution)/shard_map/ppermute | solution.py:732
  19.7 0.9 collective-permute-done.4
  20.6 2.7 %collective-permute-start.5 = (f32[2,128,256]{2,1,0:T(8,128)S(1)}, f32[2,128,256]{2,1,0:T(8,128)S(1)}, u32[]{:S(2)}, u32[]{:S(2)}) collective-permute-start(f32[2,128,256]{2,1,0:T(8,128)S(1)} %pad_maximum_fusion.1.mine_ref), channel_id=1, source_target_pairs={{0,1},{1,0},{2,3},{3,2},{4,5},{5,4},{6,7},{7,6},{8,9},{9,8},{10,11... | collective-permute-start | bytes 786440 | tf_op jit(solution)/shard_map/ppermute | solution.py:736
  23.4 1.2 collective-permute-done.5.theirs_ref
  24.5 4.3 %shard_map.51 = (f32[16,304,128]{2,1,0:T(8,128)S(1)}, f32[512,256]{1,0:T(8,128)S(1)}, f32[8,256]{1,0:T(8,128)}) custom-call(s32[1]{0:T(128)} %bitcast.n_ref, f32[2,128,256]{2,1,0:T(8,128)S(1)} %pad_maximum_fusion.1.mine_ref, f32[2,128,256]{2,1,0:T(8,128)S(1)} %collective-permute-done.5.theirs_ref, f32[512,2048]{1,0:T(8,128)} %m_ref.5, ...), custom_call_target="tpu_custom_call" | custom-call | flops 1610612736 | bytes 8388608 | tf_op jit(solution)/shard_map/pallas_call | solution.py:261
  28.8 38.5 %all_to_all.25.x_ref = f32[16,304,128]{2,1,0:T(8,128)S(1)} all-to-all(f32[16,304,128]{2,1,0:T(8,128)S(1)} %get-tuple-element.46), channel_id=1, replica_groups=mesh['row'=16,'col'=8] {'row'}, dimensions={0} | all-to-all | bytes 4980736 | tf_op jit(solution)/shard_map/all_to_all | solution.py:774
  67.3 1.5 shard_map.52
  68.9 4.2 %all-to-all-start.1 = ((f32[16,256,128]{2,1,0:T(8,128)}), f32[16,256,128]{2,1,0:T(8,128)S(1)}, u32[]{:S(2)}, u32[]{:S(2)}) async-start(f32[16,256,128]{2,1,0:T(8,128)} %get-tuple-element.50), calls=%async_computation.1 | async-start | bytes 4194304 | tf_op jit(solution)/shard_map/all_to_all | solution.py:774
  73.1 1.9 collective-permute-start.6
  75.0 0.8 collective-permute-done.6
  75.9 0.9 collective-permute-start.7
  76.8 0.6 collective-permute-start.8
  77.5 5.5 %shard_map.54.a_ref = bf16[2,512,2048]{2,1,0:T(8,128)(2,1)} custom-call(f32[48,128]{1,0:T(8,128)S(1)} %get-tuple-element.47.after_ref, f32[512,2048]{1,0:T(8,128)} %m_ref.5, bf16[2,512,2048]{2,1,0:T(8,128)(2,1)} %g_ref.5), custom_call_target="tpu_custom_call" | custom-call | flops 8388608 | bytes 8388608 | tf_op jit(solution)/shard_map/pallas_call | solution.py:445
  83.1 10.7 %shard_map.53 = (f32[256,256]{1,0:T(8,128)S(1)}, f32[512,256]{1,0:T(8,128)S(1)}) custom-call(s32[1]{0:T(128)} %bitcast.n_ref, f32[512,256]{1,0:T(8,128)S(1)} %get-tuple-element.45.p_ref, f32[96,128]{1,0:T(8,128)S(1)} %maximum_select_fusion.refs_0_, f32[96,128]{1,0:T(8,128)S(1)} %collective-permute-done.7.refs_1_, ...), custom_call_target="tpu_custom_call" | custom-call | flops 10000000000 | bytes 8388608 | tf_op jit(solution)/shard_map/pallas_call | solution.py:415
  93.7 5.0 %all-to-all-done.1.x_ref = f32[16,256,128]{2,1,0:T(8,128)S(1)} async-done(((f32[16,256,128]{2,1,0:T(8,128)}), f32[16,256,128]{2,1,0:T(8,128)S(1)}, u32[]{:S(2)}, u32[]{:S(2)}) %all-to-all-start.1) | async-done | bytes 2097184 | tf_op jit(solution)/shard_map/all_to_all | solution.py:774
  98.7 5.5 %shard_map.55 = (f32[4,136,256]{2,1,0:T(8,128)S(1)}, bf16[2,256,2048]{2,1,0:T(8,128)(2,1)S(1)}) custom-call(f32[512,256]{1,0:T(8,128)S(1)} %get-tuple-element.48.o_ref, f32[256,256]{1,0:T(8,128)S(1)} %get-tuple-element.49.w_ref, f32[16,256,128]{2,1,0:T(8,128)S(1)} %all-to-all-done.1.x_ref, bf16[2,512,2048]{2,1,0:T(8,128)(2,1)} %shard_map.54.a_ref), custom_call_target="tpu_custom_call" | custom-call | flops 2684354560 | bytes 8388608 | tf_op jit(solution)/shard_map/pallas_call | solution.py:498
  104.3 5.3 %collective-permute-start.10 = (f32[2,136,256]{2,1,0:T(8,128)S(1)}, f32[2,136,256]{2,1,0:T(8,128)S(1)}, u32[]{:S(2)}, u32[]{:S(2)}) collective-permute-start(f32[2,136,256]{2,1,0:T(8,128)S(1)} %constant_dynamic-slice_fusion), channel_id=1, source_target_pairs={{0,1},{1,0},{2,3},{3,2},{4,5},{5,4},{6,7},{7,6},{8,9},{9,8},{10,11... | collective-permute-start | bytes 835592 | tf_op jit(solution)/shard_map/ppermute | solution.py:736
  109.6 1.2 collective-permute-done.10
  111.0 1.0 collective-permute-start.12
  111.9 4.0 %shard_map.56 = (bf16[2,256,2048]{2,1,0:T(8,128)(2,1)}, bf16[2,512,2048]{2,1,0:T(8,128)(2,1)}) custom-call(f32[512,256]{1,0:T(8,128)S(1)} %get-tuple-element.48.o_ref, f32[256,256]{1,0:T(8,128)S(1)} %get-tuple-element.49.w_ref, bf16[2,256,2048]{2,1,0:T(8,128)(2,1)S(1)} %get-tuple-element.54.rt_ref, bf16[2,512,2048]{2,1,0:T(8,128)(2,1)} %shard_map.54.a_ref), custom_call_target="tpu_custom_call" | custom-call | flops 1342177280 | bytes 8388608 | tf_op jit(solution)/shard_map/pallas_call | solution.py:557
  116.0 1.2 collective-permute-done.12
  117.2 1.0 collective-permute-start.13
  118.2 4.0 %shard_map.57 = (bf16[2,256,2048]{2,1,0:T(8,128)(2,1)}, bf16[2,512,2048]{2,1,0:T(8,128)(2,1)}) custom-call(f32[512,256]{1,0:T(8,128)S(1)} %get-tuple-element.48.o_ref, f32[256,256]{1,0:T(8,128)S(1)} %get-tuple-element.49.w_ref, bf16[2,256,2048]{2,1,0:T(8,128)(2,1)S(1)} %get-tuple-element.54.rt_ref, ...), custom_call_target="tpu_custom_call", output_to_operand_aliasing={{0}: (4, {}), {1}: (5, {})} | custom-call | flops 1342177280 | bytes 8388608 | tf_op jit(solution)/shard_map/pallas_call | solution.py:557
  122.5 2.4 %collective-permute-start.15 = (f32[2,136,256]{2,1,0:T(8,128)S(1)}, f32[2,136,256]{2,1,0:T(8,128)S(1)}, u32[]{:S(2)}, u32[]{:S(2)}) collective-permute-start(f32[2,136,256]{2,1,0:T(8,128)S(1)} %pad_maximum_fusion.mine_ref), channel_id=1, source_target_pairs={{0,1},{1,0},{2,3},{3,2},{4,5},{5,4},{6,7},{7,6},{8,9},{9,8},{10,11... | collective-permute-start | bytes 835592 | tf_op jit(solution)/shard_map/ppermute | solution.py:736
  124.9 1.2 collective-permute-done.15.theirs_ref
  126.1 4.0 %shard_map.58 = (f32[16,304,128]{2,1,0:T(8,128)S(1)}, f32[512,256]{1,0:T(8,128)S(1)}, f32[8,256]{1,0:T(8,128)S(1)}) custom-call(s32[1]{0:T(128)} %bitcast.n_ref, f32[2,136,256]{2,1,0:T(8,128)S(1)} %pad_maximum_fusion.mine_ref, f32[2,136,256]{2,1,0:T(8,128)S(1)} %collective-permute-done.15.theirs_ref, bf16[2,512,2048]{2,1,0:T(8,128)(2,1)} %get-tuple-element.65.b_ref), custom_call_target="tpu_custom_call" | custom-call | flops 1610612736 | bytes 8388608 | tf_op jit(solution)/shard_map/pallas_call | solution.py:261
  130.1 34.2 %all_to_all.26.x_ref = f32[16,304,128]{2,1,0:T(8,128)S(1)} all-to-all(f32[16,304,128]{2,1,0:T(8,128)S(1)} %get-tuple-element.67), channel_id=1, replica_groups=mesh['row'=16,'col'=8] {'row'}, dimensions={0} | all-to-all | bytes 4980736 | tf_op jit(solution)/shard_map/all_to_all | solution.py:774
  164.3 1.5 shard_map.59
  165.8 4.4 %all-to-all-start.3 = ((f32[16,256,128]{2,1,0:T(8,128)}), f32[16,256,128]{2,1,0:T(8,128)}, u32[]{:S(2)}, u32[]{:S(2)}) async-start(f32[16,256,128]{2,1,0:T(8,128)} %get-tuple-element.71), calls=%async_computation.3 | async-start | bytes 4194304 | tf_op jit(solution)/shard_map/all_to_all | solution.py:774
  170.3 2.4 %collective-permute-start.16 = (f32[48,128]{1,0:T(8,128)S(1)}, f32[48,128]{1,0:T(8,128)S(1)}, u32[]{:S(2)}, u32[]{:S(2)}) collective-permute-start(f32[48,128]{1,0:T(8,128)S(1)} %get-tuple-element.68.after_ref), channel_id=1, source_target_pairs={{0,1},{1,0},{2,3},{3,2},{4,5},{5,4},{6,7},{7,6},{8,9},{9,8},{10,11... | collective-permute-start | bytes 73736 | tf_op jit(solution)/shard_map/ppermute | solution.py:736
  172.7 0.8 collective-permute-done.16
  173.5 1.8 collective-permute-start.17
  175.3 0.8 collective-permute-start.18
  176.6 4.5 %shard_map.61.c_ref = f32[512,2048]{1,0:T(8,128)} custom-call(f32[48,128]{1,0:T(8,128)S(1)} %get-tuple-element.68.after_ref, f32[512,256]{1,0:T(8,128)S(1)} %get-tuple-element.48.o_ref, f32[8,256]{1,0:T(8,128)S(1)} %get-tuple-element.72.rs_ref, bf16[2,256,2048]{2,1,0:T(8,128)(2,1)} %get-tuple-element.73.raw_ref), custom_call_target="tpu_custom_call" | custom-call | flops 1610612736 | bytes 8388608 | tf_op jit(solution)/shard_map/pallas_call | solution.py:606
  181.1 10.7 %shard_map.60 = (f32[256,256]{1,0:T(8,128)S(1)}, f32[512,256]{1,0:T(8,128)S(1)}) custom-call(s32[1]{0:T(128)} %bitcast.n_ref, f32[512,256]{1,0:T(8,128)S(1)} %get-tuple-element.66.p_ref, f32[96,128]{1,0:T(8,128)S(1)} %maximum_select_fusion.1.refs_0_, f32[96,128]{1,0:T(8,128)S(1)} %collective-permute-done.17.refs_1_, ...), custom_call_target="tpu_custom_call" | custom-call | flops 10000000000 | bytes 8388608 | tf_op jit(solution)/shard_map/pallas_call | solution.py:415
  191.8 4.1 %all-to-all-done.3.x_ref = f32[16,256,128]{2,1,0:T(8,128)} async-done(((f32[16,256,128]{2,1,0:T(8,128)}), f32[16,256,128]{2,1,0:T(8,128)}, u32[]{:S(2)}, u32[]{:S(2)}) %all-to-all-start.3) | async-done | bytes 2097184 | tf_op jit(solution)/shard_map/all_to_all | solution.py:774
  195.9 3.6 %shard_map.62 = (bf16[2,256,2048]{2,1,0:T(8,128)(2,1)S(1)}, f32[8,8,256]{2,1,0:T(8,128)}) custom-call(f32[256,256]{1,0:T(8,128)S(1)} %get-tuple-element.70.w_ref, f32[16,256,128]{2,1,0:T(8,128)} %all-to-all-done.3.x_ref), custom_call_target="tpu_custom_call" | custom-call | flops 805306368 | bytes 8388608 | tf_op jit(solution)/shard_map/pallas_call | solution.py:648
  199.5 8.9 %all-to-all-start.4 = ((f32[8,8,256]{2,1,0:T(8,128)}), f32[8,8,256]{2,1,0:T(8,128)S(1)}, u32[]{:S(2)}, u32[]{:S(2)}) async-start(f32[8,8,256]{2,1,0:T(8,128)} %get-tuple-element.75), calls=%async_computation.4 | async-start | bytes 131072 | tf_op jit(solution)/shard_map/all_to_all | solution.py:774
  208.4 4.6 %shard_map.63 = f32[512,2048]{1,0:T(8,128)} custom-call(f32[512,256]{1,0:T(8,128)S(1)} %get-tuple-element.69.o_ref, bf16[2,256,2048]{2,1,0:T(8,128)(2,1)S(1)} %get-tuple-element.76.raw_ref, bf16[2,512,2048]{2,1,0:T(8,128)(2,1)} %get-tuple-element.65.b_ref), custom_call_target="tpu_custom_call" | custom-call | flops 1610612736 | bytes 8388608 | tf_op jit(solution)/shard_map/pallas_call | solution.py:676
  213.2 4.4 %shard_map.64 = bf16[512,2048]{1,0:T(8,128)(2,1)} custom-call(f32[512,256]{1,0:T(8,128)S(1)} %get-tuple-element.69.o_ref, f32[8,8,256]{2,1,0:T(8,128)S(1)} %all-to-all-done.4.sq_ref, bf16[2,256,2048]{2,1,0:T(8,128)(2,1)S(1)} %get-tuple-element.76.raw_ref, f32[512,2048]{1,0:T(8,128)} %shard_map.61.c_ref), custom_call_target="tpu_custom_call" | custom-call | flops 1610612736 | bytes 8388608 | tf_op jit(solution)/shard_map/pallas_call | solution.py:712
  (30 shorter events, 1.6 us)
Async XLA Ops:
  4.8 2.7 %collective-permute-start = (f32[2,128,256]{2,1,0:T(8,128)S(1)}, f32[2,128,256]{2,1,0:T(8,128)S(1)}, u32[]{:S(2)}, u32[]{:S(2)}) collective-permute-start(f32[2,128,256]{2,1,0:T(8,128)S(1)} %constant_dynamic-slice_fusion.1), channel_id=1, source_target_pairs={{0,1},{1,0},{2,3},{3,2},{4,5},{5,4},{6,7},{7,6},{8,9},{9,8},{10,11... | collective-permute-start | bytes 786440 | tf_op jit(solution)/shard_map/ppermute | solution.py:736
  7.6 4.8 %collective-permute-start.1 = (f32[128,256]{1,0:T(8,128)S(1)}, f32[128,256]{1,0:T(8,128)S(1)}, u32[]{:S(2)}, u32[]{:S(2)}) collective-permute-start(f32[128,256]{1,0:T(8,128)S(1)} %get-tuple-element.87), channel_id=1, source_target_pairs={{0,2},{1,3},{2,0},{3,1},{4,6},{5,7},{6,4},{7,5},{8,10},{9,11},{10,... | collective-permute-start | bytes 393224 | tf_op jit(solution)/shard_map/ppermute | solution.py:732
  8.9 5.6 %collective-permute-start.2 = (f32[128,256]{1,0:T(8,128)S(1)}, f32[128,256]{1,0:T(8,128)S(1)}, u32[]{:S(2)}, u32[]{:S(2)}) collective-permute-start(f32[128,256]{1,0:T(8,128)S(1)} %get-tuple-element.86), channel_id=1, source_target_pairs={{0,6},{1,7},{2,4},{3,5},{4,2},{5,3},{6,0},{7,1},{8,14},{9,15},{10,... | collective-permute-start | bytes 393224 | tf_op jit(solution)/shard_map/ppermute | solution.py:732
  14.6 5.1 %collective-permute-start.3 = (f32[128,256]{1,0:T(8,128)S(1)}, f32[128,256]{1,0:T(8,128)S(1)}, u32[]{:S(2)}, u32[]{:S(2)}) collective-permute-start(f32[128,256]{1,0:T(8,128)S(1)} %get-tuple-element.84), channel_id=1, source_target_pairs={{0,6},{1,7},{2,4},{3,5},{4,2},{5,3},{6,0},{7,1},{8,14},{9,15},{10,... | collective-permute-start | bytes 393224 | tf_op jit(solution)/shard_map/ppermute | solution.py:732
  16.5 4.1 %collective-permute-start.4 = (f32[128,256]{1,0:T(8,128)S(1)}, f32[128,256]{1,0:T(8,128)S(1)}, u32[]{:S(2)}, u32[]{:S(2)}) collective-permute-start(f32[128,256]{1,0:T(8,128)S(1)} %get-tuple-element.85), channel_id=1, source_target_pairs={{0,2},{1,3},{2,0},{3,1},{4,6},{5,7},{6,4},{7,5},{8,10},{9,11},{10,... | collective-permute-start | bytes 393224 | tf_op jit(solution)/shard_map/ppermute | solution.py:732
  20.6 3.9 %collective-permute-start.5 = (f32[2,128,256]{2,1,0:T(8,128)S(1)}, f32[2,128,256]{2,1,0:T(8,128)S(1)}, u32[]{:S(2)}, u32[]{:S(2)}) collective-permute-start(f32[2,128,256]{2,1,0:T(8,128)S(1)} %pad_maximum_fusion.1.mine_ref), channel_id=1, source_target_pairs={{0,1},{1,0},{2,3},{3,2},{4,5},{5,4},{6,7},{7,6},{8,9},{9,8},{10,11... | collective-permute-start | bytes 786440 | tf_op jit(solution)/shard_map/ppermute | solution.py:736
  68.9 29.9 %all-to-all-start.1 = ((f32[16,256,128]{2,1,0:T(8,128)}), f32[16,256,128]{2,1,0:T(8,128)S(1)}, u32[]{:S(2)}, u32[]{:S(2)}) async-start(f32[16,256,128]{2,1,0:T(8,128)} %get-tuple-element.50), calls=%async_computation.1 | async-start | bytes 4194304 | tf_op jit(solution)/shard_map/all_to_all | solution.py:774
  73.1 2.7 %collective-permute-start.6 = (f32[48,128]{1,0:T(8,128)S(1)}, f32[48,128]{1,0:T(8,128)S(1)}, u32[]{:S(2)}, u32[]{:S(2)}) collective-permute-start(f32[48,128]{1,0:T(8,128)S(1)} %get-tuple-element.47.after_ref), channel_id=1, source_target_pairs={{0,1},{1,0},{2,3},{3,2},{4,5},{5,4},{6,7},{7,6},{8,9},{9,8},{10,11... | collective-permute-start | bytes 73736 | tf_op jit(solution)/shard_map/ppermute | solution.py:736
  75.9 7.2 %collective-permute-start.7 = (f32[96,128]{1,0:T(8,128)S(1)}, f32[96,128]{1,0:T(8,128)S(1)}, u32[]{:S(2)}, u32[]{:S(2)}) collective-permute-start(f32[96,128]{1,0:T(8,128)S(1)} %maximum_select_fusion.refs_0_), channel_id=1, source_target_pairs={{0,6},{1,7},{2,0},{3,1},{4,2},{5,3},{6,4},{7,5},{8,14},{9,15},{10,... | collective-permute-start | bytes 147464 | tf_op jit(solution)/shard_map/ppermute | solution.py:732
  76.8 6.2 %collective-permute-start.8 = (f32[96,128]{1,0:T(8,128)S(1)}, f32[96,128]{1,0:T(8,128)S(1)}, u32[]{:S(2)}, u32[]{:S(2)}) collective-permute-start(f32[96,128]{1,0:T(8,128)S(1)} %maximum_select_fusion.refs_0_), channel_id=1, source_target_pairs={{0,4},{1,5},{2,6},{3,7},{4,0},{5,1},{6,2},{7,3},{8,12},{9,13},{10,... | collective-permute-start | bytes 147464 | tf_op jit(solution)/shard_map/ppermute | solution.py:732
  77.4 5.7 %collective-permute-start.9 = (f32[96,128]{1,0:T(8,128)S(1)}, f32[96,128]{1,0:T(8,128)S(1)}, u32[]{:S(2)}, u32[]{:S(2)}) collective-permute-start(f32[96,128]{1,0:T(8,128)S(1)} %maximum_select_fusion.refs_0_), channel_id=1, source_target_pairs={{0,2},{1,3},{2,4},{3,5},{4,6},{5,7},{6,0},{7,1},{8,10},{9,11},{10,... | collective-permute-start | bytes 147464 | tf_op jit(solution)/shard_map/ppermute | solution.py:732
  104.3 6.5 %collective-permute-start.10 = (f32[2,136,256]{2,1,0:T(8,128)S(1)}, f32[2,136,256]{2,1,0:T(8,128)S(1)}, u32[]{:S(2)}, u32[]{:S(2)}) collective-permute-start(f32[2,136,256]{2,1,0:T(8,128)S(1)} %constant_dynamic-slice_fusion), channel_id=1, source_target_pairs={{0,1},{1,0},{2,3},{3,2},{4,5},{5,4},{6,7},{7,6},{8,9},{9,8},{10,11... | collective-permute-start | bytes 835592 | tf_op jit(solution)/shard_map/ppermute | solution.py:736
  110.9 5.1 %collective-permute-start.11 = (f32[136,256]{1,0:T(8,128)S(1)}, f32[136,256]{1,0:T(8,128)S(1)}, u32[]{:S(2)}, u32[]{:S(2)}) collective-permute-start(f32[136,256]{1,0:T(8,128)S(1)} %get-tuple-element.83), channel_id=1, source_target_pairs={{0,2},{1,3},{2,0},{3,1},{4,6},{5,7},{6,4},{7,5},{8,10},{9,11},{10,... | collective-permute-start | bytes 417800 | tf_op jit(solution)/shard_map/ppermute | solution.py:732
  111.0 6.2 %collective-permute-start.12 = (f32[136,256]{1,0:T(8,128)S(1)}, f32[136,256]{1,0:T(8,128)S(1)}, u32[]{:S(2)}, u32[]{:S(2)}) collective-permute-start(f32[136,256]{1,0:T(8,128)S(1)} %get-tuple-element.82), channel_id=1, source_target_pairs={{0,6},{1,7},{2,4},{3,5},{4,2},{5,3},{6,0},{7,1},{8,14},{9,15},{10,... | collective-permute-start | bytes 417800 | tf_op jit(solution)/shard_map/ppermute | solution.py:732
  117.2 5.2 %collective-permute-start.13 = (f32[136,256]{1,0:T(8,128)S(1)}, f32[136,256]{1,0:T(8,128)S(1)}, u32[]{:S(2)}, u32[]{:S(2)}) collective-permute-start(f32[136,256]{1,0:T(8,128)S(1)} %get-tuple-element.80), channel_id=1, source_target_pairs={{0,6},{1,7},{2,4},{3,5},{4,2},{5,3},{6,0},{7,1},{8,14},{9,15},{10,... | collective-permute-start | bytes 417800 | tf_op jit(solution)/shard_map/ppermute | solution.py:732
  118.2 4.2 %collective-permute-start.14 = (f32[136,256]{1,0:T(8,128)S(1)}, f32[136,256]{1,0:T(8,128)S(1)}, u32[]{:S(2)}, u32[]{:S(2)}) collective-permute-start(f32[136,256]{1,0:T(8,128)S(1)} %get-tuple-element.81), channel_id=1, source_target_pairs={{0,2},{1,3},{2,0},{3,1},{4,6},{5,7},{6,4},{7,5},{8,10},{9,11},{10,... | collective-permute-start | bytes 417800 | tf_op jit(solution)/shard_map/ppermute | solution.py:732
  122.5 3.6 %collective-permute-start.15 = (f32[2,136,256]{2,1,0:T(8,128)S(1)}, f32[2,136,256]{2,1,0:T(8,128)S(1)}, u32[]{:S(2)}, u32[]{:S(2)}) collective-permute-start(f32[2,136,256]{2,1,0:T(8,128)S(1)} %pad_maximum_fusion.mine_ref), channel_id=1, source_target_pairs={{0,1},{1,0},{2,3},{3,2},{4,5},{5,4},{6,7},{7,6},{8,9},{9,8},{10,11... | collective-permute-start | bytes 835592 | tf_op jit(solution)/shard_map/ppermute | solution.py:736
  165.8 30.1 %all-to-all-start.3 = ((f32[16,256,128]{2,1,0:T(8,128)}), f32[16,256,128]{2,1,0:T(8,128)}, u32[]{:S(2)}, u32[]{:S(2)}) async-start(f32[16,256,128]{2,1,0:T(8,128)} %get-tuple-element.71), calls=%async_computation.3 | async-start | bytes 4194304 | tf_op jit(solution)/shard_map/all_to_all | solution.py:774
  170.3 3.3 %collective-permute-start.16 = (f32[48,128]{1,0:T(8,128)S(1)}, f32[48,128]{1,0:T(8,128)S(1)}, u32[]{:S(2)}, u32[]{:S(2)}) collective-permute-start(f32[48,128]{1,0:T(8,128)S(1)} %get-tuple-element.68.after_ref), channel_id=1, source_target_pairs={{0,1},{1,0},{2,3},{3,2},{4,5},{5,4},{6,7},{7,6},{8,9},{9,8},{10,11... | collective-permute-start | bytes 73736 | tf_op jit(solution)/shard_map/ppermute | solution.py:736
  173.5 7.6 %collective-permute-start.17 = (f32[96,128]{1,0:T(8,128)S(1)}, f32[96,128]{1,0:T(8,128)S(1)}, u32[]{:S(2)}, u32[]{:S(2)}) collective-permute-start(f32[96,128]{1,0:T(8,128)S(1)} %maximum_select_fusion.1.refs_0_), channel_id=1, source_target_pairs={{0,6},{1,7},{2,0},{3,1},{4,2},{5,3},{6,4},{7,5},{8,14},{9,15},{10,... | collective-permute-start | bytes 147464 | tf_op jit(solution)/shard_map/ppermute | solution.py:732
  175.3 5.8 %collective-permute-start.18 = (f32[96,128]{1,0:T(8,128)S(1)}, f32[96,128]{1,0:T(8,128)S(1)}, u32[]{:S(2)}, u32[]{:S(2)}) collective-permute-start(f32[96,128]{1,0:T(8,128)S(1)} %maximum_select_fusion.1.refs_0_), channel_id=1, source_target_pairs={{0,4},{1,5},{2,6},{3,7},{4,0},{5,1},{6,2},{7,3},{8,12},{9,13},{10,... | collective-permute-start | bytes 147464 | tf_op jit(solution)/shard_map/ppermute | solution.py:732
  176.0 5.1 %collective-permute-start.19 = (f32[96,128]{1,0:T(8,128)S(1)}, f32[96,128]{1,0:T(8,128)S(1)}, u32[]{:S(2)}, u32[]{:S(2)}) collective-permute-start(f32[96,128]{1,0:T(8,128)S(1)} %maximum_select_fusion.1.refs_0_), channel_id=1, source_target_pairs={{0,2},{1,3},{2,4},{3,5},{4,6},{5,7},{6,0},{7,1},{8,10},{9,11},{10,... | collective-permute-start | bytes 147464 | tf_op jit(solution)/shard_map/ppermute | solution.py:732
  199.5 13.8 %all-to-all-start.4 = ((f32[8,8,256]{2,1,0:T(8,128)}), f32[8,8,256]{2,1,0:T(8,128)S(1)}, u32[]{:S(2)}, u32[]{:S(2)}) async-start(f32[8,8,256]{2,1,0:T(8,128)} %get-tuple-element.75), calls=%async_computation.4 | async-start | bytes 131072 | tf_op jit(solution)/shard_map/all_to_all | solution.py:774

commit v4 on v3

--- a/solution.py
+++ b/solution.py
@@ -116,6 +116,11 @@
 
 def each(block, count=CHUNKS):
     lax.fori_loop(0, count, lambda k, _: (block(k), 0)[1], 0)
+
+
+def lower(n):
+    i = lax.broadcasted_iota(jnp.int32, (n, n), 0)
+    return i >= lax.broadcasted_iota(jnp.int32, (n, n), 1)
 
 
 def same(n):
@@ -196,8 +201,11 @@
     p_ref[...] = p
     turned, half = p.T, LANES
     gram = exact(turned, p, NN)
-    t[: 2 * half] = gram[:, :half]
-    t[2 * half :] = gram[half:, half:]
+    head, last = gram[:half, :half], gram[half:, half:]
+    t[:half] = jnp.where(lower(half), head, last)
+    t[half : 2 * half] = gram[half:, :half]
+    diagonal = jnp.sum(jnp.where(same(half), last, 0.0), axis=0, keepdims=True)
+    t[2 * half :] = jnp.broadcast_to(diagonal, (t.shape[0] - 2 * half, half))
     size = x_ref.shape[1] - rank
     share = t[pl.ds(pl.multiple_of(n_ref[0] * size, size), size), :]
     pt = split(turned)
@@ -256,7 +264,7 @@
 def products(kernel, place, mine, theirs, bigs, held, peers):
     rows, cols = bigs[0].shape[-2:]
     _, height, rank = mine.shape
-    tail = 3 * LANES // peers
+    tail = -(-(2 * LANES + 8) // (8 * peers)) * 8
     shape = (cols // LANES, rank + tail, LANES)
     return call(
         kernel,
@@ -271,7 +279,7 @@
         + [
             dma(CHUNKS, len(bigs)),
             pltpu.VMEM((4, height, rank), F32),
-            pltpu.VMEM((3 * LANES, LANES), F32),
+            pltpu.VMEM((peers * tail, LANES), F32),
             pltpu.VMEM((tail, LANES), F32),
             pltpu.VMEM((2, rank, rows), BF16),
         ],
@@ -382,13 +390,20 @@
 
 
 def cholesky_kernel(n_ref, p_ref, *refs):
-    pieces, (w_ref, o_ref, a, low) = refs[:-4], refs[-4:]
+    pieces, (w_ref, o_ref, packed, a, low) = refs[:-5], refs[-5:]
     size = pieces[0].shape[0]
     count = len(pieces)
     for k, piece in enumerate(pieces):
         place = lax.rem(n_ref[0] // 2 + k, count)
-        a[pl.ds(pl.multiple_of(place * size, size), size), :] = piece[...]
+        packed[pl.ds(pl.multiple_of(place * size, size), size), :] = piece[...]
     half = LANES
+    both = packed[:half]
+    turned = both.T
+    a[:half] = jnp.where(lower(half), both, turned)
+    a[half : 2 * half] = packed[half : 2 * half]
+    a[2 * half :] = jnp.where(
+        same(half), packed[2 * half : 2 * half + 1], jnp.where(lower(half), turned, both)
+    )
 
     def body(b, carry):
         w = eliminated(a[pl.ds(pl.multiple_of(2 * b * half, half), half), :])
@@ -417,7 +432,11 @@
         [SM, VM] + [VM] * len(pieces),
         [jax.ShapeDtypeStruct((rank, rank), F32), jax.ShapeDtypeStruct(p.shape, F32)],
         [VM, VM],
-        [pltpu.VMEM((3 * LANES, LANES), F32), pltpu.VMEM((LANES, LANES), F32)],
+        [
+            pltpu.VMEM((len(pieces) * pieces[0].shape[0], LANES), F32),
+            pltpu.VMEM((3 * LANES, LANES), F32),
+            pltpu.VMEM((LANES, LANES), F32),
+        ],
         10**10,
     )(place, p, *pieces)
 

time: 218 us -> 217 us (level)
  no operation moved by 1% of the time
where the time goes in v4:
time: 217 us
  Pallas kernels  73.1 us (34%)
  blocking collectives  71.9 us (33%)
  starting transfers between devices  44.8 us (21%)
  waiting for transfers between devices  25.3 us (12%)
    all_to_all x2, blocking collectives, exchange(): return lax.all_to_all(x, axis, 0, 0, tiled=True)  71.9 us
    pallas_call x2, Pallas kernels, inverse_factor(): call(cholesky_kernel, [SM, VM] + [VM] * len(pieces), [jax.ShapeDtypeStruc...  21.5 us
    all_to_all x3, starting transfers between devices, exchange(): return lax.all_to_all(x, axis, 0, 0, tiled=True)  17.1 us
    ppermute x6, starting transfers between devices, core_permute(): return lax.ppermute(x, 'col', [(k, k ^ 1) for k in range(2 * SIDE)])  15.9 us
    ppermute x14, starting transfers between devices, chip_permute(): return lax.ppermute(x, 'col', pairs)  11.8 us
    all_to_all x3, waiting for transfers between devices, exchange(): return lax.all_to_all(x, axis, 0, 0, tiled=True)  9.61 us
    ppermute x14, waiting for transfers between devices, chip_permute(): return lax.ppermute(x, 'col', pairs)  9.28 us
    pallas_call x2, Pallas kernels, products(): call(kernel, [SM, VM, VM] + [ANY] * len(bigs), [jax.ShapeDtypeStruct(shap...  8.26 us
  transfers between devices with their start and end apart: 23, of which 15 were waited for; matrix products, arithmetic and copies ran while one was open for 0% of the time, Pallas kernels for 20%

profile of v4, /device:TPU:1, one launch (start us, length us, event | category | flops | bytes accessed | tf_op | source)
XLA Modules:
  0.0 216.5 jit_solution(8425362748764643591)
XLA Ops:
  0.6 4.1 %shard_map.50 = f32[512,256]{1,0:T(8,128)S(1)} custom-call(f32[512,2048]{1,0:T(8,128)} %m_ref.5, bf16[2,512,2048]{2,1,0:T(8,128)(2,1)} %g_ref.5, f32[2048,256]{1,0:T(8,128)} %v_ref.1), custom_call_target="tpu_custom_call" | custom-call | flops 1610612736 | bytes 8388608 | tf_op jit(solution)/shard_map/pallas_call | solution.py:170
  4.8 1.5 collective-permute-start
  6.3 1.2 collective-permute-done
  7.6 1.4 collective-permute-start.1
  8.9 1.8 collective-permute-start.2
  10.8 1.6 collective-permute-done.1
  12.3 2.2 %collective-permute-done.2 = f32[128,256]{1,0:T(8,128)S(1)} collective-permute-done((f32[128,256]{1,0:T(8,128)S(1)}, f32[128,256]{1,0:T(8,128)S(1)}, u32[]{:S(2)}, u32[]{:S(2)}) %collective-permute-start.2) | collective-permute-done | bytes 131104 | tf_op jit(solution)/shard_map/ppermute | solution.py:751
  14.6 1.9 collective-permute-start.3
  16.5 3.2 %collective-permute-done.3 = f32[128,256]{1,0:T(8,128)S(1)} collective-permute-done((f32[128,256]{1,0:T(8,128)S(1)}, f32[128,256]{1,0:T(8,128)S(1)}, u32[]{:S(2)}, u32[]{:S(2)}) %collective-permute-start.3) | collective-permute-done | bytes 131104 | tf_op jit(solution)/shard_map/ppermute | solution.py:751
  19.7 0.9 collective-permute-done.4
  20.6 2.7 %collective-permute-start.5 = (f32[2,128,256]{2,1,0:T(8,128)S(1)}, f32[2,128,256]{2,1,0:T(8,128)S(1)}, u32[]{:S(2)}, u32[]{:S(2)}) collective-permute-start(f32[2,128,256]{2,1,0:T(8,128)S(1)} %pad_maximum_fusion.1.mine_ref), channel_id=1, source_target_pairs={{0,1},{1,0},{2,3},{3,2},{4,5},{5,4},{6,7},{7,6},{8,9},{9,8},{10,11... | collective-permute-start | bytes 786440 | tf_op jit(solution)/shard_map/ppermute | solution.py:755
  23.4 1.2 collective-permute-done.5.theirs_ref
  24.5 4.3 %shard_map.51 = (f32[16,296,128]{2,1,0:T(8,128)S(1)}, f32[512,256]{1,0:T(8,128)S(1)}, f32[8,256]{1,0:T(8,128)}) custom-call(s32[1]{0:T(128)} %bitcast.n_ref, f32[2,128,256]{2,1,0:T(8,128)S(1)} %pad_maximum_fusion.1.mine_ref, f32[2,128,256]{2,1,0:T(8,128)S(1)} %collective-permute-done.5.theirs_ref, f32[512,2048]{1,0:T(8,128)} %m_ref.5, ...), custom_call_target="tpu_custom_call" | custom-call | flops 1610612736 | bytes 8388608 | tf_op jit(solution)/shard_map/pallas_call | solution.py:269
  28.8 38.1 %all_to_all.25.x_ref = f32[16,296,128]{2,1,0:T(8,128)S(1)} all-to-all(f32[16,296,128]{2,1,0:T(8,128)S(1)} %get-tuple-element.46), channel_id=1, replica_groups=mesh['row'=16,'col'=8] {'row'}, dimensions={0} | all-to-all | bytes 4849664 | tf_op jit(solution)/shard_map/all_to_all | solution.py:793
  67.0 1.5 shard_map.52
  68.5 3.9 %all-to-all-start.1 = ((f32[16,256,128]{2,1,0:T(8,128)}), f32[16,256,128]{2,1,0:T(8,128)S(1)}, u32[]{:S(2)}, u32[]{:S(2)}) async-start(f32[16,256,128]{2,1,0:T(8,128)} %get-tuple-element.50), calls=%async_computation.1 | async-start | bytes 4194304 | tf_op jit(solution)/shard_map/all_to_all | solution.py:793
  72.4 1.9 collective-permute-start.6
  74.4 0.8 collective-permute-done.6
  75.2 0.9 collective-permute-start.7
  76.2 0.6 collective-permute-start.8
  76.8 5.5 %shard_map.54.a_ref = bf16[2,512,2048]{2,1,0:T(8,128)(2,1)} custom-call(f32[40,128]{1,0:T(8,128)S(1)} %get-tuple-element.47.after_ref, f32[512,2048]{1,0:T(8,128)} %m_ref.5, bf16[2,512,2048]{2,1,0:T(8,128)(2,1)} %g_ref.5), custom_call_target="tpu_custom_call" | custom-call | flops 8388608 | bytes 8388608 | tf_op jit(solution)/shard_map/pallas_call | solution.py:464
  82.4 10.7 %shard_map.53 = (f32[256,256]{1,0:T(8,128)S(1)}, f32[512,256]{1,0:T(8,128)S(1)}) custom-call(s32[1]{0:T(128)} %bitcast.n_ref, f32[512,256]{1,0:T(8,128)S(1)} %get-tuple-element.45.p_ref, f32[80,128]{1,0:T(8,128)S(1)} %maximum_select_fusion.refs_0_, f32[80,128]{1,0:T(8,128)S(1)} %collective-permute-done.7.refs_1_, ...), custom_call_target="tpu_custom_call" | custom-call | flops 10000000000 | bytes 8388608 | tf_op jit(solution)/shard_map/pallas_call | solution.py:430
  93.1 4.9 %all-to-all-done.1.x_ref = f32[16,256,128]{2,1,0:T(8,128)S(1)} async-done(((f32[16,256,128]{2,1,0:T(8,128)}), f32[16,256,128]{2,1,0:T(8,128)S(1)}, u32[]{:S(2)}, u32[]{:S(2)}) %all-to-all-start.1) | async-done | bytes 2097184 | tf_op jit(solution)/shard_map/all_to_all | solution.py:793
  98.1 5.5 %shard_map.55 = (f32[4,136,256]{2,1,0:T(8,128)S(1)}, bf16[2,256,2048]{2,1,0:T(8,128)(2,1)S(1)}) custom-call(f32[512,256]{1,0:T(8,128)S(1)} %get-tuple-element.48.o_ref, f32[256,256]{1,0:T(8,128)S(1)} %get-tuple-element.49.w_ref, f32[16,256,128]{2,1,0:T(8,128)S(1)} %all-to-all-done.1.x_ref, bf16[2,512,2048]{2,1,0:T(8,128)(2,1)} %shard_map.54.a_ref), custom_call_target="tpu_custom_call" | custom-call | flops 2684354560 | bytes 8388608 | tf_op jit(solution)/shard_map/pallas_call | solution.py:517
  103.6 5.2 %collective-permute-start.10 = (f32[2,136,256]{2,1,0:T(8,128)S(1)}, f32[2,136,256]{2,1,0:T(8,128)S(1)}, u32[]{:S(2)}, u32[]{:S(2)}) collective-permute-start(f32[2,136,256]{2,1,0:T(8,128)S(1)} %constant_dynamic-slice_fusion), channel_id=1, source_target_pairs={{0,1},{1,0},{2,3},{3,2},{4,5},{5,4},{6,7},{7,6},{8,9},{9,8},{10,11... | collective-permute-start | bytes 835592 | tf_op jit(solution)/shard_map/ppermute | solution.py:755
  108.8 1.2 collective-permute-done.10
  110.1 1.0 collective-permute-start.12
  111.1 4.0 %shard_map.56 = (bf16[2,256,2048]{2,1,0:T(8,128)(2,1)}, bf16[2,512,2048]{2,1,0:T(8,128)(2,1)}) custom-call(f32[512,256]{1,0:T(8,128)S(1)} %get-tuple-element.48.o_ref, f32[256,256]{1,0:T(8,128)S(1)} %get-tuple-element.49.w_ref, bf16[2,256,2048]{2,1,0:T(8,128)(2,1)S(1)} %get-tuple-element.54.rt_ref, bf16[2,512,2048]{2,1,0:T(8,128)(2,1)} %shard_map.54.a_ref), custom_call_target="tpu_custom_call" | custom-call | flops 1342177280 | bytes 8388608 | tf_op jit(solution)/shard_map/pallas_call | solution.py:576
  115.1 1.2 collective-permute-done.12
  116.3 1.0 collective-permute-start.13
  117.3 4.0 %shard_map.57 = (bf16[2,256,2048]{2,1,0:T(8,128)(2,1)}, bf16[2,512,2048]{2,1,0:T(8,128)(2,1)}) custom-call(f32[512,256]{1,0:T(8,128)S(1)} %get-tuple-element.48.o_ref, f32[256,256]{1,0:T(8,128)S(1)} %get-tuple-element.49.w_ref, bf16[2,256,2048]{2,1,0:T(8,128)(2,1)S(1)} %get-tuple-element.54.rt_ref, ...), custom_call_target="tpu_custom_call", output_to_operand_aliasing={{0}: (4, {}), {1}: (5, {})} | custom-call | flops 1342177280 | bytes 8388608 | tf_op jit(solution)/shard_map/pallas_call | solution.py:576
  121.6 2.4 %collective-permute-start.15 = (f32[2,136,256]{2,1,0:T(8,128)S(1)}, f32[2,136,256]{2,1,0:T(8,128)S(1)}, u32[]{:S(2)}, u32[]{:S(2)}) collective-permute-start(f32[2,136,256]{2,1,0:T(8,128)S(1)} %pad_maximum_fusion.mine_ref), channel_id=1, source_target_pairs={{0,1},{1,0},{2,3},{3,2},{4,5},{5,4},{6,7},{7,6},{8,9},{9,8},{10,11... | collective-permute-start | bytes 835592 | tf_op jit(solution)/shard_map/ppermute | solution.py:755
  124.0 1.2 collective-permute-done.15.theirs_ref
  125.2 4.0 %shard_map.58 = (f32[16,296,128]{2,1,0:T(8,128)S(1)}, f32[512,256]{1,0:T(8,128)S(1)}, f32[8,256]{1,0:T(8,128)S(1)}) custom-call(s32[1]{0:T(128)} %bitcast.n_ref, f32[2,136,256]{2,1,0:T(8,128)S(1)} %pad_maximum_fusion.mine_ref, f32[2,136,256]{2,1,0:T(8,128)S(1)} %collective-permute-done.15.theirs_ref, bf16[2,512,2048]{2,1,0:T(8,128)(2,1)} %get-tuple-element.65.b_ref), custom_call_target="tpu_custom_call" | custom-call | flops 1610612736 | bytes 8388608 | tf_op jit(solution)/shard_map/pallas_call | solution.py:269
  129.2 33.8 %all_to_all.26.x_ref = f32[16,296,128]{2,1,0:T(8,128)S(1)} all-to-all(f32[16,296,128]{2,1,0:T(8,128)S(1)} %get-tuple-element.67), channel_id=1, replica_groups=mesh['row'=16,'col'=8] {'row'}, dimensions={0} | all-to-all | bytes 4849664 | tf_op jit(solution)/shard_map/all_to_all | solution.py:793
  163.0 1.5 shard_map.59
  164.6 4.4 %all-to-all-start.3 = ((f32[16,256,128]{2,1,0:T(8,128)}), f32[16,256,128]{2,1,0:T(8,128)}, u32[]{:S(2)}, u32[]{:S(2)}) async-start(f32[16,256,128]{2,1,0:T(8,128)} %get-tuple-element.71), calls=%async_computation.3 | async-start | bytes 4194304 | tf_op jit(solution)/shard_map/all_to_all | solution.py:793
  169.0 2.1 collective-permute-start.16
  171.1 0.8 collective-permute-done.16
  172.0 1.7 collective-permute-start.17
  173.7 0.8 collective-permute-start.18
  175.1 4.5 %shard_map.61.c_ref = f32[512,2048]{1,0:T(8,128)} custom-call(f32[40,128]{1,0:T(8,128)S(1)} %get-tuple-element.68.after_ref, f32[512,256]{1,0:T(8,128)S(1)} %get-tuple-element.48.o_ref, f32[8,256]{1,0:T(8,128)S(1)} %get-tuple-element.72.rs_ref, bf16[2,256,2048]{2,1,0:T(8,128)(2,1)} %get-tuple-element.73.raw_ref), custom_call_target="tpu_custom_call" | custom-call | flops 1610612736 | bytes 8388608 | tf_op jit(solution)/shard_map/pallas_call | solution.py:625
  179.6 10.7 %shard_map.60 = (f32[256,256]{1,0:T(8,128)S(1)}, f32[512,256]{1,0:T(8,128)S(1)}) custom-call(s32[1]{0:T(128)} %bitcast.n_ref, f32[512,256]{1,0:T(8,128)S(1)} %get-tuple-element.66.p_ref, f32[80,128]{1,0:T(8,128)S(1)} %maximum_select_fusion.1.refs_0_, f32[80,128]{1,0:T(8,128)S(1)} %collective-permute-done.17.refs_1_, ...), custom_call_target="tpu_custom_call" | custom-call | flops 10000000000 | bytes 8388608 | tf_op jit(solution)/shard_map/pallas_call | solution.py:430
  190.3 4.4 %all-to-all-done.3.x_ref = f32[16,256,128]{2,1,0:T(8,128)} async-done(((f32[16,256,128]{2,1,0:T(8,128)}), f32[16,256,128]{2,1,0:T(8,128)}, u32[]{:S(2)}, u32[]{:S(2)}) %all-to-all-start.3) | async-done | bytes 2097184 | tf_op jit(solution)/shard_map/all_to_all | solution.py:793
  194.8 3.6 %shard_map.62 = (bf16[2,256,2048]{2,1,0:T(8,128)(2,1)S(1)}, f32[8,8,256]{2,1,0:T(8,128)}) custom-call(f32[256,256]{1,0:T(8,128)S(1)} %get-tuple-element.70.w_ref, f32[16,256,128]{2,1,0:T(8,128)} %all-to-all-done.3.x_ref), custom_call_target="tpu_custom_call" | custom-call | flops 805306368 | bytes 8388608 | tf_op jit(solution)/shard_map/pallas_call | solution.py:667
  198.4 8.7 %all-to-all-start.4 = ((f32[8,8,256]{2,1,0:T(8,128)}), f32[8,8,256]{2,1,0:T(8,128)S(1)}, u32[]{:S(2)}, u32[]{:S(2)}) async-start(f32[8,8,256]{2,1,0:T(8,128)} %get-tuple-element.75), calls=%async_computation.4 | async-start | bytes 131072 | tf_op jit(solution)/shard_map/all_to_all | solution.py:793
  207.1 4.6 %shard_map.63 = f32[512,2048]{1,0:T(8,128)} custom-call(f32[512,256]{1,0:T(8,128)S(1)} %get-tuple-element.69.o_ref, bf16[2,256,2048]{2,1,0:T(8,128)(2,1)S(1)} %get-tuple-element.76.raw_ref, bf16[2,512,2048]{2,1,0:T(8,128)(2,1)} %get-tuple-element.65.b_ref), custom_call_target="tpu_custom_call" | custom-call | flops 1610612736 | bytes 8388608 | tf_op jit(solution)/shard_map/pallas_call | solution.py:695
  211.9 4.4 %shard_map.64 = bf16[512,2048]{1,0:T(8,128)(2,1)} custom-call(f32[512,256]{1,0:T(8,128)S(1)} %get-tuple-element.69.o_ref, f32[8,8,256]{2,1,0:T(8,128)S(1)} %all-to-all-done.4.sq_ref, bf16[2,256,2048]{2,1,0:T(8,128)(2,1)S(1)} %get-tuple-element.76.raw_ref, f32[512,2048]{1,0:T(8,128)} %shard_map.61.c_ref), custom_call_target="tpu_custom_call" | custom-call | flops 1610612736 | bytes 8388608 | tf_op jit(solution)/shard_map/pallas_call | solution.py:731
  (30 shorter events, 1.6 us)
Async XLA Ops:
  4.8 2.7 %collective-permute-start = (f32[2,128,256]{2,1,0:T(8,128)S(1)}, f32[2,128,256]{2,1,0:T(8,128)S(1)}, u32[]{:S(2)}, u32[]{:S(2)}) collective-permute-start(f32[2,128,256]{2,1,0:T(8,128)S(1)} %constant_dynamic-slice_fusion.1), channel_id=1, source_target_pairs={{0,1},{1,0},{2,3},{3,2},{4,5},{5,4},{6,7},{7,6},{8,9},{9,8},{10,11... | collective-permute-start | bytes 786440 | tf_op jit(solution)/shard_map/ppermute | solution.py:755
  7.6 4.8 %collective-permute-start.1 = (f32[128,256]{1,0:T(8,128)S(1)}, f32[128,256]{1,0:T(8,128)S(1)}, u32[]{:S(2)}, u32[]{:S(2)}) collective-permute-start(f32[128,256]{1,0:T(8,128)S(1)} %get-tuple-element.87), channel_id=1, source_target_pairs={{0,2},{1,3},{2,0},{3,1},{4,6},{5,7},{6,4},{7,5},{8,10},{9,11},{10,... | collective-permute-start | bytes 393224 | tf_op jit(solution)/shard_map/ppermute | solution.py:751
  8.9 5.6 %collective-permute-start.2 = (f32[128,256]{1,0:T(8,128)S(1)}, f32[128,256]{1,0:T(8,128)S(1)}, u32[]{:S(2)}, u32[]{:S(2)}) collective-permute-start(f32[128,256]{1,0:T(8,128)S(1)} %get-tuple-element.86), channel_id=1, source_target_pairs={{0,6},{1,7},{2,4},{3,5},{4,2},{5,3},{6,0},{7,1},{8,14},{9,15},{10,... | collective-permute-start | bytes 393224 | tf_op jit(solution)/shard_map/ppermute | solution.py:751
  14.6 5.1 %collective-permute-start.3 = (f32[128,256]{1,0:T(8,128)S(1)}, f32[128,256]{1,0:T(8,128)S(1)}, u32[]{:S(2)}, u32[]{:S(2)}) collective-permute-start(f32[128,256]{1,0:T(8,128)S(1)} %get-tuple-element.84), channel_id=1, source_target_pairs={{0,6},{1,7},{2,4},{3,5},{4,2},{5,3},{6,0},{7,1},{8,14},{9,15},{10,... | collective-permute-start | bytes 393224 | tf_op jit(solution)/shard_map/ppermute | solution.py:751
  16.5 4.1 %collective-permute-start.4 = (f32[128,256]{1,0:T(8,128)S(1)}, f32[128,256]{1,0:T(8,128)S(1)}, u32[]{:S(2)}, u32[]{:S(2)}) collective-permute-start(f32[128,256]{1,0:T(8,128)S(1)} %get-tuple-element.85), channel_id=1, source_target_pairs={{0,2},{1,3},{2,0},{3,1},{4,6},{5,7},{6,4},{7,5},{8,10},{9,11},{10,... | collective-permute-start | bytes 393224 | tf_op jit(solution)/shard_map/ppermute | solution.py:751
  20.6 3.9 %collective-permute-start.5 = (f32[2,128,256]{2,1,0:T(8,128)S(1)}, f32[2,128,256]{2,1,0:T(8,128)S(1)}, u32[]{:S(2)}, u32[]{:S(2)}) collective-permute-start(f32[2,128,256]{2,1,0:T(8,128)S(1)} %pad_maximum_fusion.1.mine_ref), channel_id=1, source_target_pairs={{0,1},{1,0},{2,3},{3,2},{4,5},{5,4},{6,7},{7,6},{8,9},{9,8},{10,11... | collective-permute-start | bytes 786440 | tf_op jit(solution)/shard_map/ppermute | solution.py:755
  68.5 29.5 %all-to-all-start.1 = ((f32[16,256,128]{2,1,0:T(8,128)}), f32[16,256,128]{2,1,0:T(8,128)S(1)}, u32[]{:S(2)}, u32[]{:S(2)}) async-start(f32[16,256,128]{2,1,0:T(8,128)} %get-tuple-element.50), calls=%async_computation.1 | async-start | bytes 4194304 | tf_op jit(solution)/shard_map/all_to_all | solution.py:793
  72.4 2.8 %collective-permute-start.6 = (f32[40,128]{1,0:T(8,128)S(1)}, f32[40,128]{1,0:T(8,128)S(1)}, u32[]{:S(2)}, u32[]{:S(2)}) collective-permute-start(f32[40,128]{1,0:T(8,128)S(1)} %get-tuple-element.47.after_ref), channel_id=1, source_target_pairs={{0,1},{1,0},{2,3},{3,2},{4,5},{5,4},{6,7},{7,6},{8,9},{9,8},{10,11... | collective-permute-start | bytes 61448 | tf_op jit(solution)/shard_map/ppermute | solution.py:755
  75.2 7.2 %collective-permute-start.7 = (f32[80,128]{1,0:T(8,128)S(1)}, f32[80,128]{1,0:T(8,128)S(1)}, u32[]{:S(2)}, u32[]{:S(2)}) collective-permute-start(f32[80,128]{1,0:T(8,128)S(1)} %maximum_select_fusion.refs_0_), channel_id=1, source_target_pairs={{0,6},{1,7},{2,0},{3,1},{4,2},{5,3},{6,4},{7,5},{8,14},{9,15},{10,... | collective-permute-start | bytes 122888 | tf_op jit(solution)/shard_map/ppermute | solution.py:751
  76.2 6.2 %collective-permute-start.8 = (f32[80,128]{1,0:T(8,128)S(1)}, f32[80,128]{1,0:T(8,128)S(1)}, u32[]{:S(2)}, u32[]{:S(2)}) collective-permute-start(f32[80,128]{1,0:T(8,128)S(1)} %maximum_select_fusion.refs_0_), channel_id=1, source_target_pairs={{0,4},{1,5},{2,6},{3,7},{4,0},{5,1},{6,2},{7,3},{8,12},{9,13},{10,... | collective-permute-start | bytes 122888 | tf_op jit(solution)/shard_map/ppermute | solution.py:751
  76.7 5.7 %collective-permute-start.9 = (f32[80,128]{1,0:T(8,128)S(1)}, f32[80,128]{1,0:T(8,128)S(1)}, u32[]{:S(2)}, u32[]{:S(2)}) collective-permute-start(f32[80,128]{1,0:T(8,128)S(1)} %maximum_select_fusion.refs_0_), channel_id=1, source_target_pairs={{0,2},{1,3},{2,4},{3,5},{4,6},{5,7},{6,0},{7,1},{8,10},{9,11},{10,... | collective-permute-start | bytes 122888 | tf_op jit(solution)/shard_map/ppermute | solution.py:751
  103.6 6.4 %collective-permute-start.10 = (f32[2,136,256]{2,1,0:T(8,128)S(1)}, f32[2,136,256]{2,1,0:T(8,128)S(1)}, u32[]{:S(2)}, u32[]{:S(2)}) collective-permute-start(f32[2,136,256]{2,1,0:T(8,128)S(1)} %constant_dynamic-slice_fusion), channel_id=1, source_target_pairs={{0,1},{1,0},{2,3},{3,2},{4,5},{5,4},{6,7},{7,6},{8,9},{9,8},{10,11... | collective-permute-start | bytes 835592 | tf_op jit(solution)/shard_map/ppermute | solution.py:755
  110.0 5.1 %collective-permute-start.11 = (f32[136,256]{1,0:T(8,128)S(1)}, f32[136,256]{1,0:T(8,128)S(1)}, u32[]{:S(2)}, u32[]{:S(2)}) collective-permute-start(f32[136,256]{1,0:T(8,128)S(1)} %get-tuple-element.83), channel_id=1, source_target_pairs={{0,2},{1,3},{2,0},{3,1},{4,6},{5,7},{6,4},{7,5},{8,10},{9,11},{10,... | collective-permute-start | bytes 417800 | tf_op jit(solution)/shard_map/ppermute | solution.py:751
  110.1 6.2 %collective-permute-start.12 = (f32[136,256]{1,0:T(8,128)S(1)}, f32[136,256]{1,0:T(8,128)S(1)}, u32[]{:S(2)}, u32[]{:S(2)}) collective-permute-start(f32[136,256]{1,0:T(8,128)S(1)} %get-tuple-element.82), channel_id=1, source_target_pairs={{0,6},{1,7},{2,4},{3,5},{4,2},{5,3},{6,0},{7,1},{8,14},{9,15},{10,... | collective-permute-start | bytes 417800 | tf_op jit(solution)/shard_map/ppermute | solution.py:751
  116.3 5.2 %collective-permute-start.13 = (f32[136,256]{1,0:T(8,128)S(1)}, f32[136,256]{1,0:T(8,128)S(1)}, u32[]{:S(2)}, u32[]{:S(2)}) collective-permute-start(f32[136,256]{1,0:T(8,128)S(1)} %get-tuple-element.80), channel_id=1, source_target_pairs={{0,6},{1,7},{2,4},{3,5},{4,2},{5,3},{6,0},{7,1},{8,14},{9,15},{10,... | collective-permute-start | bytes 417800 | tf_op jit(solution)/shard_map/ppermute | solution.py:751
  117.3 4.2 %collective-permute-start.14 = (f32[136,256]{1,0:T(8,128)S(1)}, f32[136,256]{1,0:T(8,128)S(1)}, u32[]{:S(2)}, u32[]{:S(2)}) collective-permute-start(f32[136,256]{1,0:T(8,128)S(1)} %get-tuple-element.81), channel_id=1, source_target_pairs={{0,2},{1,3},{2,0},{3,1},{4,6},{5,7},{6,4},{7,5},{8,10},{9,11},{10,... | collective-permute-start | bytes 417800 | tf_op jit(solution)/shard_map/ppermute | solution.py:751
  121.6 3.6 %collective-permute-start.15 = (f32[2,136,256]{2,1,0:T(8,128)S(1)}, f32[2,136,256]{2,1,0:T(8,128)S(1)}, u32[]{:S(2)}, u32[]{:S(2)}) collective-permute-start(f32[2,136,256]{2,1,0:T(8,128)S(1)} %pad_maximum_fusion.mine_ref), channel_id=1, source_target_pairs={{0,1},{1,0},{2,3},{3,2},{4,5},{5,4},{6,7},{7,6},{8,9},{9,8},{10,11... | collective-permute-start | bytes 835592 | tf_op jit(solution)/shard_map/ppermute | solution.py:755
  164.6 30.2 %all-to-all-start.3 = ((f32[16,256,128]{2,1,0:T(8,128)}), f32[16,256,128]{2,1,0:T(8,128)}, u32[]{:S(2)}, u32[]{:S(2)}) async-start(f32[16,256,128]{2,1,0:T(8,128)} %get-tuple-element.71), calls=%async_computation.3 | async-start | bytes 4194304 | tf_op jit(solution)/shard_map/all_to_all | solution.py:793
  169.0 3.0 %collective-permute-start.16 = (f32[40,128]{1,0:T(8,128)S(1)}, f32[40,128]{1,0:T(8,128)S(1)}, u32[]{:S(2)}, u32[]{:S(2)}) collective-permute-start(f32[40,128]{1,0:T(8,128)S(1)} %get-tuple-element.68.after_ref), channel_id=1, source_target_pairs={{0,1},{1,0},{2,3},{3,2},{4,5},{5,4},{6,7},{7,6},{8,9},{9,8},{10,11... | collective-permute-start | bytes 61448 | tf_op jit(solution)/shard_map/ppermute | solution.py:755
  172.0 7.6 %collective-permute-start.17 = (f32[80,128]{1,0:T(8,128)S(1)}, f32[80,128]{1,0:T(8,128)S(1)}, u32[]{:S(2)}, u32[]{:S(2)}) collective-permute-start(f32[80,128]{1,0:T(8,128)S(1)} %maximum_select_fusion.1.refs_0_), channel_id=1, source_target_pairs={{0,6},{1,7},{2,0},{3,1},{4,2},{5,3},{6,4},{7,5},{8,14},{9,15},{10,... | collective-permute-start | bytes 122888 | tf_op jit(solution)/shard_map/ppermute | solution.py:751
  173.7 5.8 %collective-permute-start.18 = (f32[80,128]{1,0:T(8,128)S(1)}, f32[80,128]{1,0:T(8,128)S(1)}, u32[]{:S(2)}, u32[]{:S(2)}) collective-permute-start(f32[80,128]{1,0:T(8,128)S(1)} %maximum_select_fusion.1.refs_0_), channel_id=1, source_target_pairs={{0,4},{1,5},{2,6},{3,7},{4,0},{5,1},{6,2},{7,3},{8,12},{9,13},{10,... | collective-permute-start | bytes 122888 | tf_op jit(solution)/shard_map/ppermute | solution.py:751
  174.5 5.1 %collective-permute-start.19 = (f32[80,128]{1,0:T(8,128)S(1)}, f32[80,128]{1,0:T(8,128)S(1)}, u32[]{:S(2)}, u32[]{:S(2)}) collective-permute-start(f32[80,128]{1,0:T(8,128)S(1)} %maximum_select_fusion.1.refs_0_), channel_id=1, source_target_pairs={{0,2},{1,3},{2,4},{3,5},{4,6},{5,7},{6,0},{7,1},{8,10},{9,11},{10,... | collective-permute-start | bytes 122888 | tf_op jit(solution)/shard_map/ppermute | solution.py:751
  198.4 13.6 %all-to-all-start.4 = ((f32[8,8,256]{2,1,0:T(8,128)}), f32[8,8,256]{2,1,0:T(8,128)S(1)}, u32[]{:S(2)}, u32[]{:S(2)}) async-start(f32[8,8,256]{2,1,0:T(8,128)} %get-tuple-element.75), calls=%async_computation.4 | async-start | bytes 131072 | tf_op jit(solution)/shard_map/all_to_all | solution.py:793

commit v5 on v4

--- a/solution.py
+++ b/solution.py
@@ -11,6 +11,7 @@
 NORM_EPS = 1e-06
 LANES = 128
 CHUNKS = 4
+FEW = 2
 F32 = jnp.float32
 BF16 = jnp.bfloat16
 VMEM_LIMIT = 20 * 1024 * 1024
@@ -236,8 +237,8 @@
     )
 
 
-def pair_moves(b_ref, b):
-    width = b.shape[2] // CHUNKS
+def pair_moves(b_ref, b, count=CHUNKS):
+    width = b.shape[2] // count
 
     def moves(k):
         c = columns(k, width)
@@ -478,7 +479,7 @@
 
 
 def middle_kernel(o_ref, w_ref, x_ref, a_ref, q_ref, rt_ref, a, q_sum, s_ref, sems):
-    wait = fetch(pair_moves(a_ref, a), sems)
+    wait = fetch(pair_moves(a_ref, a, FEW), sems, FEW)
 
     def turn(k):
         c = columns(k, LANES)
@@ -488,7 +489,7 @@
     rt = (rt_ref[0], rt_ref[1])
     w = split(w_ref[...])
     s_ref[...] = dot3(split(dot3(w, split(dot3(rt, rt, NT)), NN)), w, NT)
-    width = a.shape[2] // CHUNKS
+    width = a.shape[2] // FEW
     q_sum[...] = jnp.zeros_like(q_sum)
 
     def block(k):
@@ -498,7 +499,7 @@
             (a[0, :, c], a[1, :, c]), (rt_ref[0, :, c], rt_ref[1, :, c]), NT
         )
 
-    each(block)
+    each(block, FEW)
     s = s_ref[...]
     q = dot3(split(q_sum[...]), split(w_ref[...]), NT) - dot3(
         split((1.0 - KEEP_RATE) * o_ref[...]), split(s), NN
@@ -523,7 +524,7 @@
             pltpu.VMEM((2, rows, cols), BF16),
             pltpu.VMEM((rows, rank), F32),
             pltpu.VMEM((rank, rank), F32),
-            dma(CHUNKS, 1),
+            dma(FEW, 1),
         ],
         10 * rows * cols * rank,
     )(o, w, x, *in_hbm(ahead))
@@ -590,10 +591,12 @@
     )(o, w, rt, *in_hbm(ahead), *in_hbm(*begun))
 
 
-def write_out(value, out_ref, buffer, sems):
-    width = buffer.shape[1] // CHUNKS
+def write_out(value, out_ref, buffer, sems, count=CHUNKS):
+    width = buffer.shape[1] // count
     start, finish = send(
-        lambda k: [(buffer.at[:, columns(k, width)], out_ref.at[:, columns(k, width)])], sems
+        lambda k: [(buffer.at[:, columns(k, width)], out_ref.at[:, columns(k, width)])],
+        sems,
+        count,
     )
 
     def block(k):
@@ -601,7 +604,7 @@
         buffer[:, c] = value(k, c).astype(buffer.dtype)
         start(k)
 
-    each(block)
+    each(block, count)
     finish()
 
 
@@ -638,9 +641,11 @@
 
 
 def last_raw_kernel(w_ref, x_ref, raw_ref, sq_ref, x, total, came):
-    blocks = x_ref.shape[0] // CHUNKS
+    blocks = x_ref.shape[0] // FEW
     wait = fetch(
-        lambda k: [(x_ref.at[columns(k, blocks)], x.at[columns(k, blocks)])], came
+        lambda k: [(x_ref.at[columns(k, blocks)], x.at[columns(k, blocks)])],
+        came,
+        FEW,
     )
     total[...] = jnp.zeros_like(total)
     w = split(w_ref[...])
@@ -655,7 +660,7 @@
         for q in range(blocks):
             total[...] += square[:, q * LANES : (q + 1) * LANES]
 
-    each(block)
+    each(block, FEW)
     row = exact(jnp.ones((8, LANES), F32), total[...], NT)
     for k in range(sq_ref.shape[0]):
         sq_ref[k] = row
@@ -672,7 +677,7 @@
         [
             pltpu.VMEM(x.shape, F32),
             pltpu.VMEM((rank, LANES), F32),
-            dma(CHUNKS, 1),
+            dma(FEW, 1),
         ],
         6 * rank * cols * rank,
     )(w, *in_hbm(x))

time: 217 us -> 216 us (level)
  no operation moved by 1% of the time
where the time goes in v5:
time: 216 us
  Pallas kernels  72.4 us (34%)
  blocking collectives  72 us (33%)
  starting transfers between devices  45 us (21%)
  waiting for transfers between devices  25 us (12%)
    all_to_all x2, blocking collectives, exchange(): return lax.all_to_all(x, axis, 0, 0, tiled=True)  72 us
    pallas_call x2, Pallas kernels, inverse_factor(): call(cholesky_kernel, [SM, VM] + [VM] * len(pieces), [jax.ShapeDtypeStruc...  21.5 us
    all_to_all x3, starting transfers between devices, exchange(): return lax.all_to_all(x, axis, 0, 0, tiled=True)  17.1 us
    ppermute x6, starting transfers between devices, core_permute(): return lax.ppermute(x, 'col', [(k, k ^ 1) for k in range(2 * SIDE)])  16.1 us
    ppermute x14, starting transfers between devices, chip_permute(): return lax.ppermute(x, 'col', pairs)  11.8 us
    all_to_all x3, waiting for transfers between devices, exchange(): return lax.all_to_all(x, axis, 0, 0, tiled=True)  9.39 us
    ppermute x14, waiting for transfers between devices, chip_permute(): return lax.ppermute(x, 'col', pairs)  9.21 us
    pallas_call x2, Pallas kernels, products(): call(kernel, [SM, VM, VM] + [ANY] * len(bigs), [jax.ShapeDtypeStruct(shap...  8.26 us
  transfers between devices with their start and end apart: 23, of which 15 were waited for; matrix products, arithmetic and copies ran while one was open for 0% of the time, Pallas kernels for 20%

profile of v5, /device:TPU:1, one launch (start us, length us, event | category | flops | bytes accessed | tf_op | source)
XLA Modules:
  0.0 215.9 jit_solution(9731332472502437689)
XLA Ops:
  0.6 4.1 %shard_map.50 = f32[512,256]{1,0:T(8,128)S(1)} custom-call(f32[512,2048]{1,0:T(8,128)} %m_ref.5, bf16[2,512,2048]{2,1,0:T(8,128)(2,1)} %g_ref.5, f32[2048,256]{1,0:T(8,128)} %v_ref.1), custom_call_target="tpu_custom_call" | custom-call | flops 1610612736 | bytes 8388608 | tf_op jit(solution)/shard_map/pallas_call | solution.py:171
  4.8 1.5 collective-permute-start
  6.3 1.2 collective-permute-done
  7.6 1.4 collective-permute-start.1
  8.9 1.8 collective-permute-start.2
  10.8 1.6 collective-permute-done.1
  12.3 2.2 %collective-permute-done.2 = f32[128,256]{1,0:T(8,128)S(1)} collective-permute-done((f32[128,256]{1,0:T(8,128)S(1)}, f32[128,256]{1,0:T(8,128)S(1)}, u32[]{:S(2)}, u32[]{:S(2)}) %collective-permute-start.2) | collective-permute-done | bytes 131104 | tf_op jit(solution)/shard_map/ppermute | solution.py:756
  14.6 1.9 collective-permute-start.3
  16.5 3.2 %collective-permute-done.3 = f32[128,256]{1,0:T(8,128)S(1)} collective-permute-done((f32[128,256]{1,0:T(8,128)S(1)}, f32[128,256]{1,0:T(8,128)S(1)}, u32[]{:S(2)}, u32[]{:S(2)}) %collective-permute-start.3) | collective-permute-done | bytes 131104 | tf_op jit(solution)/shard_map/ppermute | solution.py:756
  19.7 0.9 collective-permute-done.4
  20.6 2.7 %collective-permute-start.5 = (f32[2,128,256]{2,1,0:T(8,128)S(1)}, f32[2,128,256]{2,1,0:T(8,128)S(1)}, u32[]{:S(2)}, u32[]{:S(2)}) collective-permute-start(f32[2,128,256]{2,1,0:T(8,128)S(1)} %pad_maximum_fusion.1.mine_ref), channel_id=1, source_target_pairs={{0,1},{1,0},{2,3},{3,2},{4,5},{5,4},{6,7},{7,6},{8,9},{9,8},{10,11... | collective-permute-start | bytes 786440 | tf_op jit(solution)/shard_map/ppermute | solution.py:760
  23.4 1.2 collective-permute-done.5.theirs_ref
  24.5 4.3 %shard_map.51 = (f32[16,296,128]{2,1,0:T(8,128)S(1)}, f32[512,256]{1,0:T(8,128)S(1)}, f32[8,256]{1,0:T(8,128)}) custom-call(s32[1]{0:T(128)} %bitcast.n_ref, f32[2,128,256]{2,1,0:T(8,128)S(1)} %pad_maximum_fusion.1.mine_ref, f32[2,128,256]{2,1,0:T(8,128)S(1)} %collective-permute-done.5.theirs_ref, f32[512,2048]{1,0:T(8,128)} %m_ref.5, ...), custom_call_target="tpu_custom_call" | custom-call | flops 1610612736 | bytes 8388608 | tf_op jit(solution)/shard_map/pallas_call | solution.py:270
  28.8 38.1 %all_to_all.25.x_ref = f32[16,296,128]{2,1,0:T(8,128)S(1)} all-to-all(f32[16,296,128]{2,1,0:T(8,128)S(1)} %get-tuple-element.46), channel_id=1, replica_groups=mesh['row'=16,'col'=8] {'row'}, dimensions={0} | all-to-all | bytes 4849664 | tf_op jit(solution)/shard_map/all_to_all | solution.py:798
  67.0 1.5 shard_map.52
  68.5 3.9 %all-to-all-start.1 = ((f32[16,256,128]{2,1,0:T(8,128)}), f32[16,256,128]{2,1,0:T(8,128)S(1)}, u32[]{:S(2)}, u32[]{:S(2)}) async-start(f32[16,256,128]{2,1,0:T(8,128)} %get-tuple-element.50), calls=%async_computation.1 | async-start | bytes 4194304 | tf_op jit(solution)/shard_map/all_to_all | solution.py:798
  72.4 1.9 collective-permute-start.6
  74.4 0.8 collective-permute-done.6
  75.2 0.9 collective-permute-start.7
  76.2 0.6 collective-permute-start.8
  76.8 5.5 %shard_map.54.a_ref = bf16[2,512,2048]{2,1,0:T(8,128)(2,1)} custom-call(f32[40,128]{1,0:T(8,128)S(1)} %get-tuple-element.47.after_ref, f32[512,2048]{1,0:T(8,128)} %m_ref.5, bf16[2,512,2048]{2,1,0:T(8,128)(2,1)} %g_ref.5), custom_call_target="tpu_custom_call" | custom-call | flops 8388608 | bytes 8388608 | tf_op jit(solution)/shard_map/pallas_call | solution.py:465
  82.4 10.7 %shard_map.53 = (f32[256,256]{1,0:T(8,128)S(1)}, f32[512,256]{1,0:T(8,128)S(1)}) custom-call(s32[1]{0:T(128)} %bitcast.n_ref, f32[512,256]{1,0:T(8,128)S(1)} %get-tuple-element.45.p_ref, f32[80,128]{1,0:T(8,128)S(1)} %maximum_select_fusion.refs_0_, f32[80,128]{1,0:T(8,128)S(1)} %collective-permute-done.7.refs_1_, ...), custom_call_target="tpu_custom_call" | custom-call | flops 10000000000 | bytes 8388608 | tf_op jit(solution)/shard_map/pallas_call | solution.py:431
  93.1 4.9 %all-to-all-done.1.x_ref = f32[16,256,128]{2,1,0:T(8,128)S(1)} async-done(((f32[16,256,128]{2,1,0:T(8,128)}), f32[16,256,128]{2,1,0:T(8,128)S(1)}, u32[]{:S(2)}, u32[]{:S(2)}) %all-to-all-start.1) | async-done | bytes 2097184 | tf_op jit(solution)/shard_map/all_to_all | solution.py:798
  98.1 5.0 %shard_map.55 = (f32[4,136,256]{2,1,0:T(8,128)S(1)}, bf16[2,256,2048]{2,1,0:T(8,128)(2,1)S(1)}) custom-call(f32[512,256]{1,0:T(8,128)S(1)} %get-tuple-element.48.o_ref, f32[256,256]{1,0:T(8,128)S(1)} %get-tuple-element.49.w_ref, f32[16,256,128]{2,1,0:T(8,128)S(1)} %all-to-all-done.1.x_ref, bf16[2,512,2048]{2,1,0:T(8,128)(2,1)} %shard_map.54.a_ref), custom_call_target="tpu_custom_call" | custom-call | flops 2684354560 | bytes 8388608 | tf_op jit(solution)/shard_map/pallas_call | solution.py:518
  103.1 5.2 %collective-permute-start.10 = (f32[2,136,256]{2,1,0:T(8,128)S(1)}, f32[2,136,256]{2,1,0:T(8,128)S(1)}, u32[]{:S(2)}, u32[]{:S(2)}) collective-permute-start(f32[2,136,256]{2,1,0:T(8,128)S(1)} %constant_dynamic-slice_fusion), channel_id=1, source_target_pairs={{0,1},{1,0},{2,3},{3,2},{4,5},{5,4},{6,7},{7,6},{8,9},{9,8},{10,11... | collective-permute-start | bytes 835592 | tf_op jit(solution)/shard_map/ppermute | solution.py:760
  108.3 1.2 collective-permute-done.10
  109.7 1.0 collective-permute-start.12
  110.6 4.0 %shard_map.56 = (bf16[2,256,2048]{2,1,0:T(8,128)(2,1)}, bf16[2,512,2048]{2,1,0:T(8,128)(2,1)}) custom-call(f32[512,256]{1,0:T(8,128)S(1)} %get-tuple-element.48.o_ref, f32[256,256]{1,0:T(8,128)S(1)} %get-tuple-element.49.w_ref, bf16[2,256,2048]{2,1,0:T(8,128)(2,1)S(1)} %get-tuple-element.54.rt_ref, bf16[2,512,2048]{2,1,0:T(8,128)(2,1)} %shard_map.54.a_ref), custom_call_target="tpu_custom_call" | custom-call | flops 1342177280 | bytes 8388608 | tf_op jit(solution)/shard_map/pallas_call | solution.py:577
  114.7 1.1 collective-permute-done.12
  115.9 1.0 collective-permute-start.13
  116.9 4.0 %shard_map.57 = (bf16[2,256,2048]{2,1,0:T(8,128)(2,1)}, bf16[2,512,2048]{2,1,0:T(8,128)(2,1)}) custom-call(f32[512,256]{1,0:T(8,128)S(1)} %get-tuple-element.48.o_ref, f32[256,256]{1,0:T(8,128)S(1)} %get-tuple-element.49.w_ref, bf16[2,256,2048]{2,1,0:T(8,128)(2,1)S(1)} %get-tuple-element.54.rt_ref, ...), custom_call_target="tpu_custom_call", output_to_operand_aliasing={{0}: (4, {}), {1}: (5, {})} | custom-call | flops 1342177280 | bytes 8388608 | tf_op jit(solution)/shard_map/pallas_call | solution.py:577
  121.2 2.4 %collective-permute-start.15 = (f32[2,136,256]{2,1,0:T(8,128)S(1)}, f32[2,136,256]{2,1,0:T(8,128)S(1)}, u32[]{:S(2)}, u32[]{:S(2)}) collective-permute-start(f32[2,136,256]{2,1,0:T(8,128)S(1)} %pad_maximum_fusion.mine_ref), channel_id=1, source_target_pairs={{0,1},{1,0},{2,3},{3,2},{4,5},{5,4},{6,7},{7,6},{8,9},{9,8},{10,11... | collective-permute-start | bytes 835592 | tf_op jit(solution)/shard_map/ppermute | solution.py:760
  123.6 1.2 collective-permute-done.15.theirs_ref
  124.8 4.0 %shard_map.58 = (f32[16,296,128]{2,1,0:T(8,128)S(1)}, f32[512,256]{1,0:T(8,128)S(1)}, f32[8,256]{1,0:T(8,128)S(1)}) custom-call(s32[1]{0:T(128)} %bitcast.n_ref, f32[2,136,256]{2,1,0:T(8,128)S(1)} %pad_maximum_fusion.mine_ref, f32[2,136,256]{2,1,0:T(8,128)S(1)} %collective-permute-done.15.theirs_ref, bf16[2,512,2048]{2,1,0:T(8,128)(2,1)} %get-tuple-element.65.b_ref), custom_call_target="tpu_custom_call" | custom-call | flops 1610612736 | bytes 8388608 | tf_op jit(solution)/shard_map/pallas_call | solution.py:270
  128.7 33.8 %all_to_all.26.x_ref = f32[16,296,128]{2,1,0:T(8,128)S(1)} all-to-all(f32[16,296,128]{2,1,0:T(8,128)S(1)} %get-tuple-element.67), channel_id=1, replica_groups=mesh['row'=16,'col'=8] {'row'}, dimensions={0} | all-to-all | bytes 4849664 | tf_op jit(solution)/shard_map/all_to_all | solution.py:798
  162.6 1.5 shard_map.59
  164.1 4.4 %all-to-all-start.3 = ((f32[16,256,128]{2,1,0:T(8,128)}), f32[16,256,128]{2,1,0:T(8,128)}, u32[]{:S(2)}, u32[]{:S(2)}) async-start(f32[16,256,128]{2,1,0:T(8,128)} %get-tuple-element.71), calls=%async_computation.3 | async-start | bytes 4194304 | tf_op jit(solution)/shard_map/all_to_all | solution.py:798
  168.6 2.3 %collective-permute-start.16 = (f32[40,128]{1,0:T(8,128)S(1)}, f32[40,128]{1,0:T(8,128)S(1)}, u32[]{:S(2)}, u32[]{:S(2)}) collective-permute-start(f32[40,128]{1,0:T(8,128)S(1)} %get-tuple-element.68.after_ref), channel_id=1, source_target_pairs={{0,1},{1,0},{2,3},{3,2},{4,5},{5,4},{6,7},{7,6},{8,9},{9,8},{10,11... | collective-permute-start | bytes 61448 | tf_op jit(solution)/shard_map/ppermute | solution.py:760
  170.9 0.8 collective-permute-done.16
  171.8 1.7 collective-permute-start.17
  173.5 0.8 collective-permute-start.18
  174.8 4.5 %shard_map.61.c_ref = f32[512,2048]{1,0:T(8,128)} custom-call(f32[40,128]{1,0:T(8,128)S(1)} %get-tuple-element.68.after_ref, f32[512,256]{1,0:T(8,128)S(1)} %get-tuple-element.48.o_ref, f32[8,256]{1,0:T(8,128)S(1)} %get-tuple-element.72.rs_ref, bf16[2,256,2048]{2,1,0:T(8,128)(2,1)} %get-tuple-element.73.raw_ref), custom_call_target="tpu_custom_call" | custom-call | flops 1610612736 | bytes 8388608 | tf_op jit(solution)/shard_map/pallas_call | solution.py:628
  179.4 10.7 %shard_map.60 = (f32[256,256]{1,0:T(8,128)S(1)}, f32[512,256]{1,0:T(8,128)S(1)}) custom-call(s32[1]{0:T(128)} %bitcast.n_ref, f32[512,256]{1,0:T(8,128)S(1)} %get-tuple-element.66.p_ref, f32[80,128]{1,0:T(8,128)S(1)} %maximum_select_fusion.1.refs_0_, f32[80,128]{1,0:T(8,128)S(1)} %collective-permute-done.17.refs_1_, ...), custom_call_target="tpu_custom_call" | custom-call | flops 10000000000 | bytes 8388608 | tf_op jit(solution)/shard_map/pallas_call | solution.py:431
  190.1 4.2 %all-to-all-done.3.x_ref = f32[16,256,128]{2,1,0:T(8,128)} async-done(((f32[16,256,128]{2,1,0:T(8,128)}), f32[16,256,128]{2,1,0:T(8,128)}, u32[]{:S(2)}, u32[]{:S(2)}) %all-to-all-start.3) | async-done | bytes 2097184 | tf_op jit(solution)/shard_map/all_to_all | solution.py:798
  194.3 3.4 %shard_map.62 = (bf16[2,256,2048]{2,1,0:T(8,128)(2,1)S(1)}, f32[8,8,256]{2,1,0:T(8,128)}) custom-call(f32[256,256]{1,0:T(8,128)S(1)} %get-tuple-element.70.w_ref, f32[16,256,128]{2,1,0:T(8,128)} %all-to-all-done.3.x_ref), custom_call_target="tpu_custom_call" | custom-call | flops 805306368 | bytes 8388608 | tf_op jit(solution)/shard_map/pallas_call | solution.py:672
  197.7 8.7 %all-to-all-start.4 = ((f32[8,8,256]{2,1,0:T(8,128)}), f32[8,8,256]{2,1,0:T(8,128)S(1)}, u32[]{:S(2)}, u32[]{:S(2)}) async-start(f32[8,8,256]{2,1,0:T(8,128)} %get-tuple-element.75), calls=%async_computation.4 | async-start | bytes 131072 | tf_op jit(solution)/shard_map/all_to_all | solution.py:798
  206.5 4.6 %shard_map.63 = f32[512,2048]{1,0:T(8,128)} custom-call(f32[512,256]{1,0:T(8,128)S(1)} %get-tuple-element.69.o_ref, bf16[2,256,2048]{2,1,0:T(8,128)(2,1)S(1)} %get-tuple-element.76.raw_ref, bf16[2,512,2048]{2,1,0:T(8,128)(2,1)} %get-tuple-element.65.b_ref), custom_call_target="tpu_custom_call" | custom-call | flops 1610612736 | bytes 8388608 | tf_op jit(solution)/shard_map/pallas_call | solution.py:700
  211.3 4.4 %shard_map.64 = bf16[512,2048]{1,0:T(8,128)(2,1)} custom-call(f32[512,256]{1,0:T(8,128)S(1)} %get-tuple-element.69.o_ref, f32[8,8,256]{2,1,0:T(8,128)S(1)} %all-to-all-done.4.sq_ref, bf16[2,256,2048]{2,1,0:T(8,128)(2,1)S(1)} %get-tuple-element.76.raw_ref, f32[512,2048]{1,0:T(8,128)} %shard_map.61.c_ref), custom_call_target="tpu_custom_call" | custom-call | flops 1610612736 | bytes 8388608 | tf_op jit(solution)/shard_map/pallas_call | solution.py:736
  (30 shorter events, 1.5 us)
Async XLA Ops:
  4.8 2.7 %collective-permute-start = (f32[2,128,256]{2,1,0:T(8,128)S(1)}, f32[2,128,256]{2,1,0:T(8,128)S(1)}, u32[]{:S(2)}, u32[]{:S(2)}) collective-permute-start(f32[2,128,256]{2,1,0:T(8,128)S(1)} %constant_dynamic-slice_fusion.1), channel_id=1, source_target_pairs={{0,1},{1,0},{2,3},{3,2},{4,5},{5,4},{6,7},{7,6},{8,9},{9,8},{10,11... | collective-permute-start | bytes 786440 | tf_op jit(solution)/shard_map/ppermute | solution.py:760
  7.6 4.8 %collective-permute-start.1 = (f32[128,256]{1,0:T(8,128)S(1)}, f32[128,256]{1,0:T(8,128)S(1)}, u32[]{:S(2)}, u32[]{:S(2)}) collective-permute-start(f32[128,256]{1,0:T(8,128)S(1)} %get-tuple-element.87), channel_id=1, source_target_pairs={{0,2},{1,3},{2,0},{3,1},{4,6},{5,7},{6,4},{7,5},{8,10},{9,11},{10,... | collective-permute-start | bytes 393224 | tf_op jit(solution)/shard_map/ppermute | solution.py:756
  8.9 5.6 %collective-permute-start.2 = (f32[128,256]{1,0:T(8,128)S(1)}, f32[128,256]{1,0:T(8,128)S(1)}, u32[]{:S(2)}, u32[]{:S(2)}) collective-permute-start(f32[128,256]{1,0:T(8,128)S(1)} %get-tuple-element.86), channel_id=1, source_target_pairs={{0,6},{1,7},{2,4},{3,5},{4,2},{5,3},{6,0},{7,1},{8,14},{9,15},{10,... | collective-permute-start | bytes 393224 | tf_op jit(solution)/shard_map/ppermute | solution.py:756
  14.6 5.1 %collective-permute-start.3 = (f32[128,256]{1,0:T(8,128)S(1)}, f32[128,256]{1,0:T(8,128)S(1)}, u32[]{:S(2)}, u32[]{:S(2)}) collective-permute-start(f32[128,256]{1,0:T(8,128)S(1)} %get-tuple-element.84), channel_id=1, source_target_pairs={{0,6},{1,7},{2,4},{3,5},{4,2},{5,3},{6,0},{7,1},{8,14},{9,15},{10,... | collective-permute-start | bytes 393224 | tf_op jit(solution)/shard_map/ppermute | solution.py:756
  16.5 4.1 %collective-permute-start.4 = (f32[128,256]{1,0:T(8,128)S(1)}, f32[128,256]{1,0:T(8,128)S(1)}, u32[]{:S(2)}, u32[]{:S(2)}) collective-permute-start(f32[128,256]{1,0:T(8,128)S(1)} %get-tuple-element.85), channel_id=1, source_target_pairs={{0,2},{1,3},{2,0},{3,1},{4,6},{5,7},{6,4},{7,5},{8,10},{9,11},{10,... | collective-permute-start | bytes 393224 | tf_op jit(solution)/shard_map/ppermute | solution.py:756
  20.6 3.9 %collective-permute-start.5 = (f32[2,128,256]{2,1,0:T(8,128)S(1)}, f32[2,128,256]{2,1,0:T(8,128)S(1)}, u32[]{:S(2)}, u32[]{:S(2)}) collective-permute-start(f32[2,128,256]{2,1,0:T(8,128)S(1)} %pad_maximum_fusion.1.mine_ref), channel_id=1, source_target_pairs={{0,1},{1,0},{2,3},{3,2},{4,5},{5,4},{6,7},{7,6},{8,9},{9,8},{10,11... | collective-permute-start | bytes 786440 | tf_op jit(solution)/shard_map/ppermute | solution.py:760
  68.5 29.5 %all-to-all-start.1 = ((f32[16,256,128]{2,1,0:T(8,128)}), f32[16,256,128]{2,1,0:T(8,128)S(1)}, u32[]{:S(2)}, u32[]{:S(2)}) async-start(f32[16,256,128]{2,1,0:T(8,128)} %get-tuple-element.50), calls=%async_computation.1 | async-start | bytes 4194304 | tf_op jit(solution)/shard_map/all_to_all | solution.py:798
  72.4 2.8 %collective-permute-start.6 = (f32[40,128]{1,0:T(8,128)S(1)}, f32[40,128]{1,0:T(8,128)S(1)}, u32[]{:S(2)}, u32[]{:S(2)}) collective-permute-start(f32[40,128]{1,0:T(8,128)S(1)} %get-tuple-element.47.after_ref), channel_id=1, source_target_pairs={{0,1},{1,0},{2,3},{3,2},{4,5},{5,4},{6,7},{7,6},{8,9},{9,8},{10,11... | collective-permute-start | bytes 61448 | tf_op jit(solution)/shard_map/ppermute | solution.py:760
  75.2 7.2 %collective-permute-start.7 = (f32[80,128]{1,0:T(8,128)S(1)}, f32[80,128]{1,0:T(8,128)S(1)}, u32[]{:S(2)}, u32[]{:S(2)}) collective-permute-start(f32[80,128]{1,0:T(8,128)S(1)} %maximum_select_fusion.refs_0_), channel_id=1, source_target_pairs={{0,6},{1,7},{2,0},{3,1},{4,2},{5,3},{6,4},{7,5},{8,14},{9,15},{10,... | collective-permute-start | bytes 122888 | tf_op jit(solution)/shard_map/ppermute | solution.py:756
  76.2 6.2 %collective-permute-start.8 = (f32[80,128]{1,0:T(8,128)S(1)}, f32[80,128]{1,0:T(8,128)S(1)}, u32[]{:S(2)}, u32[]{:S(2)}) collective-permute-start(f32[80,128]{1,0:T(8,128)S(1)} %maximum_select_fusion.refs_0_), channel_id=1, source_target_pairs={{0,4},{1,5},{2,6},{3,7},{4,0},{5,1},{6,2},{7,3},{8,12},{9,13},{10,... | collective-permute-start | bytes 122888 | tf_op jit(solution)/shard_map/ppermute | solution.py:756
  76.7 5.7 %collective-permute-start.9 = (f32[80,128]{1,0:T(8,128)S(1)}, f32[80,128]{1,0:T(8,128)S(1)}, u32[]{:S(2)}, u32[]{:S(2)}) collective-permute-start(f32[80,128]{1,0:T(8,128)S(1)} %maximum_select_fusion.refs_0_), channel_id=1, source_target_pairs={{0,2},{1,3},{2,4},{3,5},{4,6},{5,7},{6,0},{7,1},{8,10},{9,11},{10,... | collective-permute-start | bytes 122888 | tf_op jit(solution)/shard_map/ppermute | solution.py:756
  103.1 6.4 %collective-permute-start.10 = (f32[2,136,256]{2,1,0:T(8,128)S(1)}, f32[2,136,256]{2,1,0:T(8,128)S(1)}, u32[]{:S(2)}, u32[]{:S(2)}) collective-permute-start(f32[2,136,256]{2,1,0:T(8,128)S(1)} %constant_dynamic-slice_fusion), channel_id=1, source_target_pairs={{0,1},{1,0},{2,3},{3,2},{4,5},{5,4},{6,7},{7,6},{8,9},{9,8},{10,11... | collective-permute-start | bytes 835592 | tf_op jit(solution)/shard_map/ppermute | solution.py:760
  109.6 5.1 %collective-permute-start.11 = (f32[136,256]{1,0:T(8,128)S(1)}, f32[136,256]{1,0:T(8,128)S(1)}, u32[]{:S(2)}, u32[]{:S(2)}) collective-permute-start(f32[136,256]{1,0:T(8,128)S(1)} %get-tuple-element.83), channel_id=1, source_target_pairs={{0,2},{1,3},{2,0},{3,1},{4,6},{5,7},{6,4},{7,5},{8,10},{9,11},{10,... | collective-permute-start | bytes 417800 | tf_op jit(solution)/shard_map/ppermute | solution.py:756
  109.7 6.2 %collective-permute-start.12 = (f32[136,256]{1,0:T(8,128)S(1)}, f32[136,256]{1,0:T(8,128)S(1)}, u32[]{:S(2)}, u32[]{:S(2)}) collective-permute-start(f32[136,256]{1,0:T(8,128)S(1)} %get-tuple-element.82), channel_id=1, source_target_pairs={{0,6},{1,7},{2,4},{3,5},{4,2},{5,3},{6,0},{7,1},{8,14},{9,15},{10,... | collective-permute-start | bytes 417800 | tf_op jit(solution)/shard_map/ppermute | solution.py:756
  115.9 5.2 %collective-permute-start.13 = (f32[136,256]{1,0:T(8,128)S(1)}, f32[136,256]{1,0:T(8,128)S(1)}, u32[]{:S(2)}, u32[]{:S(2)}) collective-permute-start(f32[136,256]{1,0:T(8,128)S(1)} %get-tuple-element.80), channel_id=1, source_target_pairs={{0,6},{1,7},{2,4},{3,5},{4,2},{5,3},{6,0},{7,1},{8,14},{9,15},{10,... | collective-permute-start | bytes 417800 | tf_op jit(solution)/shard_map/ppermute | solution.py:756
  116.9 4.2 %collective-permute-start.14 = (f32[136,256]{1,0:T(8,128)S(1)}, f32[136,256]{1,0:T(8,128)S(1)}, u32[]{:S(2)}, u32[]{:S(2)}) collective-permute-start(f32[136,256]{1,0:T(8,128)S(1)} %get-tuple-element.81), channel_id=1, source_target_pairs={{0,2},{1,3},{2,0},{3,1},{4,6},{5,7},{6,4},{7,5},{8,10},{9,11},{10,... | collective-permute-start | bytes 417800 | tf_op jit(solution)/shard_map/ppermute | solution.py:756
  121.2 3.6 %collective-permute-start.15 = (f32[2,136,256]{2,1,0:T(8,128)S(1)}, f32[2,136,256]{2,1,0:T(8,128)S(1)}, u32[]{:S(2)}, u32[]{:S(2)}) collective-permute-start(f32[2,136,256]{2,1,0:T(8,128)S(1)} %pad_maximum_fusion.mine_ref), channel_id=1, source_target_pairs={{0,1},{1,0},{2,3},{3,2},{4,5},{5,4},{6,7},{7,6},{8,9},{9,8},{10,11... | collective-permute-start | bytes 835592 | tf_op jit(solution)/shard_map/ppermute | solution.py:760
  164.1 30.2 %all-to-all-start.3 = ((f32[16,256,128]{2,1,0:T(8,128)}), f32[16,256,128]{2,1,0:T(8,128)}, u32[]{:S(2)}, u32[]{:S(2)}) async-start(f32[16,256,128]{2,1,0:T(8,128)} %get-tuple-element.71), calls=%async_computation.3 | async-start | bytes 4194304 | tf_op jit(solution)/shard_map/all_to_all | solution.py:798
  168.6 3.2 %collective-permute-start.16 = (f32[40,128]{1,0:T(8,128)S(1)}, f32[40,128]{1,0:T(8,128)S(1)}, u32[]{:S(2)}, u32[]{:S(2)}) collective-permute-start(f32[40,128]{1,0:T(8,128)S(1)} %get-tuple-element.68.after_ref), channel_id=1, source_target_pairs={{0,1},{1,0},{2,3},{3,2},{4,5},{5,4},{6,7},{7,6},{8,9},{9,8},{10,11... | collective-permute-start | bytes 61448 | tf_op jit(solution)/shard_map/ppermute | solution.py:760
  171.8 7.6 %collective-permute-start.17 = (f32[80,128]{1,0:T(8,128)S(1)}, f32[80,128]{1,0:T(8,128)S(1)}, u32[]{:S(2)}, u32[]{:S(2)}) collective-permute-start(f32[80,128]{1,0:T(8,128)S(1)} %maximum_select_fusion.1.refs_0_), channel_id=1, source_target_pairs={{0,6},{1,7},{2,0},{3,1},{4,2},{5,3},{6,4},{7,5},{8,14},{9,15},{10,... | collective-permute-start | bytes 122888 | tf_op jit(solution)/shard_map/ppermute | solution.py:756
  173.5 5.8 %collective-permute-start.18 = (f32[80,128]{1,0:T(8,128)S(1)}, f32[80,128]{1,0:T(8,128)S(1)}, u32[]{:S(2)}, u32[]{:S(2)}) collective-permute-start(f32[80,128]{1,0:T(8,128)S(1)} %maximum_select_fusion.1.refs_0_), channel_id=1, source_target_pairs={{0,4},{1,5},{2,6},{3,7},{4,0},{5,1},{6,2},{7,3},{8,12},{9,13},{10,... | collective-permute-start | bytes 122888 | tf_op jit(solution)/shard_map/ppermute | solution.py:756
  174.3 5.1 %collective-permute-start.19 = (f32[80,128]{1,0:T(8,128)S(1)}, f32[80,128]{1,0:T(8,128)S(1)}, u32[]{:S(2)}, u32[]{:S(2)}) collective-permute-start(f32[80,128]{1,0:T(8,128)S(1)} %maximum_select_fusion.1.refs_0_), channel_id=1, source_target_pairs={{0,2},{1,3},{2,4},{3,5},{4,6},{5,7},{6,0},{7,1},{8,10},{9,11},{10,... | collective-permute-start | bytes 122888 | tf_op jit(solution)/shard_map/ppermute | solution.py:756
  197.7 13.6 %all-to-all-start.4 = ((f32[8,8,256]{2,1,0:T(8,128)}), f32[8,8,256]{2,1,0:T(8,128)S(1)}, u32[]{:S(2)}, u32[]{:S(2)}) async-start(f32[8,8,256]{2,1,0:T(8,128)} %get-tuple-element.75), calls=%async_computation.4 | async-start | bytes 131072 | tf_op jit(solution)/shard_map/all_to_all | solution.py:798

commit v6 on v5

--- a/solution.py
+++ b/solution.py
@@ -183,7 +183,7 @@
     )(*in_hbm(momentum, grads, basis))
 
 
-def store_products(inputs, outputs, scratch, block, scaled):
+def store_products(inputs, outputs, scratch, block, scaled, count):
     n_ref, mine_ref, theirs_ref = inputs
     x_ref, p_ref, rs_ref = outputs
     parts, t, shares, pair_of_p = scratch
@@ -210,7 +210,7 @@
     size = x_ref.shape[1] - rank
     share = t[pl.ds(pl.multiple_of(n_ref[0] * size, size), size), :]
     pt = split(turned)
-    blocks = x_ref.shape[0] // CHUNKS
+    blocks = x_ref.shape[0] // count
     shares[...] = share
     pair_of_p[0], pair_of_p[1] = pt
 
@@ -220,7 +220,7 @@
             x_ref[k * blocks + q, :rank] = r[:, q * LANES : (q + 1) * LANES]
             x_ref[k * blocks + q, rank:] = shares[...]
 
-    each(fill)
+    each(fill, count)
 
 
 def first_products_kernel(
@@ -233,7 +233,7 @@
         return split(buffer_block(m, g, columns(k, m.shape[1] // CHUNKS)))
 
     store_products(
-        (n_ref, mine_ref, theirs_ref), (x_ref, p_ref, rs_ref), scratch, block, False
+        (n_ref, mine_ref, theirs_ref), (x_ref, p_ref, rs_ref), scratch, block, False, CHUNKS
     )
 
 
@@ -250,15 +250,15 @@
 def second_products_kernel(
     n_ref, mine_ref, theirs_ref, b_ref, x_ref, p_ref, rs_ref, b, came, *scratch
 ):
-    wait = fetch(pair_moves(b_ref, b), came)
+    wait = fetch(pair_moves(b_ref, b, FEW), came, FEW)
 
     def block(k):
         wait(k)
-        c = columns(k, b.shape[2] // CHUNKS)
+        c = columns(k, b.shape[2] // FEW)
         return b[0, :, c], b[1, :, c]
 
     store_products(
-        (n_ref, mine_ref, theirs_ref), (x_ref, p_ref, rs_ref), scratch, block, True
+        (n_ref, mine_ref, theirs_ref), (x_ref, p_ref, rs_ref), scratch, block, True, FEW
     )
 
 

time: 216 us -> 217 us (level)
  no operation moved by 1% of the time
where the time goes in v6:
time: 217 us; the launch traced here: 216 us
  Pallas kernels  72.4 us (33%)
  blocking collectives  72 us (33%)
  starting transfers between devices  45 us (21%)
  waiting for transfers between devices  25.2 us (12%)
    all_to_all x2, blocking collectives, exchange(): return lax.all_to_all(x, axis, 0, 0, tiled=True)  72 us
    pallas_call x2, Pallas kernels, inverse_factor(): call(cholesky_kernel, [SM, VM] + [VM] * len(pieces), [jax.ShapeDtypeStruc...  21.5 us
    all_to_all x3, starting transfers between devices, exchange(): return lax.all_to_all(x, axis, 0, 0, tiled=True)  17.3 us
    ppermute x6, starting transfers between devices, core_permute(): return lax.ppermute(x, 'col', [(k, k ^ 1) for k in range(2 * SIDE)])  15.9 us
    ppermute x14, starting transfers between devices, chip_permute(): return lax.ppermute(x, 'col', pairs)  11.8 us
    all_to_all x3, waiting for transfers between devices, exchange(): return lax.all_to_all(x, axis, 0, 0, tiled=True)  9.61 us
    ppermute x14, waiting for transfers between devices, chip_permute(): return lax.ppermute(x, 'col', pairs)  9.21 us
    pallas_call x2, Pallas kernels, products(): call(kernel, [SM, VM, VM] + [ANY] * len(bigs), [jax.ShapeDtypeStruct(shap...  8.23 us
  transfers between devices with their start and end apart: 23, of which 15 were waited for; matrix products, arithmetic and copies ran while one was open for 0% of the time, Pallas kernels for 20%

profile of v6, /device:TPU:1, one launch (start us, length us, event | category | flops | bytes accessed | tf_op | source)
XLA Modules:
  0.0 216.1 jit_solution(6785683333692426236)
XLA Ops:
  0.6 4.1 %shard_map.50 = f32[512,256]{1,0:T(8,128)S(1)} custom-call(f32[512,2048]{1,0:T(8,128)} %m_ref.5, bf16[2,512,2048]{2,1,0:T(8,128)(2,1)} %g_ref.5, f32[2048,256]{1,0:T(8,128)} %v_ref.1), custom_call_target="tpu_custom_call" | custom-call | flops 1610612736 | bytes 8388608 | tf_op jit(solution)/shard_map/pallas_call | solution.py:171
  4.8 1.5 collective-permute-start
  6.3 1.2 collective-permute-done
  7.6 1.4 collective-permute-start.1
  8.9 1.8 collective-permute-start.2
  10.8 1.6 collective-permute-done.1
  12.3 2.2 %collective-permute-done.2 = f32[128,256]{1,0:T(8,128)S(1)} collective-permute-done((f32[128,256]{1,0:T(8,128)S(1)}, f32[128,256]{1,0:T(8,128)S(1)}, u32[]{:S(2)}, u32[]{:S(2)}) %collective-permute-start.2) | collective-permute-done | bytes 131104 | tf_op jit(solution)/shard_map/ppermute | solution.py:756
  14.6 1.9 collective-permute-start.3
  16.5 3.2 %collective-permute-done.3 = f32[128,256]{1,0:T(8,128)S(1)} collective-permute-done((f32[128,256]{1,0:T(8,128)S(1)}, f32[128,256]{1,0:T(8,128)S(1)}, u32[]{:S(2)}, u32[]{:S(2)}) %collective-permute-start.3) | collective-permute-done | bytes 131104 | tf_op jit(solution)/shard_map/ppermute | solution.py:756
  19.7 0.9 collective-permute-done.4
  20.6 2.7 %collective-permute-start.5 = (f32[2,128,256]{2,1,0:T(8,128)S(1)}, f32[2,128,256]{2,1,0:T(8,128)S(1)}, u32[]{:S(2)}, u32[]{:S(2)}) collective-permute-start(f32[2,128,256]{2,1,0:T(8,128)S(1)} %pad_maximum_fusion.1.mine_ref), channel_id=1, source_target_pairs={{0,1},{1,0},{2,3},{3,2},{4,5},{5,4},{6,7},{7,6},{8,9},{9,8},{10,11... | collective-permute-start | bytes 786440 | tf_op jit(solution)/shard_map/ppermute | solution.py:760
  23.4 1.2 collective-permute-done.5.theirs_ref
  24.5 4.3 %shard_map.51 = (f32[16,296,128]{2,1,0:T(8,128)S(1)}, f32[512,256]{1,0:T(8,128)S(1)}, f32[8,256]{1,0:T(8,128)}) custom-call(s32[1]{0:T(128)} %bitcast.n_ref, f32[2,128,256]{2,1,0:T(8,128)S(1)} %pad_maximum_fusion.1.mine_ref, f32[2,128,256]{2,1,0:T(8,128)S(1)} %collective-permute-done.5.theirs_ref, f32[512,2048]{1,0:T(8,128)} %m_ref.5, ...), custom_call_target="tpu_custom_call" | custom-call | flops 1610612736 | bytes 8388608 | tf_op jit(solution)/shard_map/pallas_call | solution.py:270
  28.8 38.1 %all_to_all.25.x_ref = f32[16,296,128]{2,1,0:T(8,128)S(1)} all-to-all(f32[16,296,128]{2,1,0:T(8,128)S(1)} %get-tuple-element.46), channel_id=1, replica_groups=mesh['row'=16,'col'=8] {'row'}, dimensions={0} | all-to-all | bytes 4849664 | tf_op jit(solution)/shard_map/all_to_all | solution.py:798
  67.0 1.5 shard_map.52
  68.5 3.9 %all-to-all-start.1 = ((f32[16,256,128]{2,1,0:T(8,128)}), f32[16,256,128]{2,1,0:T(8,128)S(1)}, u32[]{:S(2)}, u32[]{:S(2)}) async-start(f32[16,256,128]{2,1,0:T(8,128)} %get-tuple-element.50), calls=%async_computation.1 | async-start | bytes 4194304 | tf_op jit(solution)/shard_map/all_to_all | solution.py:798
  72.4 1.9 collective-permute-start.6
  74.4 0.8 collective-permute-done.6
  75.2 0.9 collective-permute-start.7
  76.2 0.6 collective-permute-start.8
  76.8 5.5 %shard_map.54.a_ref = bf16[2,512,2048]{2,1,0:T(8,128)(2,1)} custom-call(f32[40,128]{1,0:T(8,128)S(1)} %get-tuple-element.47.after_ref, f32[512,2048]{1,0:T(8,128)} %m_ref.5, bf16[2,512,2048]{2,1,0:T(8,128)(2,1)} %g_ref.5), custom_call_target="tpu_custom_call" | custom-call | flops 8388608 | bytes 8388608 | tf_op jit(solution)/shard_map/pallas_call | solution.py:465
  82.4 10.7 %shard_map.53 = (f32[256,256]{1,0:T(8,128)S(1)}, f32[512,256]{1,0:T(8,128)S(1)}) custom-call(s32[1]{0:T(128)} %bitcast.n_ref, f32[512,256]{1,0:T(8,128)S(1)} %get-tuple-element.45.p_ref, f32[80,128]{1,0:T(8,128)S(1)} %maximum_select_fusion.refs_0_, f32[80,128]{1,0:T(8,128)S(1)} %collective-permute-done.7.refs_1_, ...), custom_call_target="tpu_custom_call" | custom-call | flops 10000000000 | bytes 8388608 | tf_op jit(solution)/shard_map/pallas_call | solution.py:431
  93.1 4.9 %all-to-all-done.1.x_ref = f32[16,256,128]{2,1,0:T(8,128)S(1)} async-done(((f32[16,256,128]{2,1,0:T(8,128)}), f32[16,256,128]{2,1,0:T(8,128)S(1)}, u32[]{:S(2)}, u32[]{:S(2)}) %all-to-all-start.1) | async-done | bytes 2097184 | tf_op jit(solution)/shard_map/all_to_all | solution.py:798
  98.1 5.0 %shard_map.55 = (f32[4,136,256]{2,1,0:T(8,128)S(1)}, bf16[2,256,2048]{2,1,0:T(8,128)(2,1)S(1)}) custom-call(f32[512,256]{1,0:T(8,128)S(1)} %get-tuple-element.48.o_ref, f32[256,256]{1,0:T(8,128)S(1)} %get-tuple-element.49.w_ref, f32[16,256,128]{2,1,0:T(8,128)S(1)} %all-to-all-done.1.x_ref, bf16[2,512,2048]{2,1,0:T(8,128)(2,1)} %shard_map.54.a_ref), custom_call_target="tpu_custom_call" | custom-call | flops 2684354560 | bytes 8388608 | tf_op jit(solution)/shard_map/pallas_call | solution.py:518
  103.1 5.2 %collective-permute-start.10 = (f32[2,136,256]{2,1,0:T(8,128)S(1)}, f32[2,136,256]{2,1,0:T(8,128)S(1)}, u32[]{:S(2)}, u32[]{:S(2)}) collective-permute-start(f32[2,136,256]{2,1,0:T(8,128)S(1)} %constant_dynamic-slice_fusion), channel_id=1, source_target_pairs={{0,1},{1,0},{2,3},{3,2},{4,5},{5,4},{6,7},{7,6},{8,9},{9,8},{10,11... | collective-permute-start | bytes 835592 | tf_op jit(solution)/shard_map/ppermute | solution.py:760
  108.3 1.2 collective-permute-done.10
  109.7 1.0 collective-permute-start.12
  110.6 4.0 %shard_map.56 = (bf16[2,256,2048]{2,1,0:T(8,128)(2,1)}, bf16[2,512,2048]{2,1,0:T(8,128)(2,1)}) custom-call(f32[512,256]{1,0:T(8,128)S(1)} %get-tuple-element.48.o_ref, f32[256,256]{1,0:T(8,128)S(1)} %get-tuple-element.49.w_ref, bf16[2,256,2048]{2,1,0:T(8,128)(2,1)S(1)} %get-tuple-element.54.rt_ref, bf16[2,512,2048]{2,1,0:T(8,128)(2,1)} %shard_map.54.a_ref), custom_call_target="tpu_custom_call" | custom-call | flops 1342177280 | bytes 8388608 | tf_op jit(solution)/shard_map/pallas_call | solution.py:577
  114.7 1.1 collective-permute-done.12
  115.9 1.0 collective-permute-start.13
  116.9 4.0 %shard_map.57 = (bf16[2,256,2048]{2,1,0:T(8,128)(2,1)}, bf16[2,512,2048]{2,1,0:T(8,128)(2,1)}) custom-call(f32[512,256]{1,0:T(8,128)S(1)} %get-tuple-element.48.o_ref, f32[256,256]{1,0:T(8,128)S(1)} %get-tuple-element.49.w_ref, bf16[2,256,2048]{2,1,0:T(8,128)(2,1)S(1)} %get-tuple-element.54.rt_ref, ...), custom_call_target="tpu_custom_call", output_to_operand_aliasing={{0}: (4, {}), {1}: (5, {})} | custom-call | flops 1342177280 | bytes 8388608 | tf_op jit(solution)/shard_map/pallas_call | solution.py:577
  121.2 2.4 %collective-permute-start.15 = (f32[2,136,256]{2,1,0:T(8,128)S(1)}, f32[2,136,256]{2,1,0:T(8,128)S(1)}, u32[]{:S(2)}, u32[]{:S(2)}) collective-permute-start(f32[2,136,256]{2,1,0:T(8,128)S(1)} %pad_maximum_fusion.mine_ref), channel_id=1, source_target_pairs={{0,1},{1,0},{2,3},{3,2},{4,5},{5,4},{6,7},{7,6},{8,9},{9,8},{10,11... | collective-permute-start | bytes 835592 | tf_op jit(solution)/shard_map/ppermute | solution.py:760
  123.6 1.2 collective-permute-done.15.theirs_ref
  124.8 3.9 %shard_map.58 = (f32[16,296,128]{2,1,0:T(8,128)S(1)}, f32[512,256]{1,0:T(8,128)S(1)}, f32[8,256]{1,0:T(8,128)S(1)}) custom-call(s32[1]{0:T(128)} %bitcast.n_ref, f32[2,136,256]{2,1,0:T(8,128)S(1)} %pad_maximum_fusion.mine_ref, f32[2,136,256]{2,1,0:T(8,128)S(1)} %collective-permute-done.15.theirs_ref, bf16[2,512,2048]{2,1,0:T(8,128)(2,1)} %get-tuple-element.65.b_ref), custom_call_target="tpu_custom_call" | custom-call | flops 1610612736 | bytes 8388608 | tf_op jit(solution)/shard_map/pallas_call | solution.py:270
  128.7 33.8 %all_to_all.26.x_ref = f32[16,296,128]{2,1,0:T(8,128)S(1)} all-to-all(f32[16,296,128]{2,1,0:T(8,128)S(1)} %get-tuple-element.67), channel_id=1, replica_groups=mesh['row'=16,'col'=8] {'row'}, dimensions={0} | all-to-all | bytes 4849664 | tf_op jit(solution)/shard_map/all_to_all | solution.py:798
  162.6 1.5 shard_map.59
  164.1 4.7 %all-to-all-start.3 = ((f32[16,256,128]{2,1,0:T(8,128)}), f32[16,256,128]{2,1,0:T(8,128)}, u32[]{:S(2)}, u32[]{:S(2)}) async-start(f32[16,256,128]{2,1,0:T(8,128)} %get-tuple-element.71), calls=%async_computation.3 | async-start | bytes 4194304 | tf_op jit(solution)/shard_map/all_to_all | solution.py:798
  168.8 2.1 collective-permute-start.16
  170.9 0.8 collective-permute-done.16
  171.7 1.7 collective-permute-start.17
  173.5 0.8 collective-permute-start.18
  174.8 4.5 %shard_map.61.c_ref = f32[512,2048]{1,0:T(8,128)} custom-call(f32[40,128]{1,0:T(8,128)S(1)} %get-tuple-element.68.after_ref, f32[512,256]{1,0:T(8,128)S(1)} %get-tuple-element.48.o_ref, f32[8,256]{1,0:T(8,128)S(1)} %get-tuple-element.72.rs_ref, bf16[2,256,2048]{2,1,0:T(8,128)(2,1)} %get-tuple-element.73.raw_ref), custom_call_target="tpu_custom_call" | custom-call | flops 1610612736 | bytes 8388608 | tf_op jit(solution)/shard_map/pallas_call | solution.py:628
  179.3 10.7 %shard_map.60 = (f32[256,256]{1,0:T(8,128)S(1)}, f32[512,256]{1,0:T(8,128)S(1)}) custom-call(s32[1]{0:T(128)} %bitcast.n_ref, f32[512,256]{1,0:T(8,128)S(1)} %get-tuple-element.66.p_ref, f32[80,128]{1,0:T(8,128)S(1)} %maximum_select_fusion.1.refs_0_, f32[80,128]{1,0:T(8,128)S(1)} %collective-permute-done.17.refs_1_, ...), custom_call_target="tpu_custom_call" | custom-call | flops 10000000000 | bytes 8388608 | tf_op jit(solution)/shard_map/pallas_call | solution.py:431
  190.1 4.5 %all-to-all-done.3.x_ref = f32[16,256,128]{2,1,0:T(8,128)} async-done(((f32[16,256,128]{2,1,0:T(8,128)}), f32[16,256,128]{2,1,0:T(8,128)}, u32[]{:S(2)}, u32[]{:S(2)}) %all-to-all-start.3) | async-done | bytes 2097184 | tf_op jit(solution)/shard_map/all_to_all | solution.py:798
  194.5 3.4 %shard_map.62 = (bf16[2,256,2048]{2,1,0:T(8,128)(2,1)S(1)}, f32[8,8,256]{2,1,0:T(8,128)}) custom-call(f32[256,256]{1,0:T(8,128)S(1)} %get-tuple-element.70.w_ref, f32[16,256,128]{2,1,0:T(8,128)} %all-to-all-done.3.x_ref), custom_call_target="tpu_custom_call" | custom-call | flops 805306368 | bytes 8388608 | tf_op jit(solution)/shard_map/pallas_call | solution.py:672
  197.9 8.7 %all-to-all-start.4 = ((f32[8,8,256]{2,1,0:T(8,128)}), f32[8,8,256]{2,1,0:T(8,128)S(1)}, u32[]{:S(2)}, u32[]{:S(2)}) async-start(f32[8,8,256]{2,1,0:T(8,128)} %get-tuple-element.75), calls=%async_computation.4 | async-start | bytes 131072 | tf_op jit(solution)/shard_map/all_to_all | solution.py:798
  206.7 4.6 %shard_map.63 = f32[512,2048]{1,0:T(8,128)} custom-call(f32[512,256]{1,0:T(8,128)S(1)} %get-tuple-element.69.o_ref, bf16[2,256,2048]{2,1,0:T(8,128)(2,1)S(1)} %get-tuple-element.76.raw_ref, bf16[2,512,2048]{2,1,0:T(8,128)(2,1)} %get-tuple-element.65.b_ref), custom_call_target="tpu_custom_call" | custom-call | flops 1610612736 | bytes 8388608 | tf_op jit(solution)/shard_map/pallas_call | solution.py:700
  211.5 4.4 %shard_map.64 = bf16[512,2048]{1,0:T(8,128)(2,1)} custom-call(f32[512,256]{1,0:T(8,128)S(1)} %get-tuple-element.69.o_ref, f32[8,8,256]{2,1,0:T(8,128)S(1)} %all-to-all-done.4.sq_ref, bf16[2,256,2048]{2,1,0:T(8,128)(2,1)S(1)} %get-tuple-element.76.raw_ref, f32[512,2048]{1,0:T(8,128)} %shard_map.61.c_ref), custom_call_target="tpu_custom_call" | custom-call | flops 1610612736 | bytes 8388608 | tf_op jit(solution)/shard_map/pallas_call | solution.py:736
  (30 shorter events, 1.5 us)
Async XLA Ops:
  4.8 2.7 %collective-permute-start = (f32[2,128,256]{2,1,0:T(8,128)S(1)}, f32[2,128,256]{2,1,0:T(8,128)S(1)}, u32[]{:S(2)}, u32[]{:S(2)}) collective-permute-start(f32[2,128,256]{2,1,0:T(8,128)S(1)} %constant_dynamic-slice_fusion.1), channel_id=1, source_target_pairs={{0,1},{1,0},{2,3},{3,2},{4,5},{5,4},{6,7},{7,6},{8,9},{9,8},{10,11... | collective-permute-start | bytes 786440 | tf_op jit(solution)/shard_map/ppermute | solution.py:760
  7.6 4.8 %collective-permute-start.1 = (f32[128,256]{1,0:T(8,128)S(1)}, f32[128,256]{1,0:T(8,128)S(1)}, u32[]{:S(2)}, u32[]{:S(2)}) collective-permute-start(f32[128,256]{1,0:T(8,128)S(1)} %get-tuple-element.87), channel_id=1, source_target_pairs={{0,2},{1,3},{2,0},{3,1},{4,6},{5,7},{6,4},{7,5},{8,10},{9,11},{10,... | collective-permute-start | bytes 393224 | tf_op jit(solution)/shard_map/ppermute | solution.py:756
  8.9 5.6 %collective-permute-start.2 = (f32[128,256]{1,0:T(8,128)S(1)}, f32[128,256]{1,0:T(8,128)S(1)}, u32[]{:S(2)}, u32[]{:S(2)}) collective-permute-start(f32[128,256]{1,0:T(8,128)S(1)} %get-tuple-element.86), channel_id=1, source_target_pairs={{0,6},{1,7},{2,4},{3,5},{4,2},{5,3},{6,0},{7,1},{8,14},{9,15},{10,... | collective-permute-start | bytes 393224 | tf_op jit(solution)/shard_map/ppermute | solution.py:756
  14.6 5.1 %collective-permute-start.3 = (f32[128,256]{1,0:T(8,128)S(1)}, f32[128,256]{1,0:T(8,128)S(1)}, u32[]{:S(2)}, u32[]{:S(2)}) collective-permute-start(f32[128,256]{1,0:T(8,128)S(1)} %get-tuple-element.84), channel_id=1, source_target_pairs={{0,6},{1,7},{2,4},{3,5},{4,2},{5,3},{6,0},{7,1},{8,14},{9,15},{10,... | collective-permute-start | bytes 393224 | tf_op jit(solution)/shard_map/ppermute | solution.py:756
  16.5 4.1 %collective-permute-start.4 = (f32[128,256]{1,0:T(8,128)S(1)}, f32[128,256]{1,0:T(8,128)S(1)}, u32[]{:S(2)}, u32[]{:S(2)}) collective-permute-start(f32[128,256]{1,0:T(8,128)S(1)} %get-tuple-element.85), channel_id=1, source_target_pairs={{0,2},{1,3},{2,0},{3,1},{4,6},{5,7},{6,4},{7,5},{8,10},{9,11},{10,... | collective-permute-start | bytes 393224 | tf_op jit(solution)/shard_map/ppermute | solution.py:756
  20.6 3.9 %collective-permute-start.5 = (f32[2,128,256]{2,1,0:T(8,128)S(1)}, f32[2,128,256]{2,1,0:T(8,128)S(1)}, u32[]{:S(2)}, u32[]{:S(2)}) collective-permute-start(f32[2,128,256]{2,1,0:T(8,128)S(1)} %pad_maximum_fusion.1.mine_ref), channel_id=1, source_target_pairs={{0,1},{1,0},{2,3},{3,2},{4,5},{5,4},{6,7},{7,6},{8,9},{9,8},{10,11... | collective-permute-start | bytes 786440 | tf_op jit(solution)/shard_map/ppermute | solution.py:760
  68.5 29.5 %all-to-all-start.1 = ((f32[16,256,128]{2,1,0:T(8,128)}), f32[16,256,128]{2,1,0:T(8,128)S(1)}, u32[]{:S(2)}, u32[]{:S(2)}) async-start(f32[16,256,128]{2,1,0:T(8,128)} %get-tuple-element.50), calls=%async_computation.1 | async-start | bytes 4194304 | tf_op jit(solution)/shard_map/all_to_all | solution.py:798
  72.4 2.8 %collective-permute-start.6 = (f32[40,128]{1,0:T(8,128)S(1)}, f32[40,128]{1,0:T(8,128)S(1)}, u32[]{:S(2)}, u32[]{:S(2)}) collective-permute-start(f32[40,128]{1,0:T(8,128)S(1)} %get-tuple-element.47.after_ref), channel_id=1, source_target_pairs={{0,1},{1,0},{2,3},{3,2},{4,5},{5,4},{6,7},{7,6},{8,9},{9,8},{10,11... | collective-permute-start | bytes 61448 | tf_op jit(solution)/shard_map/ppermute | solution.py:760
  75.2 7.2 %collective-permute-start.7 = (f32[80,128]{1,0:T(8,128)S(1)}, f32[80,128]{1,0:T(8,128)S(1)}, u32[]{:S(2)}, u32[]{:S(2)}) collective-permute-start(f32[80,128]{1,0:T(8,128)S(1)} %maximum_select_fusion.refs_0_), channel_id=1, source_target_pairs={{0,6},{1,7},{2,0},{3,1},{4,2},{5,3},{6,4},{7,5},{8,14},{9,15},{10,... | collective-permute-start | bytes 122888 | tf_op jit(solution)/shard_map/ppermute | solution.py:756
  76.2 6.2 %collective-permute-start.8 = (f32[80,128]{1,0:T(8,128)S(1)}, f32[80,128]{1,0:T(8,128)S(1)}, u32[]{:S(2)}, u32[]{:S(2)}) collective-permute-start(f32[80,128]{1,0:T(8,128)S(1)} %maximum_select_fusion.refs_0_), channel_id=1, source_target_pairs={{0,4},{1,5},{2,6},{3,7},{4,0},{5,1},{6,2},{7,3},{8,12},{9,13},{10,... | collective-permute-start | bytes 122888 | tf_op jit(solution)/shard_map/ppermute | solution.py:756
  76.7 5.7 %collective-permute-start.9 = (f32[80,128]{1,0:T(8,128)S(1)}, f32[80,128]{1,0:T(8,128)S(1)}, u32[]{:S(2)}, u32[]{:S(2)}) collective-permute-start(f32[80,128]{1,0:T(8,128)S(1)} %maximum_select_fusion.refs_0_), channel_id=1, source_target_pairs={{0,2},{1,3},{2,4},{3,5},{4,6},{5,7},{6,0},{7,1},{8,10},{9,11},{10,... | collective-permute-start | bytes 122888 | tf_op jit(solution)/shard_map/ppermute | solution.py:756
  103.1 6.4 %collective-permute-start.10 = (f32[2,136,256]{2,1,0:T(8,128)S(1)}, f32[2,136,256]{2,1,0:T(8,128)S(1)}, u32[]{:S(2)}, u32[]{:S(2)}) collective-permute-start(f32[2,136,256]{2,1,0:T(8,128)S(1)} %constant_dynamic-slice_fusion), channel_id=1, source_target_pairs={{0,1},{1,0},{2,3},{3,2},{4,5},{5,4},{6,7},{7,6},{8,9},{9,8},{10,11... | collective-permute-start | bytes 835592 | tf_op jit(solution)/shard_map/ppermute | solution.py:760
  109.6 5.1 %collective-permute-start.11 = (f32[136,256]{1,0:T(8,128)S(1)}, f32[136,256]{1,0:T(8,128)S(1)}, u32[]{:S(2)}, u32[]{:S(2)}) collective-permute-start(f32[136,256]{1,0:T(8,128)S(1)} %get-tuple-element.83), channel_id=1, source_target_pairs={{0,2},{1,3},{2,0},{3,1},{4,6},{5,7},{6,4},{7,5},{8,10},{9,11},{10,... | collective-permute-start | bytes 417800 | tf_op jit(solution)/shard_map/ppermute | solution.py:756
  109.7 6.2 %collective-permute-start.12 = (f32[136,256]{1,0:T(8,128)S(1)}, f32[136,256]{1,0:T(8,128)S(1)}, u32[]{:S(2)}, u32[]{:S(2)}) collective-permute-start(f32[136,256]{1,0:T(8,128)S(1)} %get-tuple-element.82), channel_id=1, source_target_pairs={{0,6},{1,7},{2,4},{3,5},{4,2},{5,3},{6,0},{7,1},{8,14},{9,15},{10,... | collective-permute-start | bytes 417800 | tf_op jit(solution)/shard_map/ppermute | solution.py:756
  115.9 5.2 %collective-permute-start.13 = (f32[136,256]{1,0:T(8,128)S(1)}, f32[136,256]{1,0:T(8,128)S(1)}, u32[]{:S(2)}, u32[]{:S(2)}) collective-permute-start(f32[136,256]{1,0:T(8,128)S(1)} %get-tuple-element.80), channel_id=1, source_target_pairs={{0,6},{1,7},{2,4},{3,5},{4,2},{5,3},{6,0},{7,1},{8,14},{9,15},{10,... | collective-permute-start | bytes 417800 | tf_op jit(solution)/shard_map/ppermute | solution.py:756
  116.9 4.2 %collective-permute-start.14 = (f32[136,256]{1,0:T(8,128)S(1)}, f32[136,256]{1,0:T(8,128)S(1)}, u32[]{:S(2)}, u32[]{:S(2)}) collective-permute-start(f32[136,256]{1,0:T(8,128)S(1)} %get-tuple-element.81), channel_id=1, source_target_pairs={{0,2},{1,3},{2,0},{3,1},{4,6},{5,7},{6,4},{7,5},{8,10},{9,11},{10,... | collective-permute-start | bytes 417800 | tf_op jit(solution)/shard_map/ppermute | solution.py:756
  121.2 3.6 %collective-permute-start.15 = (f32[2,136,256]{2,1,0:T(8,128)S(1)}, f32[2,136,256]{2,1,0:T(8,128)S(1)}, u32[]{:S(2)}, u32[]{:S(2)}) collective-permute-start(f32[2,136,256]{2,1,0:T(8,128)S(1)} %pad_maximum_fusion.mine_ref), channel_id=1, source_target_pairs={{0,1},{1,0},{2,3},{3,2},{4,5},{5,4},{6,7},{7,6},{8,9},{9,8},{10,11... | collective-permute-start | bytes 835592 | tf_op jit(solution)/shard_map/ppermute | solution.py:760
  164.1 30.4 %all-to-all-start.3 = ((f32[16,256,128]{2,1,0:T(8,128)}), f32[16,256,128]{2,1,0:T(8,128)}, u32[]{:S(2)}, u32[]{:S(2)}) async-start(f32[16,256,128]{2,1,0:T(8,128)} %get-tuple-element.71), calls=%async_computation.3 | async-start | bytes 4194304 | tf_op jit(solution)/shard_map/all_to_all | solution.py:798
  168.8 3.0 %collective-permute-start.16 = (f32[40,128]{1,0:T(8,128)S(1)}, f32[40,128]{1,0:T(8,128)S(1)}, u32[]{:S(2)}, u32[]{:S(2)}) collective-permute-start(f32[40,128]{1,0:T(8,128)S(1)} %get-tuple-element.68.after_ref), channel_id=1, source_target_pairs={{0,1},{1,0},{2,3},{3,2},{4,5},{5,4},{6,7},{7,6},{8,9},{9,8},{10,11... | collective-permute-start | bytes 61448 | tf_op jit(solution)/shard_map/ppermute | solution.py:760
  171.7 7.6 %collective-permute-start.17 = (f32[80,128]{1,0:T(8,128)S(1)}, f32[80,128]{1,0:T(8,128)S(1)}, u32[]{:S(2)}, u32[]{:S(2)}) collective-permute-start(f32[80,128]{1,0:T(8,128)S(1)} %maximum_select_fusion.1.refs_0_), channel_id=1, source_target_pairs={{0,6},{1,7},{2,0},{3,1},{4,2},{5,3},{6,4},{7,5},{8,14},{9,15},{10,... | collective-permute-start | bytes 122888 | tf_op jit(solution)/shard_map/ppermute | solution.py:756
  173.5 5.8 %collective-permute-start.18 = (f32[80,128]{1,0:T(8,128)S(1)}, f32[80,128]{1,0:T(8,128)S(1)}, u32[]{:S(2)}, u32[]{:S(2)}) collective-permute-start(f32[80,128]{1,0:T(8,128)S(1)} %maximum_select_fusion.1.refs_0_), channel_id=1, source_target_pairs={{0,4},{1,5},{2,6},{3,7},{4,0},{5,1},{6,2},{7,3},{8,12},{9,13},{10,... | collective-permute-start | bytes 122888 | tf_op jit(solution)/shard_map/ppermute | solution.py:756
  174.3 5.1 %collective-permute-start.19 = (f32[80,128]{1,0:T(8,128)S(1)}, f32[80,128]{1,0:T(8,128)S(1)}, u32[]{:S(2)}, u32[]{:S(2)}) collective-permute-start(f32[80,128]{1,0:T(8,128)S(1)} %maximum_select_fusion.1.refs_0_), channel_id=1, source_target_pairs={{0,2},{1,3},{2,4},{3,5},{4,6},{5,7},{6,0},{7,1},{8,10},{9,11},{10,... | collective-permute-start | bytes 122888 | tf_op jit(solution)/shard_map/ppermute | solution.py:756
  197.9 13.6 %all-to-all-start.4 = ((f32[8,8,256]{2,1,0:T(8,128)}), f32[8,8,256]{2,1,0:T(8,128)S(1)}, u32[]{:S(2)}, u32[]{:S(2)}) async-start(f32[8,8,256]{2,1,0:T(8,128)} %get-tuple-element.75), calls=%async_computation.4 | async-start | bytes 131072 | tf_op jit(solution)/shard_map/all_to_all | solution.py:798
